TPU v7x, 256 devices: a whole 4x4x8 slice. The times are simulated.
256 devices in a mesh: row: 32 (over z, y_lo, core), col: 8 (over y_hi, x).
Axes of the slice: x: 4, y: 4 (y_hi: 2, y_lo: 2; y = y_hi * 2 + y_lo), z: 8, core: 2. Of those that a mesh axis runs over, the one named last changes fastest.
Arguments:
- eigvec: float32 [65536, 4096], P('row', 'col'), may hold values from -6 to 6
- reflectors: float32 [32, 8, 1024, 256], P('row', 'col'), may hold values from -0.125 to 0.125
- tfactors: float32 [32, 8, 256, 256], P('row', 'col'), may hold values from -1 to 1, as said below
- offsets: int32 [2, 32], replicated, may hold values from 1024 to 1536
- owners: int32 [2, 32], replicated, may hold values from 0 to 7
Outputs:
- result: float32 [65536, 4096], P('row', 'col')
Inputs may be any that keep to these rules, and one draw needn't show every extreme that they name: `tfactors`: every factor block is zero below its diagonal.
All inputs are finite; a program needn't handle non-finite values.
Results may differ from a plain program's by a relative error of at most 0.0003.
Values sent between devices are 32-bit elements; how exact they have to be, the bound alone decides.
No kernel may reach another device: no remote copies, remote signals or barrier semaphores. Data moves between devices by JAX's collectives and lax.ppermute only.
A program may use at most 64 MiB of HBM per device.

v0:
```python
import jax
import jax.numpy as jnp
from jax import lax
from jax.sharding import PartitionSpec as P

WIN = 1024
TICKS = 2


def from_root(block, axis, owner):
    block = jnp.where(lax.axis_index(axis) == owner, block, jnp.zeros_like(block))
    return lax.psum(block, axis)


def from_behind(shard, axis, by):
    count = lax.axis_size(axis)
    pairs = [(i, i + by) for i in range(count) if 0 <= i + by < count]
    return lax.ppermute(shard, axis, pairs)


def project(vectors, window):
    return lax.dot_general(
        vectors,
        window,
        (((0,), (0,)), ((), ())),
        precision=lax.Precision.HIGHEST,
        preferred_element_type=jnp.float32,
    )


def product(left, right):
    return jnp.dot(left, right, precision=lax.Precision.HIGHEST, preferred_element_type=jnp.float32)


def per_device(eigvec, reflectors, tfactors, offsets, owners):
    row_count = eigvec.shape[0]
    half_rows = WIN // 2
    own_row = lax.axis_index("row")
    vector_local = reflectors[0, 0]
    factor_local = tfactors[0, 0]
    lower_rows = from_behind(eigvec[:half_rows], "row", -1)
    extended = jnp.concatenate([eigvec, lower_rows], 0)
    for turn_index in range(TICKS):
        source = owners[turn_index, own_row]
        begin_row = offsets[turn_index, own_row]
        window = lax.dynamic_slice_in_dim(extended, begin_row, WIN, 0)
        vector_block = from_root(vector_local, "col", source)
        other_block = from_root(factor_local, "col", source)
        coefficients = project(vector_block, window)
        window = window - product(vector_block, product(other_block, coefficients))
        extended = lax.dynamic_update_slice_in_dim(extended, window, begin_row, 0)
    upper_rows = from_behind(extended[row_count:], "row", 1)
    top_rows = jnp.where(own_row > 0, upper_rows, extended[:half_rows])
    return jnp.concatenate([top_rows, extended[half_rows:row_count]], 0)


def solution(mesh):
    return jax.shard_map(
        per_device,
        mesh=mesh,
        in_specs=(
            P("row", "col"),
            P("row", "col", None, None),
            P("row", "col", None, None),
            P(),
            P(),
        ),
        out_specs=P("row", "col"),
        check_vma=False,
    )
```

profile of v0, /device:TPU:128, one launch (start us, length us, event | category | flops | bytes accessed | tf_op | source)
XLA Modules:
  0.0 179.8 jit_solution(17253241074773366660)
XLA Ops:
  6.5 0.0 all-reduce.3.cloned.1.call-start
  6.5 1.4 constant_dynamic-slice_fusion.2
  9.2 2.7 %select_bitcast_fusion = (f32[1024,256]{1,0:T(8,128)}, f32[1024,256]{1,0:T(8,128)}) fusion(f32[1,1,1024,256]{3,2,1,0:T(8,128)} %param.6, pred[]{:T(512)S(6)} %eq.9, pred[]{:T(512)S(6)} %eq.8), kind=kLoop, calls=%fused_computation.8 | loop fusion | flops 524288 | bytes 3145730 | tf_op jit(solution)/shard_map/jit(_where)/select_n | solution.py:11
  12.0 1.8 %select_bitcast_fusion.2 = (f32[256,256]{1,0:T(8,128)}, f32[256,256]{1,0:T(8,128)}) fusion(f32[1,1,256,256]{3,2,1,0:T(8,128)} %param.7, pred[]{:T(512)S(6)} %eq.9, pred[]{:T(512)S(6)} %eq.8), kind=kLoop, calls=%fused_computation.10 | loop fusion | flops 131072 | bytes 786434 | tf_op jit(solution)/shard_map/jit(_where)/select_n | solution.py:11
  13.8 0.0 all-reduce.3.cloned.1.call-update
  13.8 1.3 slice.12
  15.1 2.5 %collective-permute-start = (f32[512,512]{1,0:T(8,128)S(1)}, f32[512,512]{1,0:T(8,128)S(1)}, u32[]{:S(2)}, u32[]{:S(2)}) collective-permute-start(f32[512,512]{1,0:T(8,128)S(1)} %slice.12), channel_id=1, source_target_pairs={{8,0},{16,8},{24,16},{32,24},{40,32},{48,40},{56,48},{64,56},{72,6... | collective-permute-start | bytes 3145736 | tf_op jit(solution)/shard_map/ppermute | solution.py:18
  21.4 4.6 %constant_dynamic-update-slice_fusion.1 = f32[2560,512]{1,0:T(8,128)} fusion(f32[2048,512]{1,0:T(8,128)} %param.5), kind=kLoop, calls=%fused_computation.13 | loop fusion | bytes 8388608
  26.0 5.1 %collective-permute-done = f32[512,512]{1,0:T(8,128)S(1)} collective-permute-done((f32[512,512]{1,0:T(8,128)S(1)}, f32[512,512]{1,0:T(8,128)S(1)}, u32[]{:S(2)}, u32[]{:S(2)}) %collective-permute-start) | collective-permute-done | bytes 1048608 | tf_op jit(solution)/shard_map/ppermute | solution.py:18
  31.0 1.0 constant_dynamic-update-slice_fusion
  32.1 87.4 %all-reduce.3.cloned.1.call-done = (f32[1024,256]{1,0:T(8,128)}, f32[256,256]{1,0:T(8,128)}, f32[1024,256]{1,0:T(8,128)}, f32[256,256]{1,0:T(8,128)}) async-done(((f32[1024,256]{1,0:T(8,128)}, f32[256,256]{1,0:T(8,128)}, f32[1024,256]{1,0:T(8,128)}, f32[256,256]{1,0:T(8,128)}), (f32[1024,256]{1,0:T(8,128)}, f32[256,256]{1,0:T(8,128)}, f32[1024,256]{1,0:T(8,128)}, ...) | async-done | bytes 2621456 | tf_op jit(solution)/shard_map/psum | solution.py:12
  119.4 0.0 copy-start.1
  119.4 4.0 %fusion.2 = f32[256,512]{1,0:T(8,128)S(1)} fusion(f32[1024,256]{1,0:T(8,128)} %get-tuple-element.5, f32[2560,512]{1,0:T(8,128)} %constant_dynamic-update-slice_fusion, s32[]{:T(128)S(6)} %select_n.64), kind=kOutput, calls=%fused_computation.5 | convolution fusion | flops 1610612736 | bytes 3670020 | tf_op jit(solution)/shard_map/dot_general | solution.py:22
  123.5 1.6 fusion.6
  125.1 0.0 copy-done.1
  125.1 0.0 copy-start
  125.1 3.6 %dynamic-slice_subtract_fusion.1 = f32[1024,512]{1,0:T(8,128)S(1)} fusion(f32[2560,512]{1,0:T(8,128)} %constant_dynamic-update-slice_fusion, s32[]{:T(128)S(6)} %select_n.64, f32[1024,256]{1,0:T(8,128)S(1)} %copy-done.1, f32[256,512]{1,0:T(8,128)S(1)} %fusion.6), kind=kOutput, calls=%fused_computation.4 | convolution fusion | flops 1611137024 | bytes 5767172 | tf_op jit(solution)/shard_map/dot_general | solution.py:32
  128.7 0.0 copy-start.2
  128.7 6.5 %dynamic_update_slice.6 = f32[2560,512]{1,0:T(8,128)} dynamic-update-slice(f32[2560,512]{1,0:T(8,128)} %constant_dynamic-update-slice_fusion, f32[1024,512]{1,0:T(8,128)S(1)} %dynamic-slice_subtract_fusion.1, s32[]{:T(128)S(6)} %select_n.64, s32[]{:T(128)} %constant.4.clone.1) | dynamic-update-slice | bytes 4194308 | tf_op jit(solution)/shard_map/dynamic_update_slice | solution.py:51
  135.3 0.0 copy-done
  135.3 3.6 %fusion = f32[256,512]{1,0:T(8,128)S(1)} fusion(f32[1024,256]{1,0:T(8,128)S(1)} %copy-done, f32[2560,512]{1,0:T(8,128)} %dynamic_update_slice.6, s32[]{:T(128)S(6)} %select_n.71), kind=kOutput, calls=%fused_computation.2 | convolution fusion | flops 1610612736 | bytes 3670020 | tf_op jit(solution)/shard_map/dot_general | solution.py:22
  138.9 0.0 copy-done.2
  138.9 0.6 fusion.7
  139.5 3.5 %dynamic-slice_subtract_fusion = f32[1024,512]{1,0:T(8,128)S(1)} fusion(f32[2560,512]{1,0:T(8,128)} %dynamic_update_slice.6, s32[]{:T(128)S(6)} %select_n.71, f32[1024,256]{1,0:T(8,128)S(1)} %copy-done, f32[256,512]{1,0:T(8,128)S(1)} %fusion.7), kind=kOutput, calls=%fused_computation.1 | convolution fusion | flops 1611137024 | bytes 5767172 | tf_op jit(solution)/shard_map/dot_general | solution.py:32
  143.1 6.5 %dynamic_update_slice.7 = f32[2560,512]{1,0:T(8,128)} dynamic-update-slice(f32[2560,512]{1,0:T(8,128)} %dynamic_update_slice.6, f32[1024,512]{1,0:T(8,128)S(1)} %dynamic-slice_subtract_fusion, s32[]{:T(128)S(6)} %select_n.71, s32[]{:T(128)} %constant.4.clone.1) | dynamic-update-slice | bytes 4194308 | tf_op jit(solution)/shard_map/dynamic_update_slice | solution.py:51
  149.5 1.3 slice.16
  150.8 1.9 %collective-permute-start.1 = (f32[512,512]{1,0:T(8,128)S(1)}, f32[512,512]{1,0:T(8,128)S(1)}, u32[]{:S(2)}, u32[]{:S(2)}) collective-permute-start(f32[512,512]{1,0:T(8,128)S(1)} %slice.16), channel_id=1, source_target_pairs={{0,8},{8,16},{16,24},{24,32},{32,40},{40,48},{48,56},{56,64},{64,7... | collective-permute-start | bytes 3145736 | tf_op jit(solution)/shard_map/ppermute | solution.py:18
  152.8 2.2 %slice.18 = f32[1536,512]{1,0:T(8,128)S(1)} slice(f32[2560,512]{1,0:T(8,128)} %dynamic_update_slice.7), slice={[512:2048], [0:512]} | slice | bytes 6291456 | tf_op jit(solution)/shard_map/slice | solution.py:54
  155.0 14.1 %collective-permute-done.1 = f32[512,512]{1,0:T(8,128)S(1)} collective-permute-done((f32[512,512]{1,0:T(8,128)S(1)}, f32[512,512]{1,0:T(8,128)S(1)}, u32[]{:S(2)}, u32[]{:S(2)}) %collective-permute-start.1) | collective-permute-done | bytes 1048608 | tf_op jit(solution)/shard_map/ppermute | solution.py:18
  169.1 1.4 slice_select_fusion
  170.5 2.5 %pad_maximum_fusion = f32[2048,512]{1,0:T(8,128)} fusion(f32[1536,512]{1,0:T(8,128)S(1)} %slice.18, f32[512,512]{1,0:T(8,128)S(1)} %slice_select_fusion), kind=kLoop, calls=%fused_computation | loop fusion | flops 1048576 | bytes 8388608 | tf_op jit(solution)/shard_map/concatenate | solution.py:54
Async XLA Ops:
  6.5 112.9 %all-reduce.3.cloned.1.call-start = ((), (), s32[]{:S(2)}) async-start(), calls=%async_computation | async-start | bytes 5242880 | tf_op jit(solution)/shard_map/psum | solution.py:12
  15.1 15.9 %collective-permute-start = (f32[512,512]{1,0:T(8,128)S(1)}, f32[512,512]{1,0:T(8,128)S(1)}, u32[]{:S(2)}, u32[]{:S(2)}) collective-permute-start(f32[512,512]{1,0:T(8,128)S(1)} %slice.12), channel_id=1, source_target_pairs={{8,0},{16,8},{24,16},{32,24},{40,32},{48,40},{56,48},{64,56},{72,6... | collective-permute-start | bytes 3145736 | tf_op jit(solution)/shard_map/ppermute | solution.py:18
  119.4 5.6 %copy-start.1 = (f32[1024,256]{1,0:T(8,128)S(1)}, f32[1024,256]{1,0:T(8,128)}, u32[]{:S(2)}) copy-start(f32[1024,256]{1,0:T(8,128)} %get-tuple-element.5) | copy-start | bytes 3145732
  125.1 10.2 %copy-start = (f32[1024,256]{1,0:T(8,128)S(1)}, f32[1024,256]{1,0:T(8,128)}, u32[]{:S(2)}) copy-start(f32[1024,256]{1,0:T(8,128)} %get-tuple-element.7) | copy-start | bytes 3145732
  128.7 10.2 %copy-start.2 = (f32[256,256]{1,0:T(8,128)S(1)}, f32[256,256]{1,0:T(8,128)}, u32[]{:S(2)}) copy-start(f32[256,256]{1,0:T(8,128)} %get-tuple-element.8) | copy-start | bytes 786436
  150.8 18.2 %collective-permute-start.1 = (f32[512,512]{1,0:T(8,128)S(1)}, f32[512,512]{1,0:T(8,128)S(1)}, u32[]{:S(2)}, u32[]{:S(2)}) collective-permute-start(f32[512,512]{1,0:T(8,128)S(1)} %slice.16), channel_id=1, source_target_pairs={{0,8},{8,16},{16,24},{24,32},{32,40},{40,48},{48,56},{56,64},{64,7... | collective-permute-start | bytes 3145736 | tf_op jit(solution)/shard_map/ppermute | solution.py:18
Sparse Core Ops, SparseCore 0:
  14.0 105.4 all-reduce.2
where the time goes:
time: 181 us; the launch traced here: 180 us
  waiting for transfers between devices  107 us (59%)
  local copies, waits for them, and re-layouts  24.8 us (14%)
  between operations  18.6 us (10%)
  matrix products  17 us (9%)
  other arithmetic  8.46 us (5%)
  starting transfers between devices  4.39 us (2%)
    psum x1, waiting for transfers between devices, from_root(): return lax.psum(block, axis)  87.4 us
    ppermute x2, waiting for transfers between devices, from_behind(): return lax.ppermute(shard, axis, pairs)  19.2 us
    dynamic_update_slice x2, local copies, waits for them, and re-layouts, per_device(): extended = lax.dynamic_update_slice_in_dim(extended, window, begin_row, 0)  13 us
    dot_general x4, matrix products, product(): jnp.dot(left, right, precision=lax.Precision.HIGHEST, preferred_element_t...  9.34 us
    dot_general x2, matrix products, project(): lax.dot_general(vectors, window, (((0,), (0,)), ((), ())), precision=lax....  7.68 us
    unnamed x7, local copies, waits for them, and re-layouts  4.6 us
    select_n x2, other arithmetic, from_root(): jnp.where(lax.axis_index(axis) == owner, block, jnp.zeros_like(block))  4.57 us
    ppermute x2, starting transfers between devices, from_behind(): return lax.ppermute(shard, axis, pairs)  4.39 us
  transfers between devices with their start and end apart: 3, of which 3 were waited for; matrix products, arithmetic and copies ran while one was open for 5% of the time, Pallas kernels for 0%

commit v1 on v0

v1 whole, which is shorter than its diff:
```python
import jax
import jax.numpy as jnp
from jax import lax
from jax.experimental import pallas as pl
from jax.experimental.pallas import tpu as pltpu
from jax.sharding import PartitionSpec as P

WIN = 1024
HALF = 512
BLOCK = 256
TICKS = 2
PIECES = 8
VROWS = WIN // PIECES
TROWS = 24
PROWS = VROWS + TROWS
SPAN = WIN + 16
F32 = jnp.float32
BF16 = jnp.bfloat16


def split(x):
    hi = x.astype(BF16)
    return hi, (x - hi.astype(F32)).astype(BF16)


def mm(a, b, dims):
    return lax.dot_general(a, b, (dims, ((), ())), preferred_element_type=F32)


def mm3(ah, al, bh, bl, dims):
    return mm(ah, bh, dims) + mm(ah, bl, dims) + mm(al, bh, dims)


NN = ((1,), (0,))
TN = ((0,), (0,))


def update_kernel(idx, eig, halo, p, r, l, q, a, b, e, f, out, bottom, ext, vp, vh, vl, tf, wh, wl, sems):
    rows = eig.shape[0]
    load = pltpu.make_async_copy(eig.at[pl.ds(rows - WIN, WIN)], ext.at[pl.ds(0, WIN)], sems.at[0])
    keep = pltpu.make_async_copy(eig.at[pl.ds(HALF, rows - WIN - HALF)], out.at[pl.ds(HALF, rows - WIN - HALF)], sems.at[1])
    load.start()
    keep.start()
    ext[WIN : WIN + HALF, :] = halo[...]
    ext[WIN + HALF :, :] = jnp.zeros((16, ext.shape[1]), F32)
    for tick in range(TICKS):
        vp[tick, :8, :] = jnp.zeros((8, BLOCK), F32)
        vp[tick, WIN + 8 :, :] = jnp.zeros((16, BLOCK), F32)
    found = (
        (p, (0, PROWS)),
        (r, (0, PROWS)),
        (l, (0, PROWS)),
        (q, (0, PROWS)),
        (None, ((a, 0), (b, 0))),
        (a, (PROWS, 2 * PROWS)),
        (b, (PROWS, 2 * PROWS)),
        (None, ((e, 0), (f, 0))),
    )
    for tick in range(TICKS):
        for n, (ref, starts) in enumerate(found):
            src, at = starts[tick] if ref is None else (ref, starts[tick])
            k = idx[TICKS + n]
            vp[tick, pl.ds(pl.multiple_of(k * VROWS + 8, 8), VROWS), :] = src[at : at + VROWS, :]
            tf[tick, pl.ds(pl.multiple_of(k * TROWS, TROWS), TROWS), :] = src[at + VROWS : at + PROWS, :]
    for tick in range(TICKS):
        shift = idx[tick] % 8
        tiles = pltpu.roll(vp[tick].reshape(SPAN // 8 + 1, 8, BLOCK), shift, 1)
        same = lax.broadcasted_iota(jnp.int32, (SPAN // 8, 8, BLOCK), 1) >= shift
        hi, lo = split(jnp.where(same, tiles[1:], tiles[:-1]).reshape(SPAN, BLOCK))
        vh[tick] = hi
        vl[tick] = lo
    load.wait()
    for tick in range(TICKS):
        base = pl.multiple_of(idx[tick] // 8 * 8, 8)
        low = tf[tick, 128:192, :]
        corner = jnp.concatenate([low[:, :128], low[:, 128:]], 0)
        factor = jnp.concatenate([tf[tick, :128, :], jnp.concatenate([jnp.zeros((128, 128), F32), corner], 1)], 0)
        fh, fl = split(factor)
        hi, lo = split(ext[pl.ds(base, SPAN), :])
        wh[...] = hi
        wl[...] = lo
        coef = mm3(vh[tick], vl[tick], wh[...], wl[...], TN)
        ch, cl = split(coef)
        sh, sl = split(mm3(fh, fl, ch, cl, NN))
        for k in range(5):
            part = slice(k * 208, (k + 1) * 208)
            spot = pl.ds(pl.multiple_of(base + k * 208, 8), 208)
            ext[spot, :] = ext[spot, :] - mm3(vh[tick, part, :], vl[tick, part, :], sh, sl, NN)
    bottom[...] = ext[WIN : WIN + HALF, :]
    store = pltpu.make_async_copy(ext.at[pl.ds(0, WIN)], out.at[pl.ds(rows - WIN, WIN)], sems.at[2])
    store.start()
    keep.wait()
    store.wait()


def update(idx, eig, halo, pieces):
    vmem = pl.BlockSpec(memory_space=pltpu.VMEM)
    hbm = pl.BlockSpec(memory_space=pl.ANY)
    columns = eig.shape[1]
    return pl.pallas_call(
        update_kernel,
        out_shape=(
            jax.ShapeDtypeStruct(eig.shape, F32),
            jax.ShapeDtypeStruct((HALF, columns), F32),
        ),
        in_specs=[pl.BlockSpec(memory_space=pltpu.SMEM), hbm] + [vmem] * 9,
        out_specs=(hbm, vmem),
        scratch_shapes=[
            pltpu.VMEM((WIN + HALF + 16, columns), F32),
            pltpu.VMEM((TICKS, SPAN + 8, BLOCK), F32),
            pltpu.VMEM((TICKS, SPAN, BLOCK), BF16),
            pltpu.VMEM((TICKS, SPAN, BLOCK), BF16),
            pltpu.VMEM((TICKS, 192, BLOCK), F32),
            pltpu.VMEM((SPAN, columns), BF16),
            pltpu.VMEM((SPAN, columns), BF16),
            pltpu.SemaphoreType.DMA((3,)),
        ],
        compiler_params=pltpu.CompilerParams(vmem_limit_bytes=40 * 1024 * 1024),
        cost_estimate=pl.CostEstimate(flops=8_000_000_000, bytes_accessed=16_000_000, transcendentals=0),
        name="update",
    )(idx, eig, halo, *pieces)


def per_device(eigvec, reflectors, tfactors, offsets, owners):
    rows = eigvec.shape[0]
    row = lax.axis_index("row")
    col = lax.axis_index("col")
    y, x = col // 4, col % 4
    count = lax.axis_size("row")

    halo = lax.ppermute(eigvec[:HALF], "row", [(i + 1, i) for i in range(count - 1)])

    vectors = reflectors[0, 0].reshape(PIECES, VROWS, BLOCK)
    factor = tfactors[0, 0]
    packed = jnp.concatenate([factor[:128], jnp.concatenate([factor[128:192, 128:], factor[192:, 128:]], 1)], 0)
    block = jnp.concatenate([vectors, packed.reshape(PIECES, TROWS, BLOCK)], 1)
    mine = lax.all_to_all(block, "col", 0, 0)
    source = lax.dynamic_slice_in_dim(owners, row, 1, 1)[:, 0]
    begin = lax.dynamic_slice_in_dim(offsets, row, 1, 1)[:, 0]
    p = jnp.concatenate([lax.dynamic_index_in_dim(mine, source[t], 0, keepdims=False) for t in range(TICKS)], 0)

    def from_x(value, d):
        return lax.ppermute(value, "col", [((i // 4) * 4 + (i % 4 + d) % 4, i) for i in range(8)])

    r, l = from_x(p, 1), from_x(p, -1)
    q = lax.ppermute(p, "col", [(i, i ^ 4) for i in range(8)])
    a = from_x(jnp.concatenate([r[:PROWS], q], 0), 1)
    b = from_x(jnp.concatenate([l[PROWS:], q], 0), -1)
    e = from_x(a[PROWS : 2 * PROWS], 1)
    f = from_x(b[2 * PROWS :], -1)

    here, there = 4 * y, 4 * (1 - y)
    right, left, across = (x + 1) % 4, (x + 3) % 4, (x + 2) % 4
    order = [here + x, here + right, here + left, there + x, here + across, there + right, there + left, there + across]
    idx = jnp.stack([begin[0] - WIN, begin[1] - WIN] + order).astype(jnp.int32)

    out, bottom = update(idx, eigvec, halo, (p, r, l, q, a, b, e, f))
    upper = lax.ppermute(bottom, "row", [(i, i + 1) for i in range(count - 1)])
    top = jnp.where(row > 0, upper, eigvec[:HALF])
    return lax.dynamic_update_slice_in_dim(out, top, 0, 0)


def solution(mesh):
    return jax.shard_map(
        per_device,
        mesh=mesh,
        in_specs=(
            P("row", "col"),
            P("row", "col", None, None),
            P("row", "col", None, None),
            P(),
            P(),
        ),
        out_specs=P("row", "col"),
        check_vma=False,
    )
```

time: 181 us -> 99.9 us (0.55)
  waiting for transfers between devices: 107 us -> 48.4 us
  starting transfers between devices: 4.39 us -> 23 us
  matrix products: 17 us -> 0 us
  local copies, waits for them, and re-layouts: 24.8 us -> 8.85 us
  between operations: 18.6 us -> 4.92 us
  Pallas kernels: 0 us -> 8.85 us
  other arithmetic: 8.46 us -> 4.87 us
    psum x1 -> x0, waiting for transfers between devices: 87.4 us -> none  [from_root(): return lax.psum(block, axis)]
    dot_general x6 -> x0, matrix products: 17 us -> none  [the longest x4 9.34 us: product(): jnp.dot(left, right, precision=lax.Precision.HIGHEST, preferred_element_t...]
    all_to_all x0 -> x1, waiting for transfers between devices: none -> 15.1 us  [per_device(): mine = lax.all_to_all(block, 'col', 0, 0)]
    ppermute x2 -> x9, waiting for transfers between devices: 19.2 us -> 33.2 us  [the longest x1 16.5 us: per_device(): upper = lax.ppermute(bottom, 'row', [(i, i + 1) for i in range(count - 1)])]
    dynamic_update_slice x2 -> x0, local copies, waits for them, and re-layouts: 13 us -> none  [per_device(): extended = lax.dynamic_update_slice_in_dim(extended, window, begin_row, 0)]
    ppermute x2 -> x9, starting transfers between devices: 4.39 us -> 16.1 us  [the longest x6 11.7 us: from_x(): lax.ppermute(value, 'col', [(i // 4 * 4 + (i % 4 + d) % 4, i) for i in ra...]
    pallas_call x0 -> x1, Pallas kernels: none -> 8.85 us  [update(): pl.pallas_call(update_kernel, out_shape=(jax.ShapeDtypeStruct(eig.shape,...]
    all_to_all x0 -> x1, starting transfers between devices: none -> 6.93 us  [per_device(): mine = lax.all_to_all(block, 'col', 0, 0)]
  transfers between devices with their start and end apart: 3 -> 10, of which waited for: 3 -> 7; matrix products, arithmetic and copies ran while one was open for 5% -> 5% of each run, Pallas kernels for 0% -> 0%
where the time goes in v1:
time: 99.9 us; the launch traced here: 98.8 us
  waiting for transfers between devices  48.4 us (48%)
  starting transfers between devices  23 us (23%)
  local copies, waits for them, and re-layouts  8.85 us (9%)
  Pallas kernels  8.85 us (9%)
  between operations  4.92 us (5%)
  other arithmetic  4.87 us (5%)
    ppermute x1, waiting for transfers between devices, per_device(): upper = lax.ppermute(bottom, 'row', [(i, i + 1) for i in range(count - 1)])  16.5 us
    all_to_all x1, waiting for transfers between devices, per_device(): mine = lax.all_to_all(block, 'col', 0, 0)  15.1 us
    ppermute x6, waiting for transfers between devices, from_x(): lax.ppermute(value, 'col', [(i // 4 * 4 + (i % 4 + d) % 4, i) for i in ra...  13.8 us
    ppermute x6, starting transfers between devices, from_x(): lax.ppermute(value, 'col', [(i // 4 * 4 + (i % 4 + d) % 4, i) for i in ra...  11.7 us
    pallas_call x1, Pallas kernels, update(): pl.pallas_call(update_kernel, out_shape=(jax.ShapeDtypeStruct(eig.shape,...  8.85 us
    all_to_all x1, starting transfers between devices, per_device(): mine = lax.all_to_all(block, 'col', 0, 0)  6.93 us
    ppermute x1, waiting for transfers between devices, per_device(): q = lax.ppermute(p, 'col', [(i, i ^ 4) for i in range(8)])  2.93 us
    dynamic_update_slice x1, other arithmetic, per_device(): return lax.dynamic_update_slice_in_dim(out, top, 0, 0)  2.4 us
  transfers between devices with their start and end apart: 10, of which 7 were waited for; matrix products, arithmetic and copies ran while one was open for 5% of the time, Pallas kernels for 0%

profile of v1, /device:TPU:128, one launch (start us, length us, event | category | flops | bytes accessed | tf_op | source)
XLA Modules:
  0.0 98.8 jit_solution(10850766800447810069)
XLA Ops:
  0.0 0.0 copy-start.1
  0.0 0.0 copy-start.2
  0.0 0.9 slice_bitcast_fusion
  0.9 0.8 fusion
  1.8 2.4 %pad_maximum_fusion = f32[8,152,256]{2,1,0:T(8,128)} fusion(f32[8,24,256]{2,1,0:T(8,128)S(1)} %bitcast.22, f32[8,128,256]{2,1,0:T(8,128)} %bitcast.21), kind=kLoop, calls=%fused_computation | loop fusion | flops 311296 | bytes 2490368 | tf_op jit(solution)/shard_map/concatenate | solution.py:136
  4.1 6.9 %all-to-all-start = ((f32[8,152,256]{2,1,0:T(8,128)}), f32[8,152,256]{2,1,0:T(8,128)S(1)}, u32[]{:S(2)}, u32[]{:S(2)}) async-start(f32[8,152,256]{2,1,0:T(8,128)} %pad_maximum_fusion), calls=%async_computation | async-start | bytes 2490368 | tf_op jit(solution)/shard_map/all_to_all | solution.py:137
  11.1 0.0 copy-done.1
  11.1 0.0 copy-done.2
  11.1 0.1 constant_dynamic-slice_fusion
  11.1 0.5 fusion.1
  15.2 15.1 %all-to-all-done = f32[8,152,256]{2,1,0:T(8,128)S(1)} async-done(((f32[8,152,256]{2,1,0:T(8,128)}), f32[8,152,256]{2,1,0:T(8,128)S(1)}, u32[]{:S(2)}, u32[]{:S(2)}) %all-to-all-start) | async-done | bytes 1245216 | tf_op jit(solution)/shard_map/all_to_all | solution.py:137
  30.4 0.9 collective-permute-start.2
  31.4 2.4 %collective-permute-start.1 = (f32[304,256]{1,0:T(8,128)S(1)}, f32[304,256]{1,0:T(8,128)S(1)}, u32[]{:S(2)}, u32[]{:S(2)}) collective-permute-start(f32[304,256]{1,0:T(8,128)S(1)} %pad_maximum_fusion.3.p), channel_id=1, source_target_pairs={{1,0},{2,1},{3,2},{0,3},{5,4},{6,5},{7,6},{4,7},{9,8},{10,9},{11,1... | collective-permute-start | bytes 933896 | tf_op jit(solution)/shard_map/ppermute | solution.py:143
  33.7 0.6 collective-permute-start.3
  34.3 2.3 %slice.46 = f32[512,512]{1,0:T(8,128)} slice(f32[2048,512]{1,0:T(8,128)} %eig.1), slice={[0:512], [0:512]} | slice | bytes 2097152 | tf_op jit(solution)/shard_map/slice | solution.py:131
  36.6 1.9 %collective-permute-start = (f32[512,512]{1,0:T(8,128)}, f32[512,512]{1,0:T(8,128)S(1)}, u32[]{:S(2)}, u32[]{:S(2)}) collective-permute-start(f32[512,512]{1,0:T(8,128)} %slice.46), channel_id=1, source_target_pairs={{8,0},{16,8},{24,16},{32,24},{40,32},{48,40},{56,48},{64,56},{72,6... | collective-permute-start | bytes 3145736 | tf_op jit(solution)/shard_map/ppermute | solution.py:131
  38.5 2.2 %collective-permute-done.2.l = f32[304,256]{1,0:T(8,128)S(1)} collective-permute-done((f32[304,256]{1,0:T(8,128)S(1)}, f32[304,256]{1,0:T(8,128)S(1)}, u32[]{:S(2)}, u32[]{:S(2)}) %collective-permute-start.2) | collective-permute-done | bytes 311328 | tf_op jit(solution)/shard_map/ppermute | solution.py:143
  40.7 0.0 collective-permute-done.1.r
  40.7 2.9 %collective-permute-done.3.q = f32[304,256]{1,0:T(8,128)S(1)} collective-permute-done((f32[304,256]{1,0:T(8,128)S(1)}, f32[304,256]{1,0:T(8,128)S(1)}, u32[]{:S(2)}, u32[]{:S(2)}) %collective-permute-start.3) | collective-permute-done | bytes 311328 | tf_op jit(solution)/shard_map/ppermute | solution.py:146
  43.6 0.1 pad_maximum_fusion.1
  43.7 0.1 collective-permute-start.5
  43.8 3.2 %collective-permute-start.4 = (f32[456,256]{1,0:T(8,128)S(1)}, f32[456,256]{1,0:T(8,128)S(1)}, u32[]{:S(2)}, u32[]{:S(2)}) collective-permute-start(f32[456,256]{1,0:T(8,128)S(1)} %get-tuple-element.12), channel_id=1, source_target_pairs={{1,0},{2,1},{3,2},{0,3},{5,4},{6,5},{7,6},{4,7},{9,8},{10,9},{11,1... | collective-permute-start | bytes 1400840 | tf_op jit(solution)/shard_map/ppermute | solution.py:143
  47.0 8.8 %collective-permute-done.5.b = f32[456,256]{1,0:T(8,128)S(1)} collective-permute-done((f32[456,256]{1,0:T(8,128)S(1)}, f32[456,256]{1,0:T(8,128)S(1)}, u32[]{:S(2)}, u32[]{:S(2)}) %collective-permute-start.5) | collective-permute-done | bytes 466976 | tf_op jit(solution)/shard_map/ppermute | solution.py:143
  55.7 0.7 slice.62
  56.4 4.0 %collective-permute-start.7 = (f32[152,256]{1,0:T(8,128)}, f32[152,256]{1,0:T(8,128)S(1)}, u32[]{:S(2)}, u32[]{:S(2)}) collective-permute-start(f32[152,256]{1,0:T(8,128)} %slice.62), channel_id=1, source_target_pairs={{3,0},{0,1},{1,2},{2,3},{7,4},{4,5},{5,6},{6,7},{11,8},{8,9},{9,10... | collective-permute-start | bytes 466952 | tf_op jit(solution)/shard_map/ppermute | solution.py:143
  60.4 0.0 collective-permute-done.4.a
  60.4 0.7 slice.61
  61.1 1.1 %collective-permute-start.6 = (f32[152,256]{1,0:T(8,128)}, f32[152,256]{1,0:T(8,128)S(1)}, u32[]{:S(2)}, u32[]{:S(2)}) collective-permute-start(f32[152,256]{1,0:T(8,128)} %slice.61), channel_id=1, source_target_pairs={{1,0},{2,1},{3,2},{0,3},{5,4},{6,5},{7,6},{4,7},{9,8},{10,9},{11,1... | collective-permute-start | bytes 466952 | tf_op jit(solution)/shard_map/ppermute | solution.py:143
  62.1 0.6 fusion.2
  64.0 0.1 stack.43.idx
  64.1 0.0 collective-permute-done.halo
  64.1 0.8 collective-permute-done.7.f
  64.9 2.1 %collective-permute-done.6.e = f32[152,256]{1,0:T(8,128)S(1)} collective-permute-done((f32[152,256]{1,0:T(8,128)}, f32[152,256]{1,0:T(8,128)S(1)}, u32[]{:S(2)}, u32[]{:S(2)}) %collective-permute-start.6) | collective-permute-done | bytes 155680 | tf_op jit(solution)/shard_map/ppermute | solution.py:143
  67.0 0.0 copy-start
  67.0 2.2 %copy-done = f32[2048,512]{1,0:T(8,128)S(1)} copy-done((f32[2048,512]{1,0:T(8,128)S(1)}, f32[2048,512]{1,0:T(8,128)}, u32[]{:S(2)}) %copy-start) | copy-done | bytes 4194328
  69.1 8.8 %update.1 = (f32[2048,512]{1,0:T(8,128)}, f32[512,512]{1,0:T(8,128)}) custom-call(s32[10]{0:T(128)S(1)} %stack.43.idx, f32[2048,512]{1,0:T(8,128)S(1)} %copy-done, f32[512,512]{1,0:T(8,128)S(1)} %collective-permute-done.halo, f32[304,256]{1,0:T(8,128)S(1)} %pad_maximum_fusion.3.p, f32[304,256]{1,0:T(8,128)S(1)} %collective-permute-done.1.r, ...), custom_call_target="tpu_custom_call" | custom-call | flops 8000000000 | bytes 16000000 | tf_op jit(solution)/shard_map/update/pallas_call | solution.py:100
  78.0 1.9 %collective-permute-start.8 = (f32[512,512]{1,0:T(8,128)}, f32[512,512]{1,0:T(8,128)S(1)}, u32[]{:S(2)}, u32[]{:S(2)}) collective-permute-start(f32[512,512]{1,0:T(8,128)} %get-tuple-element.8), channel_id=1, source_target_pairs={{0,8},{8,16},{16,24},{24,32},{32,40},{40,48},{48,56},{56,64},{64,7... | collective-permute-start | bytes 3145736 | tf_op jit(solution)/shard_map/ppermute | solution.py:158
  79.9 16.5 %collective-permute-done.8 = f32[512,512]{1,0:T(8,128)S(1)} collective-permute-done((f32[512,512]{1,0:T(8,128)}, f32[512,512]{1,0:T(8,128)S(1)}, u32[]{:S(2)}, u32[]{:S(2)}) %collective-permute-start.8) | collective-permute-done | bytes 1048608 | tf_op jit(solution)/shard_map/ppermute | solution.py:158
  96.4 2.4 %select_dynamic-update-slice_fusion = f32[2048,512]{1,0:T(8,128)} fusion(f32[2048,512]{1,0:T(8,128)} %get-tuple-element.7, f32[512,512]{1,0:T(8,128)S(1)} %collective-permute-done.8, pred[]{:T(512)S(6)} %gt.3, f32[2048,512]{1,0:T(8,128)} %eig.1), kind=kLoop, calls=%fused_computation.1 | loop fusion | flops 262144 | bytes 3145729 | tf_op jit(solution)/shard_map/dynamic_update_slice | solution.py:160
  (5 shorter events, 0.1 us)
Async XLA Ops:
  0.0 11.1 %copy-start.1 = (s32[2,32]{1,0:T(2,128)S(1)}, s32[2,32]{1,0:T(2,128)}, u32[]{:S(2)}) copy-start(s32[2,32]{1,0:T(2,128)} %param.9) | copy-start | bytes 772
  0.0 11.1 %copy-start.2 = (s32[2,32]{1,0:T(2,128)S(1)}, s32[2,32]{1,0:T(2,128)}, u32[]{:S(2)}) copy-start(s32[2,32]{1,0:T(2,128)} %param.8) | copy-start | bytes 772
  4.1 26.2 %all-to-all-start = ((f32[8,152,256]{2,1,0:T(8,128)}), f32[8,152,256]{2,1,0:T(8,128)S(1)}, u32[]{:S(2)}, u32[]{:S(2)}) async-start(f32[8,152,256]{2,1,0:T(8,128)} %pad_maximum_fusion), calls=%async_computation | async-start | bytes 2490368 | tf_op jit(solution)/shard_map/all_to_all | solution.py:137
  30.4 10.2 %collective-permute-start.2 = (f32[304,256]{1,0:T(8,128)S(1)}, f32[304,256]{1,0:T(8,128)S(1)}, u32[]{:S(2)}, u32[]{:S(2)}) collective-permute-start(f32[304,256]{1,0:T(8,128)S(1)} %pad_maximum_fusion.3.p), channel_id=1, source_target_pairs={{3,0},{0,1},{1,2},{2,3},{7,4},{4,5},{5,6},{6,7},{11,8},{8,9},{9,10... | collective-permute-start | bytes 933896 | tf_op jit(solution)/shard_map/ppermute | solution.py:143
  31.4 9.3 %collective-permute-start.1 = (f32[304,256]{1,0:T(8,128)S(1)}, f32[304,256]{1,0:T(8,128)S(1)}, u32[]{:S(2)}, u32[]{:S(2)}) collective-permute-start(f32[304,256]{1,0:T(8,128)S(1)} %pad_maximum_fusion.3.p), channel_id=1, source_target_pairs={{1,0},{2,1},{3,2},{0,3},{5,4},{6,5},{7,6},{4,7},{9,8},{10,9},{11,1... | collective-permute-start | bytes 933896 | tf_op jit(solution)/shard_map/ppermute | solution.py:143
  33.7 9.9 %collective-permute-start.3 = (f32[304,256]{1,0:T(8,128)S(1)}, f32[304,256]{1,0:T(8,128)S(1)}, u32[]{:S(2)}, u32[]{:S(2)}) collective-permute-start(f32[304,256]{1,0:T(8,128)S(1)} %pad_maximum_fusion.3.p), channel_id=1, source_target_pairs={{0,4},{1,5},{2,6},{3,7},{4,0},{5,1},{6,2},{7,3},{8,12},{9,13},{10,... | collective-permute-start | bytes 933896 | tf_op jit(solution)/shard_map/ppermute | solution.py:146
  36.6 27.5 %collective-permute-start = (f32[512,512]{1,0:T(8,128)}, f32[512,512]{1,0:T(8,128)S(1)}, u32[]{:S(2)}, u32[]{:S(2)}) collective-permute-start(f32[512,512]{1,0:T(8,128)} %slice.46), channel_id=1, source_target_pairs={{8,0},{16,8},{24,16},{32,24},{40,32},{48,40},{56,48},{64,56},{72,6... | collective-permute-start | bytes 3145736 | tf_op jit(solution)/shard_map/ppermute | solution.py:131
  43.7 12.1 %collective-permute-start.5 = (f32[456,256]{1,0:T(8,128)S(1)}, f32[456,256]{1,0:T(8,128)S(1)}, u32[]{:S(2)}, u32[]{:S(2)}) collective-permute-start(f32[456,256]{1,0:T(8,128)S(1)} %get-tuple-element.11), channel_id=1, source_target_pairs={{3,0},{0,1},{1,2},{2,3},{7,4},{4,5},{5,6},{6,7},{11,8},{8,9},{9,10... | collective-permute-start | bytes 1400840 | tf_op jit(solution)/shard_map/ppermute | solution.py:143
  43.8 16.6 %collective-permute-start.4 = (f32[456,256]{1,0:T(8,128)S(1)}, f32[456,256]{1,0:T(8,128)S(1)}, u32[]{:S(2)}, u32[]{:S(2)}) collective-permute-start(f32[456,256]{1,0:T(8,128)S(1)} %get-tuple-element.12), channel_id=1, source_target_pairs={{1,0},{2,1},{3,2},{0,3},{5,4},{6,5},{7,6},{4,7},{9,8},{10,9},{11,1... | collective-permute-start | bytes 1400840 | tf_op jit(solution)/shard_map/ppermute | solution.py:143
  56.4 8.5 %collective-permute-start.7 = (f32[152,256]{1,0:T(8,128)}, f32[152,256]{1,0:T(8,128)S(1)}, u32[]{:S(2)}, u32[]{:S(2)}) collective-permute-start(f32[152,256]{1,0:T(8,128)} %slice.62), channel_id=1, source_target_pairs={{3,0},{0,1},{1,2},{2,3},{7,4},{4,5},{5,6},{6,7},{11,8},{8,9},{9,10... | collective-permute-start | bytes 466952 | tf_op jit(solution)/shard_map/ppermute | solution.py:143
  61.1 5.9 %collective-permute-start.6 = (f32[152,256]{1,0:T(8,128)}, f32[152,256]{1,0:T(8,128)S(1)}, u32[]{:S(2)}, u32[]{:S(2)}) collective-permute-start(f32[152,256]{1,0:T(8,128)} %slice.61), channel_id=1, source_target_pairs={{1,0},{2,1},{3,2},{0,3},{5,4},{6,5},{7,6},{4,7},{9,8},{10,9},{11,1... | collective-permute-start | bytes 466952 | tf_op jit(solution)/shard_map/ppermute | solution.py:143
  67.0 2.2 %copy-start = (f32[2048,512]{1,0:T(8,128)S(1)}, f32[2048,512]{1,0:T(8,128)}, u32[]{:S(2)}) copy-start(f32[2048,512]{1,0:T(8,128)} %eig.1) | copy-start | bytes 12582916
  78.0 18.4 %collective-permute-start.8 = (f32[512,512]{1,0:T(8,128)}, f32[512,512]{1,0:T(8,128)S(1)}, u32[]{:S(2)}, u32[]{:S(2)}) collective-permute-start(f32[512,512]{1,0:T(8,128)} %get-tuple-element.8), channel_id=1, source_target_pairs={{0,8},{8,16},{16,24},{24,32},{32,40},{40,48},{48,56},{56,64},{64,7... | collective-permute-start | bytes 3145736 | tf_op jit(solution)/shard_map/ppermute | solution.py:158

commit v2 on v1

v2 whole, which is shorter than its diff:
```python
import jax
import jax.numpy as jnp
from jax import lax
from jax.experimental import pallas as pl
from jax.experimental.pallas import tpu as pltpu
from jax.sharding import PartitionSpec as P

WIN = 1024
HALF = 512
BLOCK = 256
TICKS = 2
PIECES = 8
VROWS = WIN // PIECES
TROWS = 24
PROWS = VROWS + TROWS
SPAN = WIN + 16
EXT = WIN + HALF + 16
MIB = 1024 * 1024
F32 = jnp.float32
BF16 = jnp.bfloat16
NN = ((1,), (0,))
TN = ((0,), (0,))

SMEM = pl.BlockSpec(memory_space=pltpu.SMEM)
VMEM = pl.BlockSpec(memory_space=pltpu.VMEM)
HBM = pl.BlockSpec(memory_space=pltpu.HBM)


def split(x):
    hi = x.astype(BF16)
    return hi, (x - hi.astype(F32)).astype(BF16)


def mm(a, b, dims):
    return lax.dot_general(a, b, (dims, ((), ())), preferred_element_type=F32)


def mm3(ah, al, bh, bl, dims):
    return mm(ah, bh, dims) + mm(ah, bl, dims) + mm(al, bh, dims)


def hbm(*arrays):
    return [pltpu.with_memory_space_constraint(a, pltpu.HBM) for a in arrays]


def vmem(*arrays):
    return [pltpu.with_memory_space_constraint(a, pltpu.VMEM) for a in arrays]


def cost(flops, moved):
    return pl.CostEstimate(flops=flops, bytes_accessed=moved, transcendentals=0)


def pack_kernel(vectors, factor, block, sems):
    copies = []
    for k in range(PIECES):
        pairs = (
            (vectors.at[0, 0, pl.ds(k * VROWS, VROWS)], block.at[k, pl.ds(0, VROWS)]),
            (factor.at[0, 0, pl.ds(k * 16, 16)], block.at[k, pl.ds(VROWS, 16)]),
            (factor.at[0, 0, pl.ds(128 + k * 8, 8), pl.ds(128, 128)], block.at[k, pl.ds(VROWS + 16, 8), pl.ds(0, 128)]),
            (factor.at[0, 0, pl.ds(192 + k * 8, 8), pl.ds(128, 128)], block.at[k, pl.ds(VROWS + 16, 8), pl.ds(128, 128)]),
        )
        for n, (src, dst) in enumerate(pairs):
            copies.append(pltpu.make_async_copy(src, dst, sems.at[k, n]))
    for copy in copies:
        copy.start()
    for copy in copies:
        copy.wait()


def pack(reflectors, tfactors):
    return pl.pallas_call(
        pack_kernel,
        out_shape=pltpu.VMEM((PIECES, PROWS, BLOCK), F32),
        in_specs=[HBM, HBM],
        out_specs=VMEM,
        scratch_shapes=[pltpu.SemaphoreType.DMA((PIECES, 4))],
        compiler_params=pltpu.CompilerParams(vmem_limit_bytes=4 * MIB),
        cost_estimate=cost(0, 3 * MIB),
        name="pack",
    )(*hbm(reflectors, tfactors))


def load_kernel(eig, ext, sem):
    copy = pltpu.make_async_copy(eig.at[pl.ds(eig.shape[0] - WIN, WIN)], ext.at[pl.ds(0, WIN)], sem)
    copy.start()
    copy.wait()


def load(eig):
    return pl.pallas_call(
        load_kernel,
        out_shape=pltpu.VMEM((EXT, eig.shape[1]), F32),
        in_specs=[HBM],
        out_specs=VMEM,
        scratch_shapes=[pltpu.SemaphoreType.DMA],
        compiler_params=pltpu.CompilerParams(vmem_limit_bytes=4 * MIB),
        cost_estimate=cost(0, 4 * MIB),
        name="load",
    )(*hbm(eig))


def head_kernel(eig, *refs):
    copy = pltpu.make_async_copy(eig.at[pl.ds(0, HALF)], refs[-2], refs[-1])
    copy.start()
    copy.wait()


def head(eig, after):
    return pl.pallas_call(
        head_kernel,
        out_shape=pltpu.VMEM((HALF, eig.shape[1]), F32),
        in_specs=[HBM] + [pl.BlockSpec(memory_space=pl.ANY)] * len(after),
        out_specs=VMEM,
        scratch_shapes=[pltpu.SemaphoreType.DMA],
        compiler_params=pltpu.CompilerParams(vmem_limit_bytes=4 * MIB),
        cost_estimate=cost(0, 2 * MIB),
        name="head",
    )(*hbm(eig), *after)


def update_kernel(where, offsets, start, halo, p, r, l, s, q, u, v, z, ext, bottom, vp, vh, vl, tf, wh, wl):
    row, col = where[0], where[1]
    x, here = col & 3, col & 4
    there = 4 - here
    right, left, across = (x + 1) & 3, (x + 3) & 3, (x + 2) & 3
    places = (here + x, here + right, here + left, here + across, there + x, there + right, there + left, there + across)
    ext[WIN : WIN + HALF, :] = halo[...]
    ext[WIN + HALF :, :] = jnp.zeros((EXT - WIN - HALF, ext.shape[1]), F32)
    for tick in range(TICKS):
        vp[tick, :8, :] = jnp.zeros((8, BLOCK), F32)
        vp[tick, WIN + 8 :, :] = jnp.zeros((16, BLOCK), F32)
        tf[tick, 128:, :128] = jnp.zeros((128, 128), F32)
        at = tick * PROWS
        for ref, k in zip((p, r, l, s, q, u, v, z), places):
            vp[tick, pl.ds(pl.multiple_of(k * VROWS + 8, 8), VROWS), :] = ref[at : at + VROWS, :]
            at16, at8 = at + VROWS, at + VROWS + 16
            tf[tick, pl.ds(pl.multiple_of(k * 16, 16), 16), :] = ref[at16 : at16 + 16, :]
            tf[tick, pl.ds(pl.multiple_of(128 + k * 8, 8), 8), 128:] = ref[at8 : at8 + 8, :128]
            tf[tick, pl.ds(pl.multiple_of(192 + k * 8, 8), 8), 128:] = ref[at8 : at8 + 8, 128:]
    for tick in range(TICKS):
        shift = offsets[tick, row] & 7
        tiles = pltpu.roll(vp[tick].reshape(SPAN // 8 + 1, 8, BLOCK), shift, 1)
        same = lax.broadcasted_iota(jnp.int32, (SPAN // 8, 8, BLOCK), 1) >= shift
        hi, lo = split(jnp.where(same, tiles[1:], tiles[:-1]).reshape(SPAN, BLOCK))
        vh[tick] = hi
        vl[tick] = lo
    for tick in range(TICKS):
        base = pl.multiple_of((offsets[tick, row] - WIN) >> 3 << 3, 8)
        fh, fl = split(tf[tick])
        hi, lo = split(ext[pl.ds(base, SPAN), :])
        wh[...] = hi
        wl[...] = lo
        ch, cl = split(mm3(vh[tick], vl[tick], wh[...], wl[...], TN))
        sh, sl = split(mm3(fh, fl, ch, cl, NN))
        for k in range(5):
            part = slice(k * 208, (k + 1) * 208)
            spot = pl.ds(pl.multiple_of(base + k * 208, 8), 208)
            ext[spot, :] = ext[spot, :] - mm3(vh[tick, part, :], vl[tick, part, :], sh, sl, NN)
    bottom[...] = ext[WIN : WIN + HALF, :]


def update(where, offsets, start, halo, pieces):
    columns = start.shape[1]
    return pl.pallas_call(
        update_kernel,
        out_shape=(pltpu.VMEM((EXT, columns), F32), pltpu.VMEM((HALF, columns), F32)),
        in_specs=[SMEM, SMEM] + [VMEM] * 10,
        out_specs=(VMEM, VMEM),
        input_output_aliases={2: 0},
        scratch_shapes=[
            pltpu.VMEM((TICKS, SPAN + 8, BLOCK), F32),
            pltpu.VMEM((TICKS, SPAN, BLOCK), BF16),
            pltpu.VMEM((TICKS, SPAN, BLOCK), BF16),
            pltpu.VMEM((TICKS, BLOCK, BLOCK), F32),
            pltpu.VMEM((SPAN, columns), BF16),
            pltpu.VMEM((SPAN, columns), BF16),
        ],
        compiler_params=pltpu.CompilerParams(vmem_limit_bytes=20 * MIB),
        cost_estimate=cost(6_000_000_000, 8 * MIB),
        name="update",
    )(where, offsets, *vmem(start), halo, *pieces)


def store_kernel(eig, ext, out, sems):
    rows = eig.shape[0]
    middle = pl.ds(HALF, rows - WIN - HALF)
    keep = pltpu.make_async_copy(eig.at[middle], out.at[middle], sems.at[0])
    store = pltpu.make_async_copy(ext.at[pl.ds(0, WIN)], out.at[pl.ds(rows - WIN, WIN)], sems.at[1])
    keep.start()
    store.start()
    keep.wait()
    store.wait()


def store(eig, ext):
    return pl.pallas_call(
        store_kernel,
        out_shape=pltpu.HBM(eig.shape, F32),
        in_specs=[HBM, VMEM],
        out_specs=HBM,
        scratch_shapes=[pltpu.SemaphoreType.DMA((2,))],
        compiler_params=pltpu.CompilerParams(vmem_limit_bytes=8 * MIB),
        cost_estimate=cost(0, 8 * MIB),
        name="store",
    )(*hbm(eig), *vmem(ext))


def finish_kernel(where, eig, upper, old, out, sem):
    head = out.at[pl.ds(0, HALF)]

    @pl.when(where[0] > 0)
    def _():
        copy = pltpu.make_async_copy(upper, head, sem)
        copy.start()
        copy.wait()

    @pl.when(where[0] == 0)
    def _():
        copy = pltpu.make_async_copy(eig.at[pl.ds(0, HALF)], head, sem)
        copy.start()
        copy.wait()


def finish(where, eig, upper, out):
    return pl.pallas_call(
        finish_kernel,
        out_shape=pltpu.HBM(eig.shape, F32),
        in_specs=[SMEM, HBM, VMEM, HBM],
        out_specs=HBM,
        input_output_aliases={3: 0},
        scratch_shapes=[pltpu.SemaphoreType.DMA],
        compiler_params=pltpu.CompilerParams(vmem_limit_bytes=4 * MIB),
        cost_estimate=cost(0, 2 * MIB),
        name="finish",
    )(where, *hbm(eig), *vmem(upper), *hbm(out))


def per_device(eigvec, reflectors, tfactors, offsets, owners):
    row = lax.axis_index("row")
    col = lax.axis_index("col")
    where = jnp.stack([row, col]).astype(jnp.int32)
    count = lax.axis_size("row")
    source = lax.dynamic_slice_in_dim(owners, row, 1, 1)[:, 0]

    def from_x(value, d):
        return lax.ppermute(value, "col", [((i // 4) * 4 + (i % 4 + d) % 4, i) for i in range(8)])

    def from_y(value):
        return lax.ppermute(value, "col", [(i, i ^ 4) for i in range(8)])

    mine = lax.all_to_all(pack(reflectors, tfactors), "col", 0, 0)
    start = load(eigvec)
    p = jnp.concatenate([lax.dynamic_index_in_dim(mine, source[t], 0, keepdims=False) for t in range(TICKS)], 0)
    q, s, r, l = from_y(p), from_x(p, 2), from_x(p, 1), from_x(p, -1)
    u, v, z = from_x(q, 1), from_x(q, -1), from_y(s)
    top = head(eigvec, (q, s, r, l))
    halo = lax.ppermute(top, "row", [(i + 1, i) for i in range(count - 1)])

    ext, bottom = update(where, offsets, start, halo, (p, r, l, s, q, u, v, z))
    upper = lax.ppermute(bottom, "row", [(i, i + 1) for i in range(count - 1)])
    return finish(where, eigvec, upper, store(eigvec, ext))


def solution(mesh):
    return jax.shard_map(
        per_device,
        mesh=mesh,
        in_specs=(
            P("row", "col"),
            P("row", "col", None, None),
            P("row", "col", None, None),
            P(),
            P(),
        ),
        out_specs=P("row", "col"),
        check_vma=False,
    )
```

time: 99.9 us -> 150 us (1.50)
  the two profiles are of different devices: /device:TPU:128 before, /device:TPU:6 now
where the time goes in v2:
time: 150 us
  Pallas kernels  80.2 us (53%)
  waiting for transfers between devices  43.8 us (29%)
  starting transfers between devices  19.1 us (13%)
  between operations  3.9 us (3%)
  local copies, waits for them, and re-layouts  2.63 us (2%)
    pallas_call x1, Pallas kernels, finish(): pl.pallas_call(finish_kernel, out_shape=pltpu.HBM(eig.shape, F32), in_spe...  33.4 us
    pallas_call x1, Pallas kernels, store(): pl.pallas_call(store_kernel, out_shape=pltpu.HBM(eig.shape, F32), in_spec...  32.9 us
    ppermute x2, waiting for transfers between devices, from_y(): return lax.ppermute(value, 'col', [(i, i ^ 4) for i in range(8)])  17.9 us
    ppermute x5, waiting for transfers between devices, from_x(): lax.ppermute(value, 'col', [(i // 4 * 4 + (i % 4 + d) % 4, i) for i in ra...  13.7 us
    all_to_all x1, waiting for transfers between devices, per_device(): mine = lax.all_to_all(pack(reflectors, tfactors), 'col', 0, 0)  12.2 us
    all_to_all x1, starting transfers between devices, per_device(): mine = lax.all_to_all(pack(reflectors, tfactors), 'col', 0, 0)  7.42 us
    pallas_call x1, Pallas kernels, update(): pl.pallas_call(update_kernel, out_shape=(pltpu.VMEM((EXT, columns), F32),...  7.24 us
    ppermute x5, starting transfers between devices, from_x(): lax.ppermute(value, 'col', [(i // 4 * 4 + (i % 4 + d) % 4, i) for i in ra...  7.1 us
  transfers between devices with their start and end apart: 10, of which 4 were waited for; matrix products, arithmetic and copies ran while one was open for 0% of the time, Pallas kernels for 23%

profile of v2, /device:TPU:6, one launch (start us, length us, event | category | flops | bytes accessed | tf_op | source)
XLA Modules:
  0.0 149.7 jit_solution(2826738886222673277)
XLA Ops:
  0.0 0.0 copy-start
  0.0 2.8 %pack.1 = f32[8,152,256]{2,1,0:T(8,128)} custom-call(f32[1,1,1024,256]{3,2,1,0:T(8,128)} %vectors.1, f32[1,1,256,256]{3,2,1,0:T(8,128)} %factor.1), custom_call_target="tpu_custom_call" | custom-call | bytes 3145728 | tf_op jit(solution)/shard_map/pack/pallas_call | solution.py:72
  2.8 7.4 %all-to-all-start = ((f32[8,152,256]{2,1,0:T(8,128)}), f32[8,152,256]{2,1,0:T(8,128)S(1)}, u32[]{:S(2)}, u32[]{:S(2)}) async-start(f32[8,152,256]{2,1,0:T(8,128)} %pack.1), calls=%async_computation | async-start | bytes 2490368 | tf_op jit(solution)/shard_map/all_to_all | solution.py:252
  10.2 0.0 copy-done
  10.2 0.1 constant_dynamic-slice_fusion
  10.3 0.6 fusion
  14.6 12.2 %all-to-all-done = f32[8,152,256]{2,1,0:T(8,128)S(1)} async-done(((f32[8,152,256]{2,1,0:T(8,128)}), f32[8,152,256]{2,1,0:T(8,128)S(1)}, u32[]{:S(2)}, u32[]{:S(2)}) %all-to-all-start) | async-done | bytes 1245216 | tf_op jit(solution)/shard_map/all_to_all | solution.py:252
  26.9 0.0 copy-start.3
  26.9 2.8 %collective-permute-start.3 = (f32[304,256]{1,0:T(8,128)S(1)}, f32[304,256]{1,0:T(8,128)S(1)}, u32[]{:S(2)}, u32[]{:S(2)}) collective-permute-start(f32[304,256]{1,0:T(8,128)S(1)} %pad_maximum_fusion.p), channel_id=1, source_target_pairs={{3,0},{0,1},{1,2},{2,3},{7,4},{4,5},{5,6},{6,7},{11,8},{8,9},{9,10... | collective-permute-start | bytes 933896 | tf_op jit(solution)/shard_map/ppermute | solution.py:247
  29.6 0.0 collective-permute-start.2
  29.6 2.3 %collective-permute-start.1 = (f32[304,256]{1,0:T(8,128)S(1)}, f32[304,256]{1,0:T(8,128)}, u32[]{:S(2)}, u32[]{:S(2)}) collective-permute-start(f32[304,256]{1,0:T(8,128)S(1)} %pad_maximum_fusion.p), channel_id=1, source_target_pairs={{2,0},{3,1},{0,2},{1,3},{6,4},{7,5},{4,6},{5,7},{10,8},{11,9},{8,1... | collective-permute-start | bytes 933896 | tf_op jit(solution)/shard_map/ppermute | solution.py:247
  32.0 0.6 collective-permute-start
  32.5 10.3 %collective-permute-done.3.refs_3_.l = f32[304,256]{1,0:T(8,128)S(1)} collective-permute-done((f32[304,256]{1,0:T(8,128)S(1)}, f32[304,256]{1,0:T(8,128)S(1)}, u32[]{:S(2)}, u32[]{:S(2)}) %collective-permute-start.3) | collective-permute-done | bytes 311328 | tf_op jit(solution)/shard_map/ppermute | solution.py:247
  42.8 3.4 %collective-permute-done.2.refs_2_.r = f32[304,256]{1,0:T(8,128)S(1)} collective-permute-done((f32[304,256]{1,0:T(8,128)S(1)}, f32[304,256]{1,0:T(8,128)S(1)}, u32[]{:S(2)}, u32[]{:S(2)}) %collective-permute-start.2) | collective-permute-done | bytes 311328 | tf_op jit(solution)/shard_map/ppermute | solution.py:247
  46.2 0.0 copy-start.1
  46.2 0.0 collective-permute-done.1.refs_1_.s
  46.2 0.0 collective-permute-done.refs_0_.q
  46.2 2.3 %head.1 = f32[512,512]{1,0:T(8,128)} custom-call(f32[2048,512]{1,0:T(8,128)} %eig.7, f32[304,256]{1,0:T(8,128)} %collective-permute-done.refs_0_.q, f32[304,256]{1,0:T(8,128)} %collective-permute-done.1.refs_1_.s, f32[304,256]{1,0:T(8,128)S(1)} %collective-permute-done.2.refs_2_.r, f32[304,256]{1,0:T(8,128)S(1)} %collective-permute-done.3.refs_3_.l), custom_call_target="tpu_custom_call" | custom-call | bytes 2097152 | tf_op jit(solution)/shard_map/head/pallas_call | solution.py:110
  48.5 0.0 copy-done.3
  48.5 0.0 copy-done.1
  48.5 0.0 copy-start.5
  48.5 1.3 collective-permute-start.4
  49.8 0.6 collective-permute-start.7
  50.5 0.3 collective-permute-start.6
  50.8 1.7 %collective-permute-start.5 = (f32[304,256]{1,0:T(8,128)}, f32[304,256]{1,0:T(8,128)}, u32[]{:S(2)}, u32[]{:S(2)}) collective-permute-start(f32[304,256]{1,0:T(8,128)} %collective-permute-done.refs_0_.q), channel_id=1, source_target_pairs={{1,0},{2,1},{3,2},{0,3},{5,4},{6,5},{7,6},{4,7},{9,8},{10,9},{11,1... | collective-permute-start | bytes 933896 | tf_op jit(solution)/shard_map/ppermute | solution.py:247
  52.5 1.6 %load.1.start = f32[1552,512]{1,0:T(8,128)S(1)} custom-call(f32[2048,512]{1,0:T(8,128)} %eig.7), custom_call_target="tpu_custom_call" | custom-call | bytes 4194304 | tf_op jit(solution)/shard_map/load/pallas_call | solution.py:91
  54.1 0.1 pad_add_fusion.where
  54.2 17.9 %collective-permute-done.7.z = f32[304,256]{1,0:T(8,128)} collective-permute-done((f32[304,256]{1,0:T(8,128)}, f32[304,256]{1,0:T(8,128)}, u32[]{:S(2)}, u32[]{:S(2)}) %collective-permute-start.7) | collective-permute-done | bytes 311328 | tf_op jit(solution)/shard_map/ppermute | solution.py:250
  72.1 0.0 collective-permute-done.6.v
  72.1 0.0 collective-permute-done.5.u
  72.1 0.0 collective-permute-done.4.halo
  72.1 0.0 copy-done.5
  72.1 0.0 copy-start.2
  72.1 1.0 copy-done.2
  73.1 0.0 copy-start.4
  73.1 1.0 copy-done.4
  74.1 7.2 %update.1 = (f32[1552,512]{1,0:T(8,128)S(1)}, f32[512,512]{1,0:T(8,128)S(1)}) custom-call(s32[2]{0:T(128)S(1)} %pad_add_fusion.where, s32[2,32]{1,0:T(2,128)S(1)} %copy-done.5, f32[1552,512]{1,0:T(8,128)S(1)} %load.1.start, f32[512,512]{1,0:T(8,128)} %collective-permute-done.4.halo, f32[304,256]{1,0:T(8,128)S(1)} %copy-done.4, ...), custom_call_target="tpu_custom_call", output_to_operand_aliasing={{0}: (2, {})} | custom-call | flops 6000000000 | bytes 8388608 | tf_op jit(solution)/shard_map/update/pallas_call | solution.py:165
  81.3 2.1 %collective-permute-start.8 = (f32[512,512]{1,0:T(8,128)S(1)}, f32[512,512]{1,0:T(8,128)S(1)}, u32[]{:S(2)}, u32[]{:S(2)}) collective-permute-start(f32[512,512]{1,0:T(8,128)S(1)} %get-tuple-element.7), channel_id=1, source_target_pairs={{0,8},{8,16},{16,24},{24,32},{32,40},{40,48},{48,56},{56,64},{64,7... | collective-permute-start | bytes 3145736 | tf_op jit(solution)/shard_map/ppermute | solution.py:261
  83.4 32.9 %store.1.old = f32[2048,512]{1,0:T(8,128)} custom-call(f32[2048,512]{1,0:T(8,128)} %eig.7, f32[1552,512]{1,0:T(8,128)S(1)} %get-tuple-element.8.ext), custom_call_target="tpu_custom_call" | custom-call | bytes 8388608 | tf_op jit(solution)/shard_map/store/pallas_call | solution.py:197
  116.3 0.0 collective-permute-done.8.upper
  116.3 33.4 %finish.1 = f32[2048,512]{1,0:T(8,128)} custom-call(s32[2]{0:T(128)S(1)} %pad_add_fusion.where, f32[2048,512]{1,0:T(8,128)} %eig.7, f32[512,512]{1,0:T(8,128)S(1)} %collective-permute-done.8.upper, f32[2048,512]{1,0:T(8,128)} %store.1.old), custom_call_target="tpu_custom_call", output_to_operand_aliasing={{}: (3, {})} | custom-call | bytes 2097152 | tf_op jit(solution)/shard_map/finish/pallas_call | solution.py:226
  (2 shorter events, 0.0 us)
Async XLA Ops:
  0.0 10.2 %copy-start = (s32[2,32]{1,0:T(2,128)S(1)}, s32[2,32]{1,0:T(2,128)}, u32[]{:S(2)}) copy-start(s32[2,32]{1,0:T(2,128)} %param.9) | copy-start | bytes 772
  2.8 24.1 %all-to-all-start = ((f32[8,152,256]{2,1,0:T(8,128)}), f32[8,152,256]{2,1,0:T(8,128)S(1)}, u32[]{:S(2)}, u32[]{:S(2)}) async-start(f32[8,152,256]{2,1,0:T(8,128)} %pack.1), calls=%async_computation | async-start | bytes 2490368 | tf_op jit(solution)/shard_map/all_to_all | solution.py:252
  26.9 21.6 %copy-start.3 = (f32[304,256]{1,0:T(8,128)}, f32[304,256]{1,0:T(8,128)S(1)}, u32[]{:S(2)}) copy-start(f32[304,256]{1,0:T(8,128)S(1)} %pad_maximum_fusion.p) | copy-start | bytes 933892
  26.9 15.9 %collective-permute-start.3 = (f32[304,256]{1,0:T(8,128)S(1)}, f32[304,256]{1,0:T(8,128)S(1)}, u32[]{:S(2)}, u32[]{:S(2)}) collective-permute-start(f32[304,256]{1,0:T(8,128)S(1)} %pad_maximum_fusion.p), channel_id=1, source_target_pairs={{3,0},{0,1},{1,2},{2,3},{7,4},{4,5},{5,6},{6,7},{11,8},{8,9},{9,10... | collective-permute-start | bytes 933896 | tf_op jit(solution)/shard_map/ppermute | solution.py:247
  29.6 16.5 %collective-permute-start.2 = (f32[304,256]{1,0:T(8,128)S(1)}, f32[304,256]{1,0:T(8,128)S(1)}, u32[]{:S(2)}, u32[]{:S(2)}) collective-permute-start(f32[304,256]{1,0:T(8,128)S(1)} %pad_maximum_fusion.p), channel_id=1, source_target_pairs={{1,0},{2,1},{3,2},{0,3},{5,4},{6,5},{7,6},{4,7},{9,8},{10,9},{11,1... | collective-permute-start | bytes 933896 | tf_op jit(solution)/shard_map/ppermute | solution.py:247
  29.6 16.5 %collective-permute-start.1 = (f32[304,256]{1,0:T(8,128)S(1)}, f32[304,256]{1,0:T(8,128)}, u32[]{:S(2)}, u32[]{:S(2)}) collective-permute-start(f32[304,256]{1,0:T(8,128)S(1)} %pad_maximum_fusion.p), channel_id=1, source_target_pairs={{2,0},{3,1},{0,2},{1,3},{6,4},{7,5},{4,6},{5,7},{10,8},{11,9},{8,1... | collective-permute-start | bytes 933896 | tf_op jit(solution)/shard_map/ppermute | solution.py:247
  32.0 14.2 %collective-permute-start = (f32[304,256]{1,0:T(8,128)S(1)}, f32[304,256]{1,0:T(8,128)}, u32[]{:S(2)}, u32[]{:S(2)}) collective-permute-start(f32[304,256]{1,0:T(8,128)S(1)} %pad_maximum_fusion.p), channel_id=1, source_target_pairs={{0,4},{1,5},{2,6},{3,7},{4,0},{5,1},{6,2},{7,3},{8,12},{9,13},{10,... | collective-permute-start | bytes 933896 | tf_op jit(solution)/shard_map/ppermute | solution.py:250
  46.2 2.3 %copy-start.1 = (f32[304,256]{1,0:T(8,128)}, f32[304,256]{1,0:T(8,128)S(1)}, u32[]{:S(2)}) copy-start(f32[304,256]{1,0:T(8,128)S(1)} %collective-permute-done.2.refs_2_.r) | copy-start | bytes 933892
  48.5 23.6 %copy-start.5 = (s32[2,32]{1,0:T(2,128)S(1)}, s32[2,32]{1,0:T(2,128)}, u32[]{:S(2)}) copy-start(s32[2,32]{1,0:T(2,128)} %offsets.1) | copy-start | bytes 772
  48.5 23.6 %collective-permute-start.4 = (f32[512,512]{1,0:T(8,128)}, f32[512,512]{1,0:T(8,128)}, u32[]{:S(2)}, u32[]{:S(2)}) collective-permute-start(f32[512,512]{1,0:T(8,128)} %head.1), channel_id=1, source_target_pairs={{8,0},{16,8},{24,16},{32,24},{40,32},{48,40},{56,48},{64,56},{72,6... | collective-permute-start | bytes 3145736 | tf_op jit(solution)/shard_map/ppermute | solution.py:258
  49.8 22.3 %collective-permute-start.7 = (f32[304,256]{1,0:T(8,128)}, f32[304,256]{1,0:T(8,128)}, u32[]{:S(2)}, u32[]{:S(2)}) collective-permute-start(f32[304,256]{1,0:T(8,128)} %collective-permute-done.1.refs_1_.s), channel_id=1, source_target_pairs={{0,4},{1,5},{2,6},{3,7},{4,0},{5,1},{6,2},{7,3},{8,12},{9,13},{10,... | collective-permute-start | bytes 933896 | tf_op jit(solution)/shard_map/ppermute | solution.py:250
  50.5 21.6 %collective-permute-start.6 = (f32[304,256]{1,0:T(8,128)}, f32[304,256]{1,0:T(8,128)}, u32[]{:S(2)}, u32[]{:S(2)}) collective-permute-start(f32[304,256]{1,0:T(8,128)} %collective-permute-done.refs_0_.q), channel_id=1, source_target_pairs={{3,0},{0,1},{1,2},{2,3},{7,4},{4,5},{5,6},{6,7},{11,8},{8,9},{9,10... | collective-permute-start | bytes 933896 | tf_op jit(solution)/shard_map/ppermute | solution.py:247
  50.8 21.3 %collective-permute-start.5 = (f32[304,256]{1,0:T(8,128)}, f32[304,256]{1,0:T(8,128)}, u32[]{:S(2)}, u32[]{:S(2)}) collective-permute-start(f32[304,256]{1,0:T(8,128)} %collective-permute-done.refs_0_.q), channel_id=1, source_target_pairs={{1,0},{2,1},{3,2},{0,3},{5,4},{6,5},{7,6},{4,7},{9,8},{10,9},{11,1... | collective-permute-start | bytes 933896 | tf_op jit(solution)/shard_map/ppermute | solution.py:247
  72.1 1.0 copy-start.2
  73.1 1.0 copy-start.4
  81.3 35.0 %collective-permute-start.8 = (f32[512,512]{1,0:T(8,128)S(1)}, f32[512,512]{1,0:T(8,128)S(1)}, u32[]{:S(2)}, u32[]{:S(2)}) collective-permute-start(f32[512,512]{1,0:T(8,128)S(1)} %get-tuple-element.7), channel_id=1, source_target_pairs={{0,8},{8,16},{16,24},{24,32},{32,40},{40,48},{48,56},{56,64},{64,7... | collective-permute-start | bytes 3145736 | tf_op jit(solution)/shard_map/ppermute | solution.py:261

commit v3 on v2

v3 whole, which is shorter than its diff:
```python
import jax
import jax.numpy as jnp
from jax import lax
from jax.experimental import pallas as pl
from jax.experimental.pallas import tpu as pltpu
from jax.sharding import PartitionSpec as P

WIN = 1024
HALF = 512
BLOCK = 256
TICKS = 2
PIECES = 8
VROWS = WIN // PIECES
TROWS = 24
PROWS = VROWS + TROWS
SPAN = WIN + 16
REACH = WIN + HALF
MIB = 1024 * 1024
F32 = jnp.float32
BF16 = jnp.bfloat16
NN = ((1,), (0,))
TN = ((0,), (0,))

SMEM = pl.BlockSpec(memory_space=pltpu.SMEM)
VMEM = pl.BlockSpec(memory_space=pltpu.VMEM)
ANY = pl.BlockSpec(memory_space=pl.ANY)
HBM = pl.BlockSpec(memory_space=pltpu.HBM)


def split(x):
    hi = x.astype(BF16)
    return hi, (x - hi.astype(F32)).astype(BF16)


def mm(a, b, dims):
    return lax.dot_general(a, b, (dims, ((), ())), preferred_element_type=F32)


def mm3(ah, al, bh, bl, dims):
    return mm(ah, bh, dims) + mm(ah, bl, dims) + mm(al, bh, dims)


def hbm(*arrays):
    return [pltpu.with_memory_space_constraint(a, pltpu.HBM) for a in arrays]


def vmem(*arrays):
    return [pltpu.with_memory_space_constraint(a, pltpu.VMEM) for a in arrays]


def cost(flops, moved):
    return pl.CostEstimate(flops=flops, bytes_accessed=moved, transcendentals=0)


def pack_kernel(vectors, factor, eig, block, top, sems, first):
    lead = pltpu.make_async_copy(eig.at[pl.ds(0, HALF)], top, first)
    lead.start()
    copies = []
    for k in range(PIECES):
        pairs = (
            (vectors.at[0, 0, pl.ds(k * VROWS, VROWS)], block.at[k, pl.ds(0, VROWS)]),
            (factor.at[0, 0, pl.ds(k * 16, 16)], block.at[k, pl.ds(VROWS, 16)]),
            (factor.at[0, 0, pl.ds(128 + k * 8, 8), pl.ds(128, 128)], block.at[k, pl.ds(VROWS + 16, 8), pl.ds(0, 128)]),
            (factor.at[0, 0, pl.ds(192 + k * 8, 8), pl.ds(128, 128)], block.at[k, pl.ds(VROWS + 16, 8), pl.ds(128, 128)]),
        )
        for n, (src, dst) in enumerate(pairs):
            copies.append(pltpu.make_async_copy(src, dst, sems.at[k, n]))
    for copy in copies:
        copy.start()
    lead.wait()
    for copy in copies:
        copy.wait()


def pack(reflectors, tfactors, eig):
    return pl.pallas_call(
        pack_kernel,
        out_shape=(jax.ShapeDtypeStruct((PIECES, PROWS, BLOCK), F32), jax.ShapeDtypeStruct((HALF, eig.shape[1]), F32)),
        in_specs=[HBM, HBM, HBM],
        out_specs=(VMEM, VMEM),
        scratch_shapes=[pltpu.SemaphoreType.DMA((PIECES, 4)), pltpu.SemaphoreType.DMA],
        compiler_params=pltpu.CompilerParams(vmem_limit_bytes=6 * MIB),
        cost_estimate=cost(0, 5 * MIB),
        name="pack",
    )(*hbm(reflectors, tfactors, eig))


def stage_kernel(eig, halo, wh, wl, rows, sems):
    upper = pltpu.make_async_copy(eig.at[pl.ds(eig.shape[0] - WIN, WIN)], rows.at[pl.ds(0, WIN)], sems.at[0])
    lower = pltpu.make_async_copy(halo, rows.at[pl.ds(WIN, HALF)], sems.at[1])
    upper.start()
    lower.start()
    upper.wait()
    lower.wait()
    wh[...], wl[...] = split(rows[...])


def stage(eig, halo):
    columns = eig.shape[1]
    return pl.pallas_call(
        stage_kernel,
        out_shape=(jax.ShapeDtypeStruct((REACH, columns), BF16), jax.ShapeDtypeStruct((REACH, columns), BF16)),
        in_specs=[HBM, ANY],
        out_specs=(VMEM, VMEM),
        scratch_shapes=[pltpu.VMEM((REACH, columns), F32), pltpu.SemaphoreType.DMA((2,))],
        compiler_params=pltpu.CompilerParams(vmem_limit_bytes=10 * MIB),
        cost_estimate=cost(0, 9 * MIB),
        name="stage",
    )(*hbm(eig), halo)


def update_kernel(where, offsets, wh, wl, halo, p, r, l, s, q, u, v, z, bottom, vh, vl, sh, sl, vp, tp, va, low, sems, last):
    row, col = where[0], where[1]
    x, here = col & 3, col & 4
    there = 4 - here
    right, left, across = (x + 1) & 3, (x + 3) & 3, (x + 2) & 3
    places = (here + x, here + right, here + left, here + across, there + x, there + right, there + left, there + across)
    copies = []
    for tick in range(TICKS):
        for n, (ref, k) in enumerate(zip((p, r, l, s, q, u, v, z), places)):
            spot = pl.ds(pl.multiple_of(k * VROWS + 8, 8), VROWS)
            copies.append(pltpu.make_async_copy(ref.at[pl.ds(tick * PROWS, VROWS)], vp.at[tick, spot], sems.at[tick, n, 0]))
            spot = pl.ds(pl.multiple_of(k * TROWS, 8), TROWS)
            copies.append(pltpu.make_async_copy(ref.at[pl.ds(tick * PROWS + VROWS, TROWS)], tp.at[tick, spot], sems.at[tick, n, 1]))
    for copy in copies:
        copy.start()
    tail = pltpu.make_async_copy(halo, low, last)
    tail.start()
    for tick in range(TICKS):
        vp[tick, :8, :] = jnp.zeros((8, BLOCK), F32)
        vp[tick, WIN + 8 :, :] = jnp.zeros((16, BLOCK), F32)
        va[tick] = jnp.zeros((REACH + 16, BLOCK), F32)
    for copy in copies:
        copy.wait()
    factors = []
    for tick in range(TICKS):
        shift = offsets[tick, row] & 7
        base = pl.multiple_of((offsets[tick, row] - WIN) >> 3 << 3, 8)
        tiles = pltpu.roll(vp[tick].reshape(SPAN // 8 + 1, 8, BLOCK), shift, 1)
        same = lax.broadcasted_iota(jnp.int32, (SPAN // 8, 8, BLOCK), 1) >= shift
        va[tick, pl.ds(base, SPAN), :] = jnp.where(same, tiles[1:], tiles[:-1]).reshape(SPAN, BLOCK)
        part = slice(tick * BLOCK, (tick + 1) * BLOCK)
        vh[:, part], vl[:, part] = split(va[tick, :REACH, :])
        packed = tp[tick].reshape(PIECES, TROWS, BLOCK)
        corner = jnp.concatenate([packed[:, 16:, :128].reshape(64, 128), packed[:, 16:, 128:].reshape(64, 128)], 0)
        lower = jnp.concatenate([jnp.zeros((128, 128), F32), corner], 1)
        factors.append(split(jnp.concatenate([packed[:, :16, :].reshape(128, BLOCK), lower], 0)))
    coef = mm3(vh[...], vl[...], wh[...], wl[...], TN)
    cross = split(mm3(vh[:, BLOCK:], vl[:, BLOCK:], vh[:, :BLOCK], vl[:, :BLOCK], TN))
    first = split(mm3(*factors[0], *split(coef[:BLOCK]), NN))
    second = split(mm3(*factors[1], *split(coef[BLOCK:] - mm3(*cross, *first, NN)), NN))
    sh[:BLOCK, :], sl[:BLOCK, :] = first
    sh[BLOCK:, :], sl[BLOCK:, :] = second
    tail.wait()
    bottom[...] = low[...] - mm3(vh[WIN:, :], vl[WIN:, :], sh[...], sl[...], NN)


def update(where, offsets, wh, wl, halo, pieces):
    columns = halo.shape[1]
    both = TICKS * BLOCK
    return pl.pallas_call(
        update_kernel,
        out_shape=(
            jax.ShapeDtypeStruct((HALF, columns), F32),
            jax.ShapeDtypeStruct((REACH, both), BF16),
            jax.ShapeDtypeStruct((REACH, both), BF16),
            jax.ShapeDtypeStruct((both, columns), BF16),
            jax.ShapeDtypeStruct((both, columns), BF16),
        ),
        in_specs=[SMEM, SMEM, VMEM, VMEM] + [ANY] * 9,
        out_specs=(VMEM,) * 5,
        scratch_shapes=[
            pltpu.VMEM((TICKS, SPAN + 8, BLOCK), F32),
            pltpu.VMEM((TICKS, PIECES * TROWS, BLOCK), F32),
            pltpu.VMEM((TICKS, REACH + 16, BLOCK), F32),
            pltpu.VMEM((HALF, columns), F32),
            pltpu.SemaphoreType.DMA((TICKS, PIECES, 2)),
            pltpu.SemaphoreType.DMA,
        ],
        compiler_params=pltpu.CompilerParams(vmem_limit_bytes=24 * MIB),
        cost_estimate=cost(5_000_000_000, 8 * MIB),
        name="update",
    )(where, offsets, wh, wl, halo, *pieces)


def store_kernel(eig, vh, vl, sh, sl, out, rows, middle, sems):
    count = eig.shape[0]
    spot = pl.ds(HALF, count - WIN - HALF)
    load = pltpu.make_async_copy(eig.at[pl.ds(count - WIN, WIN)], rows, sems.at[0])
    fetch = pltpu.make_async_copy(eig.at[spot], middle, sems.at[1])
    load.start()
    fetch.start()
    fetch.wait()
    keep = pltpu.make_async_copy(middle, out.at[spot], sems.at[2])
    keep.start()
    load.wait()
    for k in range(4):
        part = slice(k * 256, (k + 1) * 256)
        rows[part, :] = rows[part, :] - mm3(vh[part, :], vl[part, :], sh[...], sl[...], NN)
    store = pltpu.make_async_copy(rows, out.at[pl.ds(count - WIN, WIN)], sems.at[3])
    store.start()
    keep.wait()
    store.wait()


def store(eig, vh, vl, sh, sl):
    columns = eig.shape[1]
    return pl.pallas_call(
        store_kernel,
        out_shape=jax.ShapeDtypeStruct(eig.shape, F32),
        in_specs=[HBM] + [VMEM] * 4,
        out_specs=HBM,
        scratch_shapes=[
            pltpu.VMEM((WIN, columns), F32),
            pltpu.VMEM((eig.shape[0] - WIN - HALF, columns), F32),
            pltpu.SemaphoreType.DMA((4,)),
        ],
        compiler_params=pltpu.CompilerParams(vmem_limit_bytes=16 * MIB),
        cost_estimate=cost(1_600_000_000, 8 * MIB),
        name="store",
    )(*hbm(eig), vh, vl, sh, sl)


def finish_kernel(where, eig, upper, old, out, rows, sems):
    head = out.at[pl.ds(0, HALF)]

    @pl.when(where[0] > 0)
    def _():
        copy = pltpu.make_async_copy(upper, head, sems.at[0])
        copy.start()
        copy.wait()

    @pl.when(where[0] == 0)
    def _():
        fetch = pltpu.make_async_copy(eig.at[pl.ds(0, HALF)], rows, sems.at[1])
        fetch.start()
        fetch.wait()
        copy = pltpu.make_async_copy(rows, head, sems.at[2])
        copy.start()
        copy.wait()


def finish(where, eig, upper, out):
    return pl.pallas_call(
        finish_kernel,
        out_shape=pltpu.HBM(eig.shape, F32),
        in_specs=[SMEM, HBM, VMEM, HBM],
        out_specs=HBM,
        input_output_aliases={3: 0},
        scratch_shapes=[pltpu.VMEM((HALF, eig.shape[1]), F32), pltpu.SemaphoreType.DMA((3,))],
        compiler_params=pltpu.CompilerParams(vmem_limit_bytes=4 * MIB),
        cost_estimate=cost(0, 2 * MIB),
        name="finish",
    )(where, *hbm(eig), *vmem(upper), *hbm(out))


def per_device(eigvec, reflectors, tfactors, offsets, owners):
    row = lax.axis_index("row")
    col = lax.axis_index("col")
    where = jnp.stack([row, col]).astype(jnp.int32)
    count = lax.axis_size("row")
    source = lax.dynamic_slice_in_dim(owners, row, 1, 1)[:, 0]

    def from_x(value, d):
        return lax.ppermute(value, "col", [((i // 4) * 4 + (i % 4 + d) % 4, i) for i in range(8)])

    def from_y(value):
        return lax.ppermute(value, "col", [(i, i ^ 4) for i in range(8)])

    block, top = pack(reflectors, tfactors, eigvec)
    halo = lax.ppermute(top, "row", [(i + 1, i) for i in range(count - 1)])
    mine = lax.all_to_all(block, "col", 0, 0)
    p = jnp.concatenate([lax.dynamic_index_in_dim(mine, source[t], 0, keepdims=False) for t in range(TICKS)], 0)
    q, s, r, l = from_y(p), from_x(p, 2), from_x(p, 1), from_x(p, -1)
    u, v, z = from_x(q, 1), from_x(q, -1), from_y(s)
    wh, wl = stage(eigvec, halo)

    bottom, *rest = update(where, offsets, wh, wl, halo, (p, r, l, s, q, u, v, z))
    upper = lax.ppermute(bottom, "row", [(i, i + 1) for i in range(count - 1)])
    return finish(where, eigvec, upper, store(eigvec, *rest))


def solution(mesh):
    return jax.shard_map(
        per_device,
        mesh=mesh,
        in_specs=(
            P("row", "col"),
            P("row", "col", None, None),
            P("row", "col", None, None),
            P(),
            P(),
        ),
        out_specs=P("row", "col"),
        check_vma=False,
    )
```

time: 150 us -> 94.6 us (0.63)
  the two profiles are of different devices: /device:TPU:6 before, /device:TPU:128 now
where the time goes in v3:
time: 94.6 us; the launch traced here: 94.2 us
  waiting for transfers between devices  35.4 us (37%)
  starting transfers between devices  31.3 us (33%)
  Pallas kernels  22.2 us (23%)
  between operations  3.58 us (4%)
  local copies, waits for them, and re-layouts  1.64 us (2%)
    ppermute x5, starting transfers between devices, from_x(): lax.ppermute(value, 'col', [(i // 4 * 4 + (i % 4 + d) % 4, i) for i in ra...  18.5 us
    all_to_all x1, waiting for transfers between devices, per_device(): mine = lax.all_to_all(block, 'col', 0, 0)  16.7 us
    ppermute x1, waiting for transfers between devices, per_device(): upper = lax.ppermute(bottom, 'row', [(i, i + 1) for i in range(count - 1)])  11.3 us
    pallas_call x1, Pallas kernels, update(): pl.pallas_call(update_kernel, out_shape=(jax.ShapeDtypeStruct((HALF, colu...  10.3 us
    ppermute x5, waiting for transfers between devices, from_x(): lax.ppermute(value, 'col', [(i // 4 * 4 + (i % 4 + d) % 4, i) for i in ra...  7.33 us
    all_to_all x1, starting transfers between devices, per_device(): mine = lax.all_to_all(block, 'col', 0, 0)  6.94 us
    pallas_call x1, Pallas kernels, store(): pl.pallas_call(store_kernel, out_shape=jax.ShapeDtypeStruct(eig.shape, F3...  5 us
    pallas_call x1, Pallas kernels, pack(): pl.pallas_call(pack_kernel, out_shape=(jax.ShapeDtypeStruct((PIECES, PROW...  3.18 us
  transfers between devices with their start and end apart: 10, of which 6 were waited for; matrix products, arithmetic and copies ran while one was open for 2% of the time, Pallas kernels for 8%

profile of v3, /device:TPU:128, one launch (start us, length us, event | category | flops | bytes accessed | tf_op | source)
XLA Modules:
  0.0 94.2 jit_solution(4741308829094480138)
XLA Ops:
  0.0 0.0 copy-start
  0.0 3.2 %pack.1 = (f32[8,152,256]{2,1,0:T(8,128)}, f32[512,512]{1,0:T(8,128)S(1)}) custom-call(f32[1,1,1024,256]{3,2,1,0:T(8,128)} %vectors.1, f32[1,1,256,256]{3,2,1,0:T(8,128)} %factor.1, f32[2048,512]{1,0:T(8,128)} %eig.7), custom_call_target="tpu_custom_call" | custom-call | bytes 5242880 | tf_op jit(solution)/shard_map/pack/pallas_call | solution.py:76
  3.2 6.9 %all-to-all-start = ((f32[8,152,256]{2,1,0:T(8,128)}), f32[8,152,256]{2,1,0:T(8,128)}, u32[]{:S(2)}, u32[]{:S(2)}) async-start(f32[8,152,256]{2,1,0:T(8,128)} %get-tuple-element.17), calls=%async_computation | async-start | bytes 2490368 | tf_op jit(solution)/shard_map/all_to_all | solution.py:272
  10.1 1.9 %collective-permute-start = (f32[512,512]{1,0:T(8,128)S(1)}, f32[512,512]{1,0:T(8,128)S(1)}, u32[]{:S(2)}, u32[]{:S(2)}) collective-permute-start(f32[512,512]{1,0:T(8,128)S(1)} %get-tuple-element.14), channel_id=1, source_target_pairs={{8,0},{16,8},{24,16},{32,24},{40,32},{48,40},{56,48},{64,56},{72,6... | collective-permute-start | bytes 3145736 | tf_op jit(solution)/shard_map/ppermute | solution.py:271
  12.1 0.0 copy-done
  12.1 0.1 constant_dynamic-slice_fusion
  12.1 0.5 fusion
  16.2 16.7 %all-to-all-done = f32[8,152,256]{2,1,0:T(8,128)} async-done(((f32[8,152,256]{2,1,0:T(8,128)}), f32[8,152,256]{2,1,0:T(8,128)}, u32[]{:S(2)}, u32[]{:S(2)}) %all-to-all-start) | async-done | bytes 1245216 | tf_op jit(solution)/shard_map/all_to_all | solution.py:272
  32.9 1.0 %dynamic-slice_bitcast_fusion.1 = (f32[152,256]{1,0:T(8,128)S(1)}, f32[152,256]{1,0:T(8,128)S(1)}) fusion(f32[8,152,256]{2,1,0:T(8,128)} %all-to-all-done, s32[]{:T(128)S(6)} %select_n.11, s32[]{:T(128)S(6)} %select_n.12), kind=kLoop, calls=%fused_computation.2 | loop fusion | bytes 622600 | tf_op jit(solution)/shard_map/jit(dynamic_index_in_dim)/squeeze | solution.py:273
  34.0 0.8 collective-permute-start.4
  34.7 8.3 %collective-permute-start.3 = (f32[304,256]{1,0:T(8,128)S(1)}, f32[304,256]{1,0:T(8,128)S(1)}, u32[]{:S(2)}, u32[]{:S(2)}) collective-permute-start(f32[304,256]{1,0:T(8,128)S(1)} %pad_maximum_fusion.p), channel_id=1, source_target_pairs={{2,0},{3,1},{0,2},{1,3},{6,4},{7,5},{4,6},{5,7},{10,8},{11,9},{8,1... | collective-permute-start | bytes 933896 | tf_op jit(solution)/shard_map/ppermute | solution.py:265
  43.1 0.6 collective-permute-start.2
  43.6 2.7 %collective-permute-start.1 = (f32[304,256]{1,0:T(8,128)S(1)}, f32[304,256]{1,0:T(8,128)}, u32[]{:S(2)}, u32[]{:S(2)}) collective-permute-start(f32[304,256]{1,0:T(8,128)S(1)} %pad_maximum_fusion.p), channel_id=1, source_target_pairs={{1,0},{2,1},{3,2},{0,3},{5,4},{6,5},{7,6},{4,7},{9,8},{10,9},{11,1... | collective-permute-start | bytes 933896 | tf_op jit(solution)/shard_map/ppermute | solution.py:265
  46.3 0.0 collective-permute-done.4.q
  46.3 0.5 collective-permute-start.6
  46.8 0.0 collective-permute-done.halo
  46.8 6.4 %collective-permute-start.5 = (f32[304,256]{1,0:T(8,128)S(1)}, f32[304,256]{1,0:T(8,128)S(1)}, u32[]{:S(2)}, u32[]{:S(2)}) collective-permute-start(f32[304,256]{1,0:T(8,128)S(1)} %collective-permute-done.4.q), channel_id=1, source_target_pairs={{1,0},{2,1},{3,2},{0,3},{5,4},{6,5},{7,6},{4,7},{9,8},{10,9},{11,1... | collective-permute-start | bytes 933896 | tf_op jit(solution)/shard_map/ppermute | solution.py:265
  53.3 0.0 collective-permute-done.3.s
  53.3 1.3 %collective-permute-start.7 = (f32[304,256]{1,0:T(8,128)S(1)}, f32[304,256]{1,0:T(8,128)S(1)}, u32[]{:S(2)}, u32[]{:S(2)}) collective-permute-start(f32[304,256]{1,0:T(8,128)S(1)} %collective-permute-done.3.s), channel_id=1, source_target_pairs={{0,4},{1,5},{2,6},{3,7},{4,0},{5,1},{6,2},{7,3},{8,12},{9,13},{10,... | collective-permute-start | bytes 933896 | tf_op jit(solution)/shard_map/ppermute | solution.py:268
  54.5 0.1 pad_add_fusion.where
  54.6 0.0 copy-start.1
  54.6 2.1 %stage.1 = (bf16[1536,512]{1,0:T(8,128)(2,1)S(1)}, bf16[1536,512]{1,0:T(8,128)(2,1)S(1)}) custom-call(f32[2048,512]{1,0:T(8,128)} %eig.7, f32[512,512]{1,0:T(8,128)S(1)} %collective-permute-done.halo), custom_call_target="tpu_custom_call" | custom-call | bytes 9437184 | tf_op jit(solution)/shard_map/stage/pallas_call | solution.py:100
  56.8 0.7 collective-permute-done.2.l
  57.5 1.2 %collective-permute-done.1.r = f32[304,256]{1,0:T(8,128)} collective-permute-done((f32[304,256]{1,0:T(8,128)S(1)}, f32[304,256]{1,0:T(8,128)}, u32[]{:S(2)}, u32[]{:S(2)}) %collective-permute-start.1) | collective-permute-done | bytes 311328 | tf_op jit(solution)/shard_map/ppermute | solution.py:265
  58.7 5.2 %collective-permute-done.6.v = f32[304,256]{1,0:T(8,128)} collective-permute-done((f32[304,256]{1,0:T(8,128)S(1)}, f32[304,256]{1,0:T(8,128)}, u32[]{:S(2)}, u32[]{:S(2)}) %collective-permute-start.6) | collective-permute-done | bytes 311328 | tf_op jit(solution)/shard_map/ppermute | solution.py:265
  63.9 0.2 collective-permute-done.5.u
  64.1 0.0 collective-permute-done.7.z
  64.1 0.0 copy-done.1
  64.1 10.3 %update.1 = (f32[512,512]{1,0:T(8,128)S(1)}, bf16[1536,512]{1,0:T(8,128)(2,1)S(1)}, bf16[1536,512]{1,0:T(8,128)(2,1)S(1)}, bf16[512,512]{1,0:T(8,128)(2,1)S(1)}, bf16[512,512]{1,0:T(8,128)(2,1)S(1)}) custom-call(s32[2]{0:T(128)S(1)} %pad_add_fusion.where, s32[2,32]{1,0:T(2,128)S(1)} %copy-done.1, bf16[1536,512]{1,0:T(8,128)(2,1)S(1)} %get-tuple-element.15.wh, ...), custom_call_target="tpu_custom_call" | custom-call | flops 5000000000 | bytes 8388608 | tf_op jit(solution)/shard_map/update/pallas_call | solution.py:161
  74.4 1.9 %collective-permute-start.8 = (f32[512,512]{1,0:T(8,128)S(1)}, f32[512,512]{1,0:T(8,128)S(1)}, u32[]{:S(2)}, u32[]{:S(2)}) collective-permute-start(f32[512,512]{1,0:T(8,128)S(1)} %get-tuple-element.18), channel_id=1, source_target_pairs={{0,8},{8,16},{16,24},{24,32},{32,40},{40,48},{48,56},{56,64},{64,7... | collective-permute-start | bytes 3145736 | tf_op jit(solution)/shard_map/ppermute | solution.py:279
  76.3 5.0 %store.1.old = f32[2048,512]{1,0:T(8,128)} custom-call(f32[2048,512]{1,0:T(8,128)} %eig.7, bf16[1536,512]{1,0:T(8,128)(2,1)S(1)} %get-tuple-element.19.vh, bf16[1536,512]{1,0:T(8,128)(2,1)S(1)} %get-tuple-element.20.vl, bf16[512,512]{1,0:T(8,128)(2,1)S(1)} %get-tuple-element.21.sh, bf16[512,512]{1,0:T(8,128)(2,1)S(1)} %get-tuple-element.22.sl), custom_call_target="tpu_custom_call" | custom-call | flops 1600000000 | bytes 8388608 | tf_op jit(solution)/shard_map/store/pallas_call | solution.py:208
  81.4 11.3 %collective-permute-done.8.upper = f32[512,512]{1,0:T(8,128)S(1)} collective-permute-done((f32[512,512]{1,0:T(8,128)S(1)}, f32[512,512]{1,0:T(8,128)S(1)}, u32[]{:S(2)}, u32[]{:S(2)}) %collective-permute-start.8) | collective-permute-done | bytes 1048608 | tf_op jit(solution)/shard_map/ppermute | solution.py:279
  92.6 1.5 %finish.1 = f32[2048,512]{1,0:T(8,128)} custom-call(s32[2]{0:T(128)S(1)} %pad_add_fusion.where, f32[2048,512]{1,0:T(8,128)} %eig.7, f32[512,512]{1,0:T(8,128)S(1)} %collective-permute-done.8.upper, f32[2048,512]{1,0:T(8,128)} %store.1.old), custom_call_target="tpu_custom_call", output_to_operand_aliasing={{}: (3, {})} | custom-call | bytes 2097152 | tf_op jit(solution)/shard_map/finish/pallas_call | solution.py:244
  (1 shorter events, 0.0 us)
Async XLA Ops:
  0.0 12.1 %copy-start = (s32[2,32]{1,0:T(2,128)S(1)}, s32[2,32]{1,0:T(2,128)}, u32[]{:S(2)}) copy-start(s32[2,32]{1,0:T(2,128)} %param.9) | copy-start | bytes 772
  3.2 29.7 %all-to-all-start = ((f32[8,152,256]{2,1,0:T(8,128)}), f32[8,152,256]{2,1,0:T(8,128)}, u32[]{:S(2)}, u32[]{:S(2)}) async-start(f32[8,152,256]{2,1,0:T(8,128)} %get-tuple-element.17), calls=%async_computation | async-start | bytes 2490368 | tf_op jit(solution)/shard_map/all_to_all | solution.py:272
  10.1 36.7 %collective-permute-start = (f32[512,512]{1,0:T(8,128)S(1)}, f32[512,512]{1,0:T(8,128)S(1)}, u32[]{:S(2)}, u32[]{:S(2)}) collective-permute-start(f32[512,512]{1,0:T(8,128)S(1)} %get-tuple-element.14), channel_id=1, source_target_pairs={{8,0},{16,8},{24,16},{32,24},{40,32},{48,40},{56,48},{64,56},{72,6... | collective-permute-start | bytes 3145736 | tf_op jit(solution)/shard_map/ppermute | solution.py:271
  34.0 12.3 %collective-permute-start.4 = (f32[304,256]{1,0:T(8,128)S(1)}, f32[304,256]{1,0:T(8,128)S(1)}, u32[]{:S(2)}, u32[]{:S(2)}) collective-permute-start(f32[304,256]{1,0:T(8,128)S(1)} %pad_maximum_fusion.p), channel_id=1, source_target_pairs={{0,4},{1,5},{2,6},{3,7},{4,0},{5,1},{6,2},{7,3},{8,12},{9,13},{10,... | collective-permute-start | bytes 933896 | tf_op jit(solution)/shard_map/ppermute | solution.py:268
  34.7 18.6 %collective-permute-start.3 = (f32[304,256]{1,0:T(8,128)S(1)}, f32[304,256]{1,0:T(8,128)S(1)}, u32[]{:S(2)}, u32[]{:S(2)}) collective-permute-start(f32[304,256]{1,0:T(8,128)S(1)} %pad_maximum_fusion.p), channel_id=1, source_target_pairs={{2,0},{3,1},{0,2},{1,3},{6,4},{7,5},{4,6},{5,7},{10,8},{11,9},{8,1... | collective-permute-start | bytes 933896 | tf_op jit(solution)/shard_map/ppermute | solution.py:265
  43.1 14.4 %collective-permute-start.2 = (f32[304,256]{1,0:T(8,128)S(1)}, f32[304,256]{1,0:T(8,128)S(1)}, u32[]{:S(2)}, u32[]{:S(2)}) collective-permute-start(f32[304,256]{1,0:T(8,128)S(1)} %pad_maximum_fusion.p), channel_id=1, source_target_pairs={{3,0},{0,1},{1,2},{2,3},{7,4},{4,5},{5,6},{6,7},{11,8},{8,9},{9,10... | collective-permute-start | bytes 933896 | tf_op jit(solution)/shard_map/ppermute | solution.py:265
  43.6 15.0 %collective-permute-start.1 = (f32[304,256]{1,0:T(8,128)S(1)}, f32[304,256]{1,0:T(8,128)}, u32[]{:S(2)}, u32[]{:S(2)}) collective-permute-start(f32[304,256]{1,0:T(8,128)S(1)} %pad_maximum_fusion.p), channel_id=1, source_target_pairs={{1,0},{2,1},{3,2},{0,3},{5,4},{6,5},{7,6},{4,7},{9,8},{10,9},{11,1... | collective-permute-start | bytes 933896 | tf_op jit(solution)/shard_map/ppermute | solution.py:265
  46.3 17.6 %collective-permute-start.6 = (f32[304,256]{1,0:T(8,128)S(1)}, f32[304,256]{1,0:T(8,128)}, u32[]{:S(2)}, u32[]{:S(2)}) collective-permute-start(f32[304,256]{1,0:T(8,128)S(1)} %collective-permute-done.4.q), channel_id=1, source_target_pairs={{3,0},{0,1},{1,2},{2,3},{7,4},{4,5},{5,6},{6,7},{11,8},{8,9},{9,10... | collective-permute-start | bytes 933896 | tf_op jit(solution)/shard_map/ppermute | solution.py:265
  46.8 17.2 %collective-permute-start.5 = (f32[304,256]{1,0:T(8,128)S(1)}, f32[304,256]{1,0:T(8,128)S(1)}, u32[]{:S(2)}, u32[]{:S(2)}) collective-permute-start(f32[304,256]{1,0:T(8,128)S(1)} %collective-permute-done.4.q), channel_id=1, source_target_pairs={{1,0},{2,1},{3,2},{0,3},{5,4},{6,5},{7,6},{4,7},{9,8},{10,9},{11,1... | collective-permute-start | bytes 933896 | tf_op jit(solution)/shard_map/ppermute | solution.py:265
  53.3 10.8 %collective-permute-start.7 = (f32[304,256]{1,0:T(8,128)S(1)}, f32[304,256]{1,0:T(8,128)S(1)}, u32[]{:S(2)}, u32[]{:S(2)}) collective-permute-start(f32[304,256]{1,0:T(8,128)S(1)} %collective-permute-done.3.s), channel_id=1, source_target_pairs={{0,4},{1,5},{2,6},{3,7},{4,0},{5,1},{6,2},{7,3},{8,12},{9,13},{10,... | collective-permute-start | bytes 933896 | tf_op jit(solution)/shard_map/ppermute | solution.py:268
  54.6 9.5 %copy-start.1 = (s32[2,32]{1,0:T(2,128)S(1)}, s32[2,32]{1,0:T(2,128)}, u32[]{:S(2)}) copy-start(s32[2,32]{1,0:T(2,128)} %offsets.1) | copy-start | bytes 772
  74.4 18.2 %collective-permute-start.8 = (f32[512,512]{1,0:T(8,128)S(1)}, f32[512,512]{1,0:T(8,128)S(1)}, u32[]{:S(2)}, u32[]{:S(2)}) collective-permute-start(f32[512,512]{1,0:T(8,128)S(1)} %get-tuple-element.18), channel_id=1, source_target_pairs={{0,8},{8,16},{16,24},{24,32},{32,40},{40,48},{48,56},{56,64},{64,7... | collective-permute-start | bytes 3145736 | tf_op jit(solution)/shard_map/ppermute | solution.py:279

commit v4 on v3

v4 whole, which is shorter than its diff:
```python
import jax
import jax.numpy as jnp
from jax import lax
from jax.experimental import pallas as pl
from jax.experimental.pallas import tpu as pltpu
from jax.sharding import PartitionSpec as P

WIN = 1024
HALF = 512
BLOCK = 256
TICKS = 2
PIECES = 8
VROWS = WIN // PIECES
TROWS = 24
PROWS = VROWS + TROWS
SPAN = WIN + 16
REACH = WIN + HALF
MIB = 1024 * 1024
F32 = jnp.float32
BF16 = jnp.bfloat16
NN = ((1,), (0,))
TN = ((0,), (0,))

SMEM = pl.BlockSpec(memory_space=pltpu.SMEM)
VMEM = pl.BlockSpec(memory_space=pltpu.VMEM)
ANY = pl.BlockSpec(memory_space=pl.ANY)
HBM = pl.BlockSpec(memory_space=pltpu.HBM)


def split(x):
    hi = x.astype(BF16)
    return hi, (x - hi.astype(F32)).astype(BF16)


def mm(a, b, dims):
    return lax.dot_general(a, b, (dims, ((), ())), preferred_element_type=F32)


def mm3(ah, al, bh, bl, dims):
    return mm(ah, bh, dims) + mm(ah, bl, dims) + mm(al, bh, dims)


def hbm(*arrays):
    return [pltpu.with_memory_space_constraint(a, pltpu.HBM) for a in arrays]


def vmem(*arrays):
    return [pltpu.with_memory_space_constraint(a, pltpu.VMEM) for a in arrays]


def cost(flops, moved):
    return pl.CostEstimate(flops=flops, bytes_accessed=moved, transcendentals=0)


def pack_kernel(vectors, factor, eig, stay, right, across, left, top, sems, first):
    col = lax.axis_index("col")
    x, side = col & 3, col >> 2
    copies = []
    for n, out in enumerate((stay, right, across, left)):
        for half in range(2):
            k = 2 * ((x + n) & 3) + (side if half == 0 else 1 - side)
            at = half * PROWS
            pairs = (
                (vectors.at[0, 0, pl.ds(pl.multiple_of(k * VROWS, 8), VROWS)], out.at[pl.ds(at, VROWS)]),
                (factor.at[0, 0, pl.ds(pl.multiple_of(k * 16, 8), 16)], out.at[pl.ds(at + VROWS, 16)]),
                (
                    factor.at[0, 0, pl.ds(pl.multiple_of(128 + k * 8, 8), 8), pl.ds(128, 128)],
                    out.at[pl.ds(at + VROWS + 16, 8), pl.ds(0, 128)],
                ),
                (
                    factor.at[0, 0, pl.ds(pl.multiple_of(192 + k * 8, 8), 8), pl.ds(128, 128)],
                    out.at[pl.ds(at + VROWS + 16, 8), pl.ds(128, 128)],
                ),
            )
            for i, (src, dst) in enumerate(pairs):
                copies.append(pltpu.make_async_copy(src, dst, sems.at[n, half, i]))
    for copy in copies:
        copy.start()
    lead = pltpu.make_async_copy(eig.at[pl.ds(0, HALF)], top, first)
    lead.start()
    for copy in copies:
        copy.wait()
    lead.wait()


def pack(reflectors, tfactors, eig):
    quarter = jax.ShapeDtypeStruct((2 * PROWS, BLOCK), F32)
    return pl.pallas_call(
        pack_kernel,
        out_shape=(quarter,) * 4 + (jax.ShapeDtypeStruct((HALF, eig.shape[1]), F32),),
        in_specs=[HBM, HBM, HBM],
        out_specs=(VMEM,) * 5,
        scratch_shapes=[pltpu.SemaphoreType.DMA((4, 2, 4)), pltpu.SemaphoreType.DMA],
        compiler_params=pltpu.CompilerParams(vmem_limit_bytes=6 * MIB),
        cost_estimate=cost(0, 5 * MIB),
        name="pack",
    )(*hbm(reflectors, tfactors, eig))


def stage_kernel(eig, halo, wh, wl, rows, sems):
    upper = pltpu.make_async_copy(eig.at[pl.ds(eig.shape[0] - WIN, WIN)], rows.at[pl.ds(0, WIN)], sems.at[0])
    lower = pltpu.make_async_copy(halo, rows.at[pl.ds(WIN, HALF)], sems.at[1])
    upper.start()
    lower.start()
    upper.wait()
    lower.wait()
    wh[...], wl[...] = split(rows[...])


def stage(eig, halo):
    columns = eig.shape[1]
    return pl.pallas_call(
        stage_kernel,
        out_shape=(jax.ShapeDtypeStruct((REACH, columns), BF16), jax.ShapeDtypeStruct((REACH, columns), BF16)),
        in_specs=[HBM, ANY],
        out_specs=(VMEM, VMEM),
        scratch_shapes=[pltpu.VMEM((REACH, columns), F32), pltpu.SemaphoreType.DMA((2,))],
        compiler_params=pltpu.CompilerParams(vmem_limit_bytes=10 * MIB),
        cost_estimate=cost(0, 9 * MIB),
        name="stage",
    )(*hbm(eig), halo)


def choose_kernel(owners, stay, near, far, back, own, send):
    row, col = lax.axis_index("row"), lax.axis_index("col")
    for tick in range(TICKS):
        step = (owners[tick, row] - col) & 3
        part = slice(tick * PROWS, (tick + 1) * PROWS)
        for n, ref in enumerate((stay, near, far, back)):

            @pl.when(step == n)
            def _():
                own[part, :] = ref[:PROWS, :]
                send[part, :] = ref[PROWS:, :]


def choose(owners, arrived):
    half = jax.ShapeDtypeStruct((TICKS * PROWS, BLOCK), F32)
    return pl.pallas_call(
        choose_kernel,
        out_shape=(half, half),
        in_specs=[SMEM] + [VMEM] * 4,
        out_specs=(VMEM, VMEM),
        compiler_params=pltpu.CompilerParams(vmem_limit_bytes=4 * MIB),
        cost_estimate=cost(0, 2 * MIB),
        name="choose",
    )(owners, *arrived)


def merge_kernel(owners, own, got, after, out):
    row, side = lax.axis_index("row"), lax.axis_index("col") >> 2
    for tick in range(TICKS):
        part = slice(tick * PROWS, (tick + 1) * PROWS)

        @pl.when(owners[tick, row] >> 2 != side)
        def _():
            out[part, :] = got[part, :]

        @pl.when(owners[tick, row] >> 2 == side)
        def _():
            out[part, :] = own[part, :]


def merge(owners, own, got, after):
    return pl.pallas_call(
        merge_kernel,
        out_shape=jax.ShapeDtypeStruct(own.shape, F32),
        in_specs=[SMEM, VMEM, VMEM, ANY],
        out_specs=VMEM,
        compiler_params=pltpu.CompilerParams(vmem_limit_bytes=4 * MIB),
        cost_estimate=cost(0, MIB),
        name="merge",
    )(owners, own, got, after)


def place(ref, tick, va, tp, base, shift, k):
    at = tick * PROWS
    tiles = pltpu.roll(ref[at : at + VROWS, :].reshape(VROWS // 8, 8, BLOCK), shift, 1)
    same = lax.broadcasted_iota(jnp.int32, (VROWS // 8 - 1, 8, BLOCK), 1) >= shift
    spot = base + k * VROWS
    inner = jnp.where(same, tiles[1:], tiles[:-1]).reshape(VROWS - 8, BLOCK)
    va[tick, pl.ds(pl.multiple_of(spot + 8, 8), VROWS - 8), :] = inner
    zero = jnp.zeros((8, BLOCK), F32)
    first = pl.ds(pl.multiple_of(spot, 8), 8)
    va[tick, first, :] = va[tick, first, :] + jnp.where(same[0], tiles[0], zero)
    last = pl.ds(pl.multiple_of(spot + VROWS, 8), 8)
    va[tick, last, :] = va[tick, last, :] + jnp.where(same[0], zero, tiles[-1])
    tp[tick, pl.ds(pl.multiple_of(k * TROWS, 8), TROWS), :] = ref[at + VROWS : at + PROWS, :]


def spots(col):
    x, here = col & 3, col >> 2
    columns = [2 * ((x + d) & 3) for d in (0, 1, 3, 2)]
    return [c + here for c in columns] + [c + 1 - here for c in columns]


def starts(offsets, row, tick):
    begin = offsets[tick, row] - WIN
    return begin >> 3 << 3, begin & 7


def prepare_kernel(offsets, p, r, l, s, q, va, tp):
    row, col = lax.axis_index("row"), lax.axis_index("col")
    va[...] = jnp.zeros(va.shape, F32)
    for tick in range(TICKS):
        base, shift = starts(offsets, row, tick)
        for ref, k in zip((p, r, l, s, q), spots(col)):
            place(ref, tick, va, tp, base, shift, k)


def prepare(offsets, pieces):
    return pl.pallas_call(
        prepare_kernel,
        out_shape=(
            jax.ShapeDtypeStruct((TICKS, REACH + 16, BLOCK), F32),
            jax.ShapeDtypeStruct((TICKS, PIECES * TROWS, BLOCK), F32),
        ),
        in_specs=[SMEM] + [VMEM] * 5,
        out_specs=(VMEM, VMEM),
        compiler_params=pltpu.CompilerParams(vmem_limit_bytes=8 * MIB),
        cost_estimate=cost(0, 6 * MIB),
        name="prepare",
    )(offsets, *pieces)


def mix(th, tl, coef):
    return mm3(th, tl, *split(coef), NN)


def update_kernel(offsets, wh, wl, low, u, v, z, old, part, bottom, vh, vl, sh, sl, va, tp):
    row, col = lax.axis_index("row"), lax.axis_index("col")
    factors = []
    for tick in range(TICKS):
        base, shift = starts(offsets, row, tick)
        for ref, k in zip((u, v, z), spots(col)[5:]):
            place(ref, tick, va, tp, base, shift, k)
        lanes = slice(tick * BLOCK, (tick + 1) * BLOCK)
        vh[:, lanes], vl[:, lanes] = split(va[tick, :REACH, :])
        packed = tp[tick].reshape(PIECES, TROWS, BLOCK)
        corner = jnp.concatenate([packed[:, 16:, :128].reshape(64, 128), packed[:, 16:, 128:].reshape(64, 128)], 0)
        lower = jnp.concatenate([jnp.zeros((128, 128), F32), corner], 1)
        factors.append(split(jnp.concatenate([packed[:, :16, :].reshape(128, BLOCK), lower], 0)))
    (fh, fl), (gh, gl) = factors
    cross = mm3(vh[:, BLOCK:], vl[:, BLOCK:], vh[:, :BLOCK], vl[:, :BLOCK], TN)
    cross = split(mm3(*split(mix(gh, gl, cross)), fh, fl, NN))
    coef = mm3(vh[...], vl[...], wh[...], wl[...], TN)
    ch, cl = split(coef)
    sh[:BLOCK, :], sl[:BLOCK, :] = split(mm3(fh, fl, ch[:BLOCK], cl[:BLOCK], NN))
    second = mm3(gh, gl, ch[BLOCK:], cl[BLOCK:], NN) - mm3(*cross, ch[:BLOCK], cl[:BLOCK], NN)
    sh[BLOCK:, :], sl[BLOCK:, :] = split(second)
    bottom[...] = low[...] - mm3(vh[WIN:, :], vl[WIN:, :], sh[...], sl[...], NN)


def update(offsets, wh, wl, halo, pieces, va, tp):
    columns = halo.shape[1]
    both = TICKS * BLOCK
    return pl.pallas_call(
        update_kernel,
        out_shape=(
            jax.ShapeDtypeStruct((HALF, columns), F32),
            jax.ShapeDtypeStruct((REACH, both), BF16),
            jax.ShapeDtypeStruct((REACH, both), BF16),
            jax.ShapeDtypeStruct((both, columns), BF16),
            jax.ShapeDtypeStruct((both, columns), BF16),
            jax.ShapeDtypeStruct(va.shape, F32),
            jax.ShapeDtypeStruct(tp.shape, F32),
        ),
        in_specs=[SMEM] + [VMEM] * 8,
        out_specs=(VMEM,) * 7,
        input_output_aliases={7: 5, 8: 6},
        compiler_params=pltpu.CompilerParams(vmem_limit_bytes=24 * MIB),
        cost_estimate=cost(5_000_000_000, 8 * MIB),
        name="update",
    )(offsets, wh, wl, halo, *pieces, va, tp)[:5]


def store_kernel(eig, vh, vl, sh, sl, out, rows, middle, sems):
    count = eig.shape[0]
    spot = pl.ds(HALF, count - WIN - HALF)
    load = pltpu.make_async_copy(eig.at[pl.ds(count - WIN, WIN)], rows, sems.at[0])
    fetch = pltpu.make_async_copy(eig.at[spot], middle, sems.at[1])
    load.start()
    fetch.start()
    fetch.wait()
    keep = pltpu.make_async_copy(middle, out.at[spot], sems.at[2])
    keep.start()
    load.wait()
    for k in range(4):
        part = slice(k * 256, (k + 1) * 256)
        rows[part, :] = rows[part, :] - mm3(vh[part, :], vl[part, :], sh[...], sl[...], NN)
    store = pltpu.make_async_copy(rows, out.at[pl.ds(count - WIN, WIN)], sems.at[3])
    store.start()
    keep.wait()
    store.wait()


def store(eig, vh, vl, sh, sl):
    columns = eig.shape[1]
    return pl.pallas_call(
        store_kernel,
        out_shape=jax.ShapeDtypeStruct(eig.shape, F32),
        in_specs=[HBM] + [VMEM] * 4,
        out_specs=HBM,
        scratch_shapes=[
            pltpu.VMEM((WIN, columns), F32),
            pltpu.VMEM((eig.shape[0] - WIN - HALF, columns), F32),
            pltpu.SemaphoreType.DMA((4,)),
        ],
        compiler_params=pltpu.CompilerParams(vmem_limit_bytes=16 * MIB),
        cost_estimate=cost(1_600_000_000, 8 * MIB),
        name="store",
    )(*hbm(eig), vh, vl, sh, sl)


def finish_kernel(eig, upper, old, out, rows, sems):
    head = out.at[pl.ds(0, HALF)]

    @pl.when(lax.axis_index("row") > 0)
    def _():
        copy = pltpu.make_async_copy(upper, head, sems.at[0])
        copy.start()
        copy.wait()

    @pl.when(lax.axis_index("row") == 0)
    def _():
        fetch = pltpu.make_async_copy(eig.at[pl.ds(0, HALF)], rows, sems.at[1])
        fetch.start()
        fetch.wait()
        copy = pltpu.make_async_copy(rows, head, sems.at[2])
        copy.start()
        copy.wait()


def finish(eig, upper, out):
    return pl.pallas_call(
        finish_kernel,
        out_shape=pltpu.HBM(eig.shape, F32),
        in_specs=[HBM, VMEM, HBM],
        out_specs=HBM,
        input_output_aliases={2: 0},
        scratch_shapes=[pltpu.VMEM((HALF, eig.shape[1]), F32), pltpu.SemaphoreType.DMA((3,))],
        compiler_params=pltpu.CompilerParams(vmem_limit_bytes=4 * MIB),
        cost_estimate=cost(0, 2 * MIB),
        name="finish",
    )(*hbm(eig), *vmem(upper), *hbm(out))


def per_device(eigvec, reflectors, tfactors, offsets, owners):
    count = lax.axis_size("row")

    def from_x(value, d):
        return lax.ppermute(value, "col", [((i // 4) * 4 + (i % 4 + d) % 4, i) for i in range(8)])

    def from_y(value):
        return lax.ppermute(value, "col", [(i, i ^ 4) for i in range(8)])

    stay, right, across, left, top = pack(reflectors, tfactors, eigvec)
    halo = lax.ppermute(top, "row", [(i + 1, i) for i in range(count - 1)])
    far, near, back = from_x(across, 2), from_x(left, 1), from_x(right, -1)
    own, send = choose(owners, (stay, near, far, back))
    got = from_y(send)
    wh, wl = stage(eigvec, halo)
    p = merge(owners, own, got, wh)
    q, s, r, l = from_y(p), from_x(p, 2), from_x(p, 1), from_x(p, -1)
    u, v, z = from_x(q, 1), from_x(q, -1), from_y(s)

    bottom, *rest = update(offsets, wh, wl, halo, (u, v, z), *prepare(offsets, (p, r, l, s, q)))
    upper = lax.ppermute(bottom, "row", [(i, i + 1) for i in range(count - 1)])
    return finish(eigvec, upper, store(eigvec, *rest))


def solution(mesh):
    return jax.shard_map(
        per_device,
        mesh=mesh,
        in_specs=(
            P("row", "col"),
            P("row", "col", None, None),
            P("row", "col", None, None),
            P(),
            P(),
        ),
        out_specs=P("row", "col"),
        check_vma=False,
    )
```

time: 94.6 us -> 87.2 us (0.922)
  waiting for transfers between devices: 35.4 us -> 40.8 us
  starting transfers between devices: 31.3 us -> 26 us
  between operations: 3.58 us -> 0.25 us
  Pallas kernels: 22.2 us -> 19.6 us
  local copies, waits for them, and re-layouts: 1.64 us -> 0.01 us
    all_to_all x1 -> x0, waiting for transfers between devices: 16.7 us -> none  [per_device(): mine = lax.all_to_all(block, 'col', 0, 0)]
    ppermute x5 -> x8, waiting for transfers between devices: 7.33 us -> 23.1 us  [from_x(): lax.ppermute(value, 'col', [(i // 4 * 4 + (i % 4 + d) % 4, i) for i in ra...]
    ppermute x2 -> x3, starting transfers between devices: 2.02 us -> 9.68 us  [from_y(): return lax.ppermute(value, 'col', [(i, i ^ 4) for i in range(8)])]
    all_to_all x1 -> x0, starting transfers between devices: 6.94 us -> none  [per_device(): mine = lax.all_to_all(block, 'col', 0, 0)]
    ppermute x5 -> x8, starting transfers between devices: 18.5 us -> 11.9 us  [from_x(): lax.ppermute(value, 'col', [(i // 4 * 4 + (i % 4 + d) % 4, i) for i in ra...]
    ppermute x2 -> x3, waiting for transfers between devices: 0.01 us -> 6.49 us  [from_y(): return lax.ppermute(value, 'col', [(i, i ^ 4) for i in range(8)])]
    pallas_call x1, Pallas kernels: 10.3 us -> 7.16 us  [update(): pl.pallas_call(update_kernel, out_shape=(jax.ShapeDtypeStruct((HALF, colu...]
    pallas_call x1 -> x4, Pallas kernels: 3.18 us -> 4.28 us  [the longest x1 2.11 us: pack(): pl.pallas_call(pack_kernel, out_shape=(quarter,) * 4 + (jax.ShapeDtypeStr...]
  transfers between devices with their start and end apart: 10 -> 13, of which waited for: 6 -> 7; matrix products, arithmetic and copies ran while one was open for 2% -> 0% of each run, Pallas kernels for 8% -> 10%
where the time goes in v4:
time: 87.2 us; the launch traced here: 86.6 us
  waiting for transfers between devices  40.8 us (47%)
  starting transfers between devices  26 us (30%)
  Pallas kernels  19.6 us (22%)
    ppermute x8, waiting for transfers between devices, from_x(): lax.ppermute(value, 'col', [(i // 4 * 4 + (i % 4 + d) % 4, i) for i in ra...  23.1 us
    ppermute x8, starting transfers between devices, from_x(): lax.ppermute(value, 'col', [(i // 4 * 4 + (i % 4 + d) % 4, i) for i in ra...  11.9 us
    ppermute x1, waiting for transfers between devices, per_device(): upper = lax.ppermute(bottom, 'row', [(i, i + 1) for i in range(count - 1)])  11.3 us
    ppermute x3, starting transfers between devices, from_y(): return lax.ppermute(value, 'col', [(i, i ^ 4) for i in range(8)])  9.68 us
    pallas_call x1, Pallas kernels, update(): pl.pallas_call(update_kernel, out_shape=(jax.ShapeDtypeStruct((HALF, colu...  7.16 us
    ppermute x3, waiting for transfers between devices, from_y(): return lax.ppermute(value, 'col', [(i, i ^ 4) for i in range(8)])  6.49 us
    pallas_call x1, Pallas kernels, store(): pl.pallas_call(store_kernel, out_shape=jax.ShapeDtypeStruct(eig.shape, F3...  5.03 us
    ppermute x1, starting transfers between devices, per_device(): halo = lax.ppermute(top, 'row', [(i + 1, i) for i in range(count - 1)])  2.47 us
  transfers between devices with their start and end apart: 13, of which 7 were waited for; matrix products, arithmetic and copies ran while one was open for 0% of the time, Pallas kernels for 10%

profile of v4, /device:TPU:128, one launch (start us, length us, event | category | flops | bytes accessed | tf_op | source)
XLA Modules:
  0.0 86.6 jit_solution(17018342892558115055)
XLA Ops:
  0.0 0.0 copy-start
  0.0 2.1 %pack.1 = (f32[304,256]{1,0:T(8,128)S(1)}, f32[304,256]{1,0:T(8,128)S(1)}, f32[304,256]{1,0:T(8,128)S(1)}, f32[304,256]{1,0:T(8,128)S(1)}, f32[512,512]{1,0:T(8,128)S(1)}) custom-call(f32[1,1,1024,256]{3,2,1,0:T(8,128)} %vectors.1, f32[1,1,256,256]{3,2,1,0:T(8,128)} %factor.1, f32[2048,512]{1,0:T(8,128)} %eig.7), custom_call_target="tpu_custom_call" | custom-call | bytes 5242880 | tf_op jit(solution)/shard_map/pack/pallas_call | solution.py:88
  2.1 2.5 %collective-permute-start = (f32[512,512]{1,0:T(8,128)S(1)}, f32[512,512]{1,0:T(8,128)S(1)}, u32[]{:S(2)}, u32[]{:S(2)}) collective-permute-start(f32[512,512]{1,0:T(8,128)S(1)} %get-tuple-element.21), channel_id=1, source_target_pairs={{8,0},{16,8},{24,16},{32,24},{40,32},{48,40},{56,48},{64,56},{72,6... | collective-permute-start | bytes 3145736 | tf_op jit(solution)/shard_map/ppermute | solution.py:358
  4.6 2.8 %collective-permute-start.1 = (f32[304,256]{1,0:T(8,128)S(1)}, f32[304,256]{1,0:T(8,128)S(1)}, u32[]{:S(2)}, u32[]{:S(2)}) collective-permute-start(f32[304,256]{1,0:T(8,128)S(1)} %get-tuple-element.25), channel_id=1, source_target_pairs={{1,0},{2,1},{3,2},{0,3},{5,4},{6,5},{7,6},{4,7},{9,8},{10,9},{11,1... | collective-permute-start | bytes 933896 | tf_op jit(solution)/shard_map/ppermute | solution.py:352
  7.4 0.8 collective-permute-start.2
  8.2 0.9 %collective-permute-start.3 = (f32[304,256]{1,0:T(8,128)S(1)}, f32[304,256]{1,0:T(8,128)S(1)}, u32[]{:S(2)}, u32[]{:S(2)}) collective-permute-start(f32[304,256]{1,0:T(8,128)S(1)} %get-tuple-element.27), channel_id=1, source_target_pairs={{3,0},{0,1},{1,2},{2,3},{7,4},{4,5},{5,6},{6,7},{11,8},{8,9},{9,10... | collective-permute-start | bytes 933896 | tf_op jit(solution)/shard_map/ppermute | solution.py:352
  9.1 11.7 %collective-permute-done.1.near = f32[304,256]{1,0:T(8,128)S(1)} collective-permute-done((f32[304,256]{1,0:T(8,128)S(1)}, f32[304,256]{1,0:T(8,128)S(1)}, u32[]{:S(2)}, u32[]{:S(2)}) %collective-permute-start.1) | collective-permute-done | bytes 311328 | tf_op jit(solution)/shard_map/ppermute | solution.py:352
  20.9 0.0 collective-permute-done.2.far
  20.9 3.7 %collective-permute-done.3.back = f32[304,256]{1,0:T(8,128)S(1)} collective-permute-done((f32[304,256]{1,0:T(8,128)S(1)}, f32[304,256]{1,0:T(8,128)S(1)}, u32[]{:S(2)}, u32[]{:S(2)}) %collective-permute-start.3) | collective-permute-done | bytes 311328 | tf_op jit(solution)/shard_map/ppermute | solution.py:352
  24.5 0.0 copy-done
  24.5 0.6 choose.1
  25.2 0.0 copy-start.1
  25.2 3.3 %collective-permute-start.4 = (f32[304,256]{1,0:T(8,128)S(1)}, f32[304,256]{1,0:T(8,128)S(1)}, u32[]{:S(2)}, u32[]{:S(2)}) collective-permute-start(f32[304,256]{1,0:T(8,128)S(1)} %get-tuple-element.29), channel_id=1, source_target_pairs={{0,4},{1,5},{2,6},{3,7},{4,0},{5,1},{6,2},{7,3},{8,12},{9,13},{10,... | collective-permute-start | bytes 933896 | tf_op jit(solution)/shard_map/ppermute | solution.py:355
  28.5 0.0 collective-permute-done.halo.low
  28.5 2.1 %stage.1 = (bf16[1536,512]{1,0:T(8,128)(2,1)S(1)}, bf16[1536,512]{1,0:T(8,128)(2,1)S(1)}) custom-call(f32[2048,512]{1,0:T(8,128)} %eig.7, f32[512,512]{1,0:T(8,128)S(1)} %collective-permute-done.halo.low), custom_call_target="tpu_custom_call" | custom-call | bytes 9437184 | tf_op jit(solution)/shard_map/stage/pallas_call | solution.py:112
  30.6 5.5 %collective-permute-done.4.got = f32[304,256]{1,0:T(8,128)S(1)} collective-permute-done((f32[304,256]{1,0:T(8,128)S(1)}, f32[304,256]{1,0:T(8,128)S(1)}, u32[]{:S(2)}, u32[]{:S(2)}) %collective-permute-start.4) | collective-permute-done | bytes 311328 | tf_op jit(solution)/shard_map/ppermute | solution.py:355
  36.1 0.6 merge.1.p
  36.7 0.9 %collective-permute-start.8 = (f32[304,256]{1,0:T(8,128)S(1)}, f32[304,256]{1,0:T(8,128)S(1)}, u32[]{:S(2)}, u32[]{:S(2)}) collective-permute-start(f32[304,256]{1,0:T(8,128)S(1)} %merge.1.p), channel_id=1, source_target_pairs={{2,0},{3,1},{0,2},{1,3},{6,4},{7,5},{4,6},{5,7},{10,8},{11,9},{8,1... | collective-permute-start | bytes 933896 | tf_op jit(solution)/shard_map/ppermute | solution.py:352
  37.6 3.2 %collective-permute-start.5 = (f32[304,256]{1,0:T(8,128)S(1)}, f32[304,256]{1,0:T(8,128)S(1)}, u32[]{:S(2)}, u32[]{:S(2)}) collective-permute-start(f32[304,256]{1,0:T(8,128)S(1)} %merge.1.p), channel_id=1, source_target_pairs={{0,4},{1,5},{2,6},{3,7},{4,0},{5,1},{6,2},{7,3},{8,12},{9,13},{10,... | collective-permute-start | bytes 933896 | tf_op jit(solution)/shard_map/ppermute | solution.py:355
  40.8 0.0 collective-permute-start.11
  40.8 3.2 %collective-permute-start.10 = (f32[304,256]{1,0:T(8,128)S(1)}, f32[304,256]{1,0:T(8,128)S(1)}, u32[]{:S(2)}, u32[]{:S(2)}) collective-permute-start(f32[304,256]{1,0:T(8,128)S(1)} %merge.1.p), channel_id=1, source_target_pairs={{1,0},{2,1},{3,2},{0,3},{5,4},{6,5},{7,6},{4,7},{9,8},{10,9},{11,1... | collective-permute-start | bytes 933896 | tf_op jit(solution)/shard_map/ppermute | solution.py:352
  44.0 4.6 %collective-permute-done.8.s = f32[304,256]{1,0:T(8,128)S(1)} collective-permute-done((f32[304,256]{1,0:T(8,128)S(1)}, f32[304,256]{1,0:T(8,128)S(1)}, u32[]{:S(2)}, u32[]{:S(2)}) %collective-permute-start.8) | collective-permute-done | bytes 311328 | tf_op jit(solution)/shard_map/ppermute | solution.py:352
  48.6 3.2 %collective-permute-start.9 = (f32[304,256]{1,0:T(8,128)S(1)}, f32[304,256]{1,0:T(8,128)S(1)}, u32[]{:S(2)}, u32[]{:S(2)}) collective-permute-start(f32[304,256]{1,0:T(8,128)S(1)} %collective-permute-done.8.s), channel_id=1, source_target_pairs={{0,4},{1,5},{2,6},{3,7},{4,0},{5,1},{6,2},{7,3},{8,12},{9,13},{10,... | collective-permute-start | bytes 933896 | tf_op jit(solution)/shard_map/ppermute | solution.py:355
  51.8 0.0 collective-permute-done.5.q
  51.8 0.0 collective-permute-start.7
  51.8 3.2 %collective-permute-start.6 = (f32[304,256]{1,0:T(8,128)S(1)}, f32[304,256]{1,0:T(8,128)S(1)}, u32[]{:S(2)}, u32[]{:S(2)}) collective-permute-start(f32[304,256]{1,0:T(8,128)S(1)} %collective-permute-done.5.q), channel_id=1, source_target_pairs={{1,0},{2,1},{3,2},{0,3},{5,4},{6,5},{7,6},{4,7},{9,8},{10,9},{11,1... | collective-permute-start | bytes 933896 | tf_op jit(solution)/shard_map/ppermute | solution.py:352
  55.1 0.0 collective-permute-done.11.l
  55.1 0.0 collective-permute-done.10.r
  55.1 0.0 copy-done.1
  55.1 0.9 %prepare.1 = (f32[2,1552,256]{2,1,0:T(8,128)S(1)}, f32[2,192,256]{2,1,0:T(8,128)S(1)}) custom-call(s32[2,32]{1,0:T(2,128)S(1)} %copy-done.1, f32[304,256]{1,0:T(8,128)S(1)} %merge.1.p, f32[304,256]{1,0:T(8,128)S(1)} %collective-permute-done.10.r, f32[304,256]{1,0:T(8,128)S(1)} %collective-permute-done.11.l, f32[304,256]{1,0:T(8,128)S(1)} %collective-permute-done.8.s, ...), custom_call_target="tpu_custom_call" | custom-call | bytes 6291456 | tf_op jit(solution)/shard_map/prepare/pallas_call | solution.py:212
  56.0 1.0 %collective-permute-done.9.z = f32[304,256]{1,0:T(8,128)S(1)} collective-permute-done((f32[304,256]{1,0:T(8,128)S(1)}, f32[304,256]{1,0:T(8,128)S(1)}, u32[]{:S(2)}, u32[]{:S(2)}) %collective-permute-start.9) | collective-permute-done | bytes 311328 | tf_op jit(solution)/shard_map/ppermute | solution.py:355
  57.0 3.1 %collective-permute-done.7.v = f32[304,256]{1,0:T(8,128)S(1)} collective-permute-done((f32[304,256]{1,0:T(8,128)S(1)}, f32[304,256]{1,0:T(8,128)S(1)}, u32[]{:S(2)}, u32[]{:S(2)}) %collective-permute-start.7) | collective-permute-done | bytes 311328 | tf_op jit(solution)/shard_map/ppermute | solution.py:352
  60.1 0.0 collective-permute-done.6.u
  60.1 7.2 %update.1 = (f32[512,512]{1,0:T(8,128)S(1)}, bf16[1536,512]{1,0:T(8,128)(2,1)S(1)}, bf16[1536,512]{1,0:T(8,128)(2,1)S(1)}, bf16[512,512]{1,0:T(8,128)(2,1)S(1)},...) custom-call(s32[2,32]{1,0:T(2,128)S(1)} %copy-done.1, ...), custom_call_target="tpu_custom_call", output_to_operand_aliasing={{5}: (7, {}), {6}: (8, {})} | custom-call | flops 5000000000 | bytes 8388608 | tf_op jit(solution)/shard_map/update/pallas_call | solution.py:257
  67.2 1.9 %collective-permute-start.12 = (f32[512,512]{1,0:T(8,128)S(1)}, f32[512,512]{1,0:T(8,128)S(1)}, u32[]{:S(2)}, u32[]{:S(2)}) collective-permute-start(f32[512,512]{1,0:T(8,128)S(1)} %get-tuple-element.32), channel_id=1, source_target_pairs={{0,8},{8,16},{16,24},{24,32},{32,40},{40,48},{48,56},{56,64},{64,7... | collective-permute-start | bytes 3145736 | tf_op jit(solution)/shard_map/ppermute | solution.py:368
  69.2 5.0 %store.1.old = f32[2048,512]{1,0:T(8,128)} custom-call(f32[2048,512]{1,0:T(8,128)} %eig.7, bf16[1536,512]{1,0:T(8,128)(2,1)S(1)} %get-tuple-element.33.vh, bf16[1536,512]{1,0:T(8,128)(2,1)S(1)} %get-tuple-element.34.vl, bf16[512,512]{1,0:T(8,128)(2,1)S(1)} %get-tuple-element.35.sh, bf16[512,512]{1,0:T(8,128)(2,1)S(1)} %get-tuple-element.36.sl), custom_call_target="tpu_custom_call" | custom-call | flops 1600000000 | bytes 8388608 | tf_op jit(solution)/shard_map/store/pallas_call | solution.py:299
  74.2 11.3 %collective-permute-done.12.upper = f32[512,512]{1,0:T(8,128)S(1)} collective-permute-done((f32[512,512]{1,0:T(8,128)S(1)}, f32[512,512]{1,0:T(8,128)S(1)}, u32[]{:S(2)}, u32[]{:S(2)}) %collective-permute-start.12) | collective-permute-done | bytes 1048608 | tf_op jit(solution)/shard_map/ppermute | solution.py:368
  85.5 1.0 %finish.1 = f32[2048,512]{1,0:T(8,128)} custom-call(f32[2048,512]{1,0:T(8,128)} %eig.7, f32[512,512]{1,0:T(8,128)S(1)} %collective-permute-done.12.upper, f32[2048,512]{1,0:T(8,128)} %store.1.old), custom_call_target="tpu_custom_call", output_to_operand_aliasing={{}: (2, {})} | custom-call | bytes 2097152 | tf_op jit(solution)/shard_map/finish/pallas_call | solution.py:335
Async XLA Ops:
  0.0 24.5 %copy-start = (s32[2,32]{1,0:T(2,128)S(1)}, s32[2,32]{1,0:T(2,128)}, u32[]{:S(2)}) copy-start(s32[2,32]{1,0:T(2,128)} %owners.3) | copy-start | bytes 772
  2.1 26.4 %collective-permute-start = (f32[512,512]{1,0:T(8,128)S(1)}, f32[512,512]{1,0:T(8,128)S(1)}, u32[]{:S(2)}, u32[]{:S(2)}) collective-permute-start(f32[512,512]{1,0:T(8,128)S(1)} %get-tuple-element.21), channel_id=1, source_target_pairs={{8,0},{16,8},{24,16},{32,24},{40,32},{48,40},{56,48},{64,56},{72,6... | collective-permute-start | bytes 3145736 | tf_op jit(solution)/shard_map/ppermute | solution.py:358
  4.6 16.3 %collective-permute-start.1 = (f32[304,256]{1,0:T(8,128)S(1)}, f32[304,256]{1,0:T(8,128)S(1)}, u32[]{:S(2)}, u32[]{:S(2)}) collective-permute-start(f32[304,256]{1,0:T(8,128)S(1)} %get-tuple-element.25), channel_id=1, source_target_pairs={{1,0},{2,1},{3,2},{0,3},{5,4},{6,5},{7,6},{4,7},{9,8},{10,9},{11,1... | collective-permute-start | bytes 933896 | tf_op jit(solution)/shard_map/ppermute | solution.py:352
  7.4 13.4 %collective-permute-start.2 = (f32[304,256]{1,0:T(8,128)S(1)}, f32[304,256]{1,0:T(8,128)S(1)}, u32[]{:S(2)}, u32[]{:S(2)}) collective-permute-start(f32[304,256]{1,0:T(8,128)S(1)} %get-tuple-element.26), channel_id=1, source_target_pairs={{2,0},{3,1},{0,2},{1,3},{6,4},{7,5},{4,6},{5,7},{10,8},{11,9},{8,1... | collective-permute-start | bytes 933896 | tf_op jit(solution)/shard_map/ppermute | solution.py:352
  8.2 16.3 %collective-permute-start.3 = (f32[304,256]{1,0:T(8,128)S(1)}, f32[304,256]{1,0:T(8,128)S(1)}, u32[]{:S(2)}, u32[]{:S(2)}) collective-permute-start(f32[304,256]{1,0:T(8,128)S(1)} %get-tuple-element.27), channel_id=1, source_target_pairs={{3,0},{0,1},{1,2},{2,3},{7,4},{4,5},{5,6},{6,7},{11,8},{8,9},{9,10... | collective-permute-start | bytes 933896 | tf_op jit(solution)/shard_map/ppermute | solution.py:352
  25.2 29.9 %copy-start.1 = (s32[2,32]{1,0:T(2,128)S(1)}, s32[2,32]{1,0:T(2,128)}, u32[]{:S(2)}) copy-start(s32[2,32]{1,0:T(2,128)} %offsets.3) | copy-start | bytes 772
  25.2 10.9 %collective-permute-start.4 = (f32[304,256]{1,0:T(8,128)S(1)}, f32[304,256]{1,0:T(8,128)S(1)}, u32[]{:S(2)}, u32[]{:S(2)}) collective-permute-start(f32[304,256]{1,0:T(8,128)S(1)} %get-tuple-element.29), channel_id=1, source_target_pairs={{0,4},{1,5},{2,6},{3,7},{4,0},{5,1},{6,2},{7,3},{8,12},{9,13},{10,... | collective-permute-start | bytes 933896 | tf_op jit(solution)/shard_map/ppermute | solution.py:355
  36.7 11.9 %collective-permute-start.8 = (f32[304,256]{1,0:T(8,128)S(1)}, f32[304,256]{1,0:T(8,128)S(1)}, u32[]{:S(2)}, u32[]{:S(2)}) collective-permute-start(f32[304,256]{1,0:T(8,128)S(1)} %merge.1.p), channel_id=1, source_target_pairs={{2,0},{3,1},{0,2},{1,3},{6,4},{7,5},{4,6},{5,7},{10,8},{11,9},{8,1... | collective-permute-start | bytes 933896 | tf_op jit(solution)/shard_map/ppermute | solution.py:352
  37.6 14.2 %collective-permute-start.5 = (f32[304,256]{1,0:T(8,128)S(1)}, f32[304,256]{1,0:T(8,128)S(1)}, u32[]{:S(2)}, u32[]{:S(2)}) collective-permute-start(f32[304,256]{1,0:T(8,128)S(1)} %merge.1.p), channel_id=1, source_target_pairs={{0,4},{1,5},{2,6},{3,7},{4,0},{5,1},{6,2},{7,3},{8,12},{9,13},{10,... | collective-permute-start | bytes 933896 | tf_op jit(solution)/shard_map/ppermute | solution.py:355
  40.8 14.3 %collective-permute-start.11 = (f32[304,256]{1,0:T(8,128)S(1)}, f32[304,256]{1,0:T(8,128)S(1)}, u32[]{:S(2)}, u32[]{:S(2)}) collective-permute-start(f32[304,256]{1,0:T(8,128)S(1)} %merge.1.p), channel_id=1, source_target_pairs={{3,0},{0,1},{1,2},{2,3},{7,4},{4,5},{5,6},{6,7},{11,8},{8,9},{9,10... | collective-permute-start | bytes 933896 | tf_op jit(solution)/shard_map/ppermute | solution.py:352
  40.8 14.3 %collective-permute-start.10 = (f32[304,256]{1,0:T(8,128)S(1)}, f32[304,256]{1,0:T(8,128)S(1)}, u32[]{:S(2)}, u32[]{:S(2)}) collective-permute-start(f32[304,256]{1,0:T(8,128)S(1)} %merge.1.p), channel_id=1, source_target_pairs={{1,0},{2,1},{3,2},{0,3},{5,4},{6,5},{7,6},{4,7},{9,8},{10,9},{11,1... | collective-permute-start | bytes 933896 | tf_op jit(solution)/shard_map/ppermute | solution.py:352
  48.6 8.4 %collective-permute-start.9 = (f32[304,256]{1,0:T(8,128)S(1)}, f32[304,256]{1,0:T(8,128)S(1)}, u32[]{:S(2)}, u32[]{:S(2)}) collective-permute-start(f32[304,256]{1,0:T(8,128)S(1)} %collective-permute-done.8.s), channel_id=1, source_target_pairs={{0,4},{1,5},{2,6},{3,7},{4,0},{5,1},{6,2},{7,3},{8,12},{9,13},{10,... | collective-permute-start | bytes 933896 | tf_op jit(solution)/shard_map/ppermute | solution.py:355
  51.8 8.2 %collective-permute-start.7 = (f32[304,256]{1,0:T(8,128)S(1)}, f32[304,256]{1,0:T(8,128)S(1)}, u32[]{:S(2)}, u32[]{:S(2)}) collective-permute-start(f32[304,256]{1,0:T(8,128)S(1)} %collective-permute-done.5.q), channel_id=1, source_target_pairs={{3,0},{0,1},{1,2},{2,3},{7,4},{4,5},{5,6},{6,7},{11,8},{8,9},{9,10... | collective-permute-start | bytes 933896 | tf_op jit(solution)/shard_map/ppermute | solution.py:352
  51.8 8.2 %collective-permute-start.6 = (f32[304,256]{1,0:T(8,128)S(1)}, f32[304,256]{1,0:T(8,128)S(1)}, u32[]{:S(2)}, u32[]{:S(2)}) collective-permute-start(f32[304,256]{1,0:T(8,128)S(1)} %collective-permute-done.5.q), channel_id=1, source_target_pairs={{1,0},{2,1},{3,2},{0,3},{5,4},{6,5},{7,6},{4,7},{9,8},{10,9},{11,1... | collective-permute-start | bytes 933896 | tf_op jit(solution)/shard_map/ppermute | solution.py:352
  67.2 18.2 %collective-permute-start.12 = (f32[512,512]{1,0:T(8,128)S(1)}, f32[512,512]{1,0:T(8,128)S(1)}, u32[]{:S(2)}, u32[]{:S(2)}) collective-permute-start(f32[512,512]{1,0:T(8,128)S(1)} %get-tuple-element.32), channel_id=1, source_target_pairs={{0,8},{8,16},{16,24},{24,32},{32,40},{40,48},{48,56},{56,64},{64,7... | collective-permute-start | bytes 3145736 | tf_op jit(solution)/shard_map/ppermute | solution.py:368

commit v5 on v4

--- a/solution.py
+++ b/solution.py
@@ -52,24 +52,25 @@
     return pl.CostEstimate(flops=flops, bytes_accessed=moved, transcendentals=0)
 
 
-def pack_kernel(vectors, factor, eig, stay, right, across, left, top, sems, first):
+def pack_kernel(vectors, factor, eig, *refs):
+    outs, (top, sems, first) = refs[:8], refs[8:]
     col = lax.axis_index("col")
     x, side = col & 3, col >> 2
     copies = []
-    for n, out in enumerate((stay, right, across, left)):
-        for half in range(2):
-            k = 2 * ((x + n) & 3) + (side if half == 0 else 1 - side)
-            at = half * PROWS
+    for half in range(2):
+        for n in range(4):
+            k = 2 * ((x + n) & 3) + (1 - side if half == 0 else side)
+            out = outs[4 * half + n]
             pairs = (
-                (vectors.at[0, 0, pl.ds(pl.multiple_of(k * VROWS, 8), VROWS)], out.at[pl.ds(at, VROWS)]),
-                (factor.at[0, 0, pl.ds(pl.multiple_of(k * 16, 8), 16)], out.at[pl.ds(at + VROWS, 16)]),
+                (vectors.at[0, 0, pl.ds(pl.multiple_of(k * VROWS, 8), VROWS)], out.at[pl.ds(0, VROWS)]),
+                (factor.at[0, 0, pl.ds(pl.multiple_of(k * 16, 8), 16)], out.at[pl.ds(VROWS, 16)]),
                 (
                     factor.at[0, 0, pl.ds(pl.multiple_of(128 + k * 8, 8), 8), pl.ds(128, 128)],
-                    out.at[pl.ds(at + VROWS + 16, 8), pl.ds(0, 128)],
+                    out.at[pl.ds(VROWS + 16, 8), pl.ds(0, 128)],
                 ),
                 (
                     factor.at[0, 0, pl.ds(pl.multiple_of(192 + k * 8, 8), 8), pl.ds(128, 128)],
-                    out.at[pl.ds(at + VROWS + 16, 8), pl.ds(128, 128)],
+                    out.at[pl.ds(VROWS + 16, 8), pl.ds(128, 128)],
                 ),
             )
             for i, (src, dst) in enumerate(pairs):
@@ -84,12 +85,12 @@
 
 
 def pack(reflectors, tfactors, eig):
-    quarter = jax.ShapeDtypeStruct((2 * PROWS, BLOCK), F32)
+    piece = jax.ShapeDtypeStruct((PROWS, BLOCK), F32)
     return pl.pallas_call(
         pack_kernel,
-        out_shape=(quarter,) * 4 + (jax.ShapeDtypeStruct((HALF, eig.shape[1]), F32),),
+        out_shape=(piece,) * 8 + (jax.ShapeDtypeStruct((HALF, eig.shape[1]), F32),),
         in_specs=[HBM, HBM, HBM],
-        out_specs=(VMEM,) * 5,
+        out_specs=(VMEM,) * 9,
         scratch_shapes=[pltpu.SemaphoreType.DMA((4, 2, 4)), pltpu.SemaphoreType.DMA],
         compiler_params=pltpu.CompilerParams(vmem_limit_bytes=6 * MIB),
         cost_estimate=cost(0, 5 * MIB),
@@ -116,12 +117,12 @@
         out_specs=(VMEM, VMEM),
         scratch_shapes=[pltpu.VMEM((REACH, columns), F32), pltpu.SemaphoreType.DMA((2,))],
         compiler_params=pltpu.CompilerParams(vmem_limit_bytes=10 * MIB),
-        cost_estimate=cost(0, 9 * MIB),
+        cost_estimate=cost(0, MIB // 4),
         name="stage",
     )(*hbm(eig), halo)
 
 
-def choose_kernel(owners, stay, near, far, back, own, send):
+def choose_kernel(owners, stay, near, far, back, send):
     row, col = lax.axis_index("row"), lax.axis_index("col")
     for tick in range(TICKS):
         step = (owners[tick, row] - col) & 3
@@ -130,47 +131,49 @@
 
             @pl.when(step == n)
             def _():
-                own[part, :] = ref[:PROWS, :]
-                send[part, :] = ref[PROWS:, :]
+                send[part, :] = ref[...]
 
 
 def choose(owners, arrived):
-    half = jax.ShapeDtypeStruct((TICKS * PROWS, BLOCK), F32)
     return pl.pallas_call(
         choose_kernel,
-        out_shape=(half, half),
+        out_shape=jax.ShapeDtypeStruct((TICKS * PROWS, BLOCK), F32),
         in_specs=[SMEM] + [VMEM] * 4,
-        out_specs=(VMEM, VMEM),
+        out_specs=VMEM,
         compiler_params=pltpu.CompilerParams(vmem_limit_bytes=4 * MIB),
-        cost_estimate=cost(0, 2 * MIB),
+        cost_estimate=cost(0, MIB),
         name="choose",
     )(owners, *arrived)
 
 
-def merge_kernel(owners, own, got, after, out):
-    row, side = lax.axis_index("row"), lax.axis_index("col") >> 2
+def merge_kernel(owners, stay, near, far, back, got, after, out):
+    row, col = lax.axis_index("row"), lax.axis_index("col")
     for tick in range(TICKS):
+        owner = owners[tick, row]
+        step, same = (owner - col) & 3, owner >> 2 == col >> 2
         part = slice(tick * PROWS, (tick + 1) * PROWS)
 
-        @pl.when(owners[tick, row] >> 2 != side)
+        @pl.when(jnp.logical_not(same))
         def _():
             out[part, :] = got[part, :]
 
-        @pl.when(owners[tick, row] >> 2 == side)
-        def _():
-            out[part, :] = own[part, :]
-
-
-def merge(owners, own, got, after):
+        for n, ref in enumerate((stay, near, far, back)):
+
+            @pl.when(jnp.logical_and(same, step == n))
+            def _():
+                out[part, :] = ref[...]
+
+
+def merge(owners, arrived, got, after):
     return pl.pallas_call(
         merge_kernel,
-        out_shape=jax.ShapeDtypeStruct(own.shape, F32),
-        in_specs=[SMEM, VMEM, VMEM, ANY],
+        out_shape=jax.ShapeDtypeStruct(got.shape, F32),
+        in_specs=[SMEM] + [VMEM] * 5 + [ANY],
         out_specs=VMEM,
         compiler_params=pltpu.CompilerParams(vmem_limit_bytes=4 * MIB),
         cost_estimate=cost(0, MIB),
         name="merge",
-    )(owners, own, got, after)
+    )(owners, *arrived, got, after)
 
 
 def place(ref, tick, va, tp, base, shift, k):
@@ -354,13 +357,15 @@
     def from_y(value):
         return lax.ppermute(value, "col", [(i, i ^ 4) for i in range(8)])
 
-    stay, right, across, left, top = pack(reflectors, tfactors, eigvec)
+    *blocks, top = pack(reflectors, tfactors, eigvec)
+
+    def ring(stay, right, across, left):
+        return stay, from_x(left, 1), from_x(across, 2), from_x(right, -1)
+
+    got = from_y(choose(owners, ring(*blocks[:4])))
     halo = lax.ppermute(top, "row", [(i + 1, i) for i in range(count - 1)])
-    far, near, back = from_x(across, 2), from_x(left, 1), from_x(right, -1)
-    own, send = choose(owners, (stay, near, far, back))
-    got = from_y(send)
     wh, wl = stage(eigvec, halo)
-    p = merge(owners, own, got, wh)
+    p = merge(owners, ring(*blocks[4:]), got, wh)
     q, s, r, l = from_y(p), from_x(p, 2), from_x(p, 1), from_x(p, -1)
     u, v, z = from_x(q, 1), from_x(q, -1), from_y(s)
 

time: 87.2 us -> 83.7 us (0.960)
  starting transfers between devices: 26 us -> 22.7 us
    ppermute x3, starting transfers between devices: 9.68 us -> 4.19 us  [from_y(): return lax.ppermute(value, 'col', [(i, i ^ 4) for i in range(8)])]
    ppermute x8 -> x11, waiting for transfers between devices: 23.1 us -> 27.7 us  [from_x(): lax.ppermute(value, 'col', [(i // 4 * 4 + (i % 4 + d) % 4, i) for i in ra...]
    ppermute x3, waiting for transfers between devices: 6.49 us -> 2.02 us  [from_y(): return lax.ppermute(value, 'col', [(i, i ^ 4) for i in range(8)])]
    ppermute x8 -> x11, starting transfers between devices: 11.9 us -> 14.1 us  [from_x(): lax.ppermute(value, 'col', [(i // 4 * 4 + (i % 4 + d) % 4, i) for i in ra...]
  transfers between devices with their start and end apart: 13 -> 16, of which waited for: 7 -> 11; matrix products, arithmetic and copies ran while one was open for 0% -> 0% of each run, Pallas kernels for 10% -> 10%
where the time goes in v5:
time: 83.7 us; the launch traced here: 83.5 us
  waiting for transfers between devices  41 us (49%)
  starting transfers between devices  22.7 us (27%)
  Pallas kernels  19.6 us (23%)
    ppermute x11, waiting for transfers between devices, from_x(): lax.ppermute(value, 'col', [(i // 4 * 4 + (i % 4 + d) % 4, i) for i in ra...  27.7 us
    ppermute x11, starting transfers between devices, from_x(): lax.ppermute(value, 'col', [(i // 4 * 4 + (i % 4 + d) % 4, i) for i in ra...  14.1 us
    ppermute x1, waiting for transfers between devices, per_device(): upper = lax.ppermute(bottom, 'row', [(i, i + 1) for i in range(count - 1)])  11.3 us
    pallas_call x1, Pallas kernels, update(): pl.pallas_call(update_kernel, out_shape=(jax.ShapeDtypeStruct((HALF, colu...  7.15 us
    pallas_call x1, Pallas kernels, store(): pl.pallas_call(store_kernel, out_shape=jax.ShapeDtypeStruct(eig.shape, F3...  5.03 us
    ppermute x3, starting transfers between devices, from_y(): return lax.ppermute(value, 'col', [(i, i ^ 4) for i in range(8)])  4.19 us
    ppermute x1, starting transfers between devices, per_device(): halo = lax.ppermute(top, 'row', [(i + 1, i) for i in range(count - 1)])  2.47 us
    pallas_call x1, Pallas kernels, pack(): pl.pallas_call(pack_kernel, out_shape=(piece,) * 8 + (jax.ShapeDtypeStruc...  2.11 us
  transfers between devices with their start and end apart: 16, of which 11 were waited for; matrix products, arithmetic and copies ran while one was open for 0% of the time, Pallas kernels for 10%

profile of v5, /device:TPU:128, one launch (start us, length us, event | category | flops | bytes accessed | tf_op | source)
XLA Modules:
  0.0 83.5 jit_solution(6755079459951410243)
XLA Ops:
  0.0 0.0 copy-start
  0.0 2.1 %pack.1 = (f32[152,256]{1,0:T(8,128)S(1)}, f32[152,256]{1,0:T(8,128)S(1)}, f32[152,256]{1,0:T(8,128)S(1)}, f32[152,256]{1,0:T(8,128)S(1)}, f32[152,256]{1,0:T(8,...) custom-call(f32[1,1,1024,256]{3,2,1,0:T(8,128)} %vectors.1, ...), custom_call_target="tpu_custom_call" | custom-call | bytes 5242880 | tf_op jit(solution)/shard_map/pack/pallas_call | solution.py:89
  2.1 2.5 %collective-permute-start = (f32[512,512]{1,0:T(8,128)S(1)}, f32[512,512]{1,0:T(8,128)S(1)}, u32[]{:S(2)}, u32[]{:S(2)}) collective-permute-start(f32[512,512]{1,0:T(8,128)S(1)} %get-tuple-element.23), channel_id=1, source_target_pairs={{8,0},{16,8},{24,16},{32,24},{40,32},{48,40},{56,48},{64,56},{72,6... | collective-permute-start | bytes 3145736 | tf_op jit(solution)/shard_map/ppermute | solution.py:366
  4.6 2.8 %collective-permute-start.4 = (f32[152,256]{1,0:T(8,128)S(1)}, f32[152,256]{1,0:T(8,128)S(1)}, u32[]{:S(2)}, u32[]{:S(2)}) collective-permute-start(f32[152,256]{1,0:T(8,128)S(1)} %get-tuple-element.31), channel_id=1, source_target_pairs={{1,0},{2,1},{3,2},{0,3},{5,4},{6,5},{7,6},{4,7},{9,8},{10,9},{11,1... | collective-permute-start | bytes 466952 | tf_op jit(solution)/shard_map/ppermute | solution.py:355
  7.4 0.8 collective-permute-start.5
  8.2 0.9 %collective-permute-start.6 = (f32[152,256]{1,0:T(8,128)S(1)}, f32[152,256]{1,0:T(8,128)S(1)}, u32[]{:S(2)}, u32[]{:S(2)}) collective-permute-start(f32[152,256]{1,0:T(8,128)S(1)} %get-tuple-element.33), channel_id=1, source_target_pairs={{3,0},{0,1},{1,2},{2,3},{7,4},{4,5},{5,6},{6,7},{11,8},{8,9},{9,10... | collective-permute-start | bytes 466952 | tf_op jit(solution)/shard_map/ppermute | solution.py:355
  9.1 5.1 %collective-permute-done.4.near = f32[152,256]{1,0:T(8,128)S(1)} collective-permute-done((f32[152,256]{1,0:T(8,128)S(1)}, f32[152,256]{1,0:T(8,128)S(1)}, u32[]{:S(2)}, u32[]{:S(2)}) %collective-permute-start.4) | collective-permute-done | bytes 155680 | tf_op jit(solution)/shard_map/ppermute | solution.py:355
  14.2 1.7 %collective-permute-done.5.far = f32[152,256]{1,0:T(8,128)S(1)} collective-permute-done((f32[152,256]{1,0:T(8,128)S(1)}, f32[152,256]{1,0:T(8,128)S(1)}, u32[]{:S(2)}, u32[]{:S(2)}) %collective-permute-start.5) | collective-permute-done | bytes 155680 | tf_op jit(solution)/shard_map/ppermute | solution.py:355
  15.9 2.0 %collective-permute-done.6.back = f32[152,256]{1,0:T(8,128)S(1)} collective-permute-done((f32[152,256]{1,0:T(8,128)S(1)}, f32[152,256]{1,0:T(8,128)S(1)}, u32[]{:S(2)}, u32[]{:S(2)}) %collective-permute-start.6) | collective-permute-done | bytes 155680 | tf_op jit(solution)/shard_map/ppermute | solution.py:355
  17.9 0.0 copy-done
  17.9 0.6 choose.1
  18.5 3.3 %collective-permute-start.7 = (f32[304,256]{1,0:T(8,128)S(1)}, f32[304,256]{1,0:T(8,128)S(1)}, u32[]{:S(2)}, u32[]{:S(2)}) collective-permute-start(f32[304,256]{1,0:T(8,128)S(1)} %choose.1), channel_id=1, source_target_pairs={{0,4},{1,5},{2,6},{3,7},{4,0},{5,1},{6,2},{7,3},{8,12},{9,13},{10,... | collective-permute-start | bytes 933896 | tf_op jit(solution)/shard_map/ppermute | solution.py:358
  21.8 0.6 collective-permute-start.1
  22.4 0.8 collective-permute-start.2
  23.1 0.0 copy-start.1
  23.2 0.9 %collective-permute-start.3 = (f32[152,256]{1,0:T(8,128)S(1)}, f32[152,256]{1,0:T(8,128)S(1)}, u32[]{:S(2)}, u32[]{:S(2)}) collective-permute-start(f32[152,256]{1,0:T(8,128)S(1)} %get-tuple-element.29), channel_id=1, source_target_pairs={{3,0},{0,1},{1,2},{2,3},{7,4},{4,5},{5,6},{6,7},{11,8},{8,9},{9,10... | collective-permute-start | bytes 466952 | tf_op jit(solution)/shard_map/ppermute | solution.py:355
  24.0 0.0 collective-permute-done.halo.low
  24.0 2.1 %stage.1 = (bf16[1536,512]{1,0:T(8,128)(2,1)S(1)}, bf16[1536,512]{1,0:T(8,128)(2,1)S(1)}) custom-call(f32[2048,512]{1,0:T(8,128)} %eig.7, f32[512,512]{1,0:T(8,128)S(1)} %collective-permute-done.halo.low), custom_call_target="tpu_custom_call" | custom-call | bytes 262144 | tf_op jit(solution)/shard_map/stage/pallas_call | solution.py:113
  26.1 2.6 %collective-permute-done.1.near = f32[152,256]{1,0:T(8,128)S(1)} collective-permute-done((f32[152,256]{1,0:T(8,128)S(1)}, f32[152,256]{1,0:T(8,128)S(1)}, u32[]{:S(2)}, u32[]{:S(2)}) %collective-permute-start.1) | collective-permute-done | bytes 155680 | tf_op jit(solution)/shard_map/ppermute | solution.py:355
  28.7 1.8 %collective-permute-done.2.far = f32[152,256]{1,0:T(8,128)S(1)} collective-permute-done((f32[152,256]{1,0:T(8,128)S(1)}, f32[152,256]{1,0:T(8,128)S(1)}, u32[]{:S(2)}, u32[]{:S(2)}) %collective-permute-start.2) | collective-permute-done | bytes 155680 | tf_op jit(solution)/shard_map/ppermute | solution.py:355
  30.6 1.7 %collective-permute-done.3.back = f32[152,256]{1,0:T(8,128)S(1)} collective-permute-done((f32[152,256]{1,0:T(8,128)S(1)}, f32[152,256]{1,0:T(8,128)S(1)}, u32[]{:S(2)}, u32[]{:S(2)}) %collective-permute-start.3) | collective-permute-done | bytes 155680 | tf_op jit(solution)/shard_map/ppermute | solution.py:355
  32.3 0.0 collective-permute-done.7.got
  32.3 0.6 merge.1.p
  32.9 0.9 %collective-permute-start.11 = (f32[304,256]{1,0:T(8,128)S(1)}, f32[304,256]{1,0:T(8,128)S(1)}, u32[]{:S(2)}, u32[]{:S(2)}) collective-permute-start(f32[304,256]{1,0:T(8,128)S(1)} %merge.1.p), channel_id=1, source_target_pairs={{2,0},{3,1},{0,2},{1,3},{6,4},{7,5},{4,6},{5,7},{10,8},{11,9},{8,1... | collective-permute-start | bytes 933896 | tf_op jit(solution)/shard_map/ppermute | solution.py:355
  33.8 0.5 collective-permute-start.8
  34.3 1.1 %collective-permute-start.14 = (f32[304,256]{1,0:T(8,128)S(1)}, f32[304,256]{1,0:T(8,128)S(1)}, u32[]{:S(2)}, u32[]{:S(2)}) collective-permute-start(f32[304,256]{1,0:T(8,128)S(1)} %merge.1.p), channel_id=1, source_target_pairs={{3,0},{0,1},{1,2},{2,3},{7,4},{4,5},{5,6},{6,7},{11,8},{8,9},{9,10... | collective-permute-start | bytes 933896 | tf_op jit(solution)/shard_map/ppermute | solution.py:355
  35.4 2.1 %collective-permute-start.13 = (f32[304,256]{1,0:T(8,128)S(1)}, f32[304,256]{1,0:T(8,128)S(1)}, u32[]{:S(2)}, u32[]{:S(2)}) collective-permute-start(f32[304,256]{1,0:T(8,128)S(1)} %merge.1.p), channel_id=1, source_target_pairs={{1,0},{2,1},{3,2},{0,3},{5,4},{6,5},{7,6},{4,7},{9,8},{10,9},{11,1... | collective-permute-start | bytes 933896 | tf_op jit(solution)/shard_map/ppermute | solution.py:355
  37.5 7.3 %collective-permute-done.11.s = f32[304,256]{1,0:T(8,128)S(1)} collective-permute-done((f32[304,256]{1,0:T(8,128)S(1)}, f32[304,256]{1,0:T(8,128)S(1)}, u32[]{:S(2)}, u32[]{:S(2)}) %collective-permute-start.11) | collective-permute-done | bytes 311328 | tf_op jit(solution)/shard_map/ppermute | solution.py:355
  44.8 0.4 collective-permute-start.12
  45.3 0.0 collective-permute-done.8.q
  45.3 0.5 collective-permute-start.10
  45.8 2.7 %collective-permute-start.9 = (f32[304,256]{1,0:T(8,128)S(1)}, f32[304,256]{1,0:T(8,128)S(1)}, u32[]{:S(2)}, u32[]{:S(2)}) collective-permute-start(f32[304,256]{1,0:T(8,128)S(1)} %collective-permute-done.8.q), channel_id=1, source_target_pairs={{1,0},{2,1},{3,2},{0,3},{5,4},{6,5},{7,6},{4,7},{9,8},{10,9},{11,1... | collective-permute-start | bytes 933896 | tf_op jit(solution)/shard_map/ppermute | solution.py:355
  48.5 1.8 %collective-permute-done.14.l = f32[304,256]{1,0:T(8,128)S(1)} collective-permute-done((f32[304,256]{1,0:T(8,128)S(1)}, f32[304,256]{1,0:T(8,128)S(1)}, u32[]{:S(2)}, u32[]{:S(2)}) %collective-permute-start.14) | collective-permute-done | bytes 311328 | tf_op jit(solution)/shard_map/ppermute | solution.py:355
  50.3 0.0 collective-permute-done.13.r
  50.3 0.0 copy-done.1
  50.3 0.9 %prepare.1 = (f32[2,1552,256]{2,1,0:T(8,128)S(1)}, f32[2,192,256]{2,1,0:T(8,128)S(1)}) custom-call(s32[2,32]{1,0:T(2,128)S(1)} %copy-done.1, f32[304,256]{1,0:T(8,128)S(1)} %merge.1.p, f32[304,256]{1,0:T(8,128)S(1)} %collective-permute-done.13.r, f32[304,256]{1,0:T(8,128)S(1)} %collective-permute-done.14.l, f32[304,256]{1,0:T(8,128)S(1)} %collective-permute-done.11.s, ...), custom_call_target="tpu_custom_call" | custom-call | bytes 6291456 | tf_op jit(solution)/shard_map/prepare/pallas_call | solution.py:215
  51.3 2.0 %collective-permute-done.12.z = f32[304,256]{1,0:T(8,128)S(1)} collective-permute-done((f32[304,256]{1,0:T(8,128)S(1)}, f32[304,256]{1,0:T(8,128)S(1)}, u32[]{:S(2)}, u32[]{:S(2)}) %collective-permute-start.12) | collective-permute-done | bytes 311328 | tf_op jit(solution)/shard_map/ppermute | solution.py:358
  53.3 3.6 %collective-permute-done.10.v = f32[304,256]{1,0:T(8,128)S(1)} collective-permute-done((f32[304,256]{1,0:T(8,128)S(1)}, f32[304,256]{1,0:T(8,128)S(1)}, u32[]{:S(2)}, u32[]{:S(2)}) %collective-permute-start.10) | collective-permute-done | bytes 311328 | tf_op jit(solution)/shard_map/ppermute | solution.py:355
  56.9 0.0 collective-permute-done.9.u
  56.9 7.2 %update.1 = (f32[512,512]{1,0:T(8,128)S(1)}, bf16[1536,512]{1,0:T(8,128)(2,1)S(1)}, bf16[1536,512]{1,0:T(8,128)(2,1)S(1)}, bf16[512,512]{1,0:T(8,128)(2,1)S(1)},...) custom-call(s32[2,32]{1,0:T(2,128)S(1)} %copy-done.1, ...), custom_call_target="tpu_custom_call", output_to_operand_aliasing={{5}: (7, {}), {6}: (8, {})} | custom-call | flops 5000000000 | bytes 8388608 | tf_op jit(solution)/shard_map/update/pallas_call | solution.py:260
  64.1 1.9 %collective-permute-start.15 = (f32[512,512]{1,0:T(8,128)S(1)}, f32[512,512]{1,0:T(8,128)S(1)}, u32[]{:S(2)}, u32[]{:S(2)}) collective-permute-start(f32[512,512]{1,0:T(8,128)S(1)} %get-tuple-element.36), channel_id=1, source_target_pairs={{0,8},{8,16},{16,24},{24,32},{32,40},{40,48},{48,56},{56,64},{64,7... | collective-permute-start | bytes 3145736 | tf_op jit(solution)/shard_map/ppermute | solution.py:373
  66.0 5.0 %store.1.old = f32[2048,512]{1,0:T(8,128)} custom-call(f32[2048,512]{1,0:T(8,128)} %eig.7, bf16[1536,512]{1,0:T(8,128)(2,1)S(1)} %get-tuple-element.37.vh, bf16[1536,512]{1,0:T(8,128)(2,1)S(1)} %get-tuple-element.38.vl, bf16[512,512]{1,0:T(8,128)(2,1)S(1)} %get-tuple-element.39.sh, bf16[512,512]{1,0:T(8,128)(2,1)S(1)} %get-tuple-element.40.sl), custom_call_target="tpu_custom_call" | custom-call | flops 1600000000 | bytes 8388608 | tf_op jit(solution)/shard_map/store/pallas_call | solution.py:302
  71.0 11.3 %collective-permute-done.15.upper = f32[512,512]{1,0:T(8,128)S(1)} collective-permute-done((f32[512,512]{1,0:T(8,128)S(1)}, f32[512,512]{1,0:T(8,128)S(1)}, u32[]{:S(2)}, u32[]{:S(2)}) %collective-permute-start.15) | collective-permute-done | bytes 1048608 | tf_op jit(solution)/shard_map/ppermute | solution.py:373
  82.3 1.0 %finish.1 = f32[2048,512]{1,0:T(8,128)} custom-call(f32[2048,512]{1,0:T(8,128)} %eig.7, f32[512,512]{1,0:T(8,128)S(1)} %collective-permute-done.15.upper, f32[2048,512]{1,0:T(8,128)} %store.1.old), custom_call_target="tpu_custom_call", output_to_operand_aliasing={{}: (2, {})} | custom-call | bytes 2097152 | tf_op jit(solution)/shard_map/finish/pallas_call | solution.py:338
Async XLA Ops:
  0.0 17.9 %copy-start = (s32[2,32]{1,0:T(2,128)S(1)}, s32[2,32]{1,0:T(2,128)}, u32[]{:S(2)}) copy-start(s32[2,32]{1,0:T(2,128)} %owners.3) | copy-start | bytes 772
  2.1 21.9 %collective-permute-start = (f32[512,512]{1,0:T(8,128)S(1)}, f32[512,512]{1,0:T(8,128)S(1)}, u32[]{:S(2)}, u32[]{:S(2)}) collective-permute-start(f32[512,512]{1,0:T(8,128)S(1)} %get-tuple-element.23), channel_id=1, source_target_pairs={{8,0},{16,8},{24,16},{32,24},{40,32},{48,40},{56,48},{64,56},{72,6... | collective-permute-start | bytes 3145736 | tf_op jit(solution)/shard_map/ppermute | solution.py:366
  4.6 9.6 %collective-permute-start.4 = (f32[152,256]{1,0:T(8,128)S(1)}, f32[152,256]{1,0:T(8,128)S(1)}, u32[]{:S(2)}, u32[]{:S(2)}) collective-permute-start(f32[152,256]{1,0:T(8,128)S(1)} %get-tuple-element.31), channel_id=1, source_target_pairs={{1,0},{2,1},{3,2},{0,3},{5,4},{6,5},{7,6},{4,7},{9,8},{10,9},{11,1... | collective-permute-start | bytes 466952 | tf_op jit(solution)/shard_map/ppermute | solution.py:355
  7.4 8.5 %collective-permute-start.5 = (f32[152,256]{1,0:T(8,128)S(1)}, f32[152,256]{1,0:T(8,128)S(1)}, u32[]{:S(2)}, u32[]{:S(2)}) collective-permute-start(f32[152,256]{1,0:T(8,128)S(1)} %get-tuple-element.32), channel_id=1, source_target_pairs={{2,0},{3,1},{0,2},{1,3},{6,4},{7,5},{4,6},{5,7},{10,8},{11,9},{8,1... | collective-permute-start | bytes 466952 | tf_op jit(solution)/shard_map/ppermute | solution.py:355
  8.2 9.6 %collective-permute-start.6 = (f32[152,256]{1,0:T(8,128)S(1)}, f32[152,256]{1,0:T(8,128)S(1)}, u32[]{:S(2)}, u32[]{:S(2)}) collective-permute-start(f32[152,256]{1,0:T(8,128)S(1)} %get-tuple-element.33), channel_id=1, source_target_pairs={{3,0},{0,1},{1,2},{2,3},{7,4},{4,5},{5,6},{6,7},{11,8},{8,9},{9,10... | collective-permute-start | bytes 466952 | tf_op jit(solution)/shard_map/ppermute | solution.py:355
  18.5 13.8 %collective-permute-start.7 = (f32[304,256]{1,0:T(8,128)S(1)}, f32[304,256]{1,0:T(8,128)S(1)}, u32[]{:S(2)}, u32[]{:S(2)}) collective-permute-start(f32[304,256]{1,0:T(8,128)S(1)} %choose.1), channel_id=1, source_target_pairs={{0,4},{1,5},{2,6},{3,7},{4,0},{5,1},{6,2},{7,3},{8,12},{9,13},{10,... | collective-permute-start | bytes 933896 | tf_op jit(solution)/shard_map/ppermute | solution.py:358
  21.8 6.9 %collective-permute-start.1 = (f32[152,256]{1,0:T(8,128)S(1)}, f32[152,256]{1,0:T(8,128)S(1)}, u32[]{:S(2)}, u32[]{:S(2)}) collective-permute-start(f32[152,256]{1,0:T(8,128)S(1)} %get-tuple-element.27), channel_id=1, source_target_pairs={{1,0},{2,1},{3,2},{0,3},{5,4},{6,5},{7,6},{4,7},{9,8},{10,9},{11,1... | collective-permute-start | bytes 466952 | tf_op jit(solution)/shard_map/ppermute | solution.py:355
  22.4 8.2 %collective-permute-start.2 = (f32[152,256]{1,0:T(8,128)S(1)}, f32[152,256]{1,0:T(8,128)S(1)}, u32[]{:S(2)}, u32[]{:S(2)}) collective-permute-start(f32[152,256]{1,0:T(8,128)S(1)} %get-tuple-element.28), channel_id=1, source_target_pairs={{2,0},{3,1},{0,2},{1,3},{6,4},{7,5},{4,6},{5,7},{10,8},{11,9},{8,1... | collective-permute-start | bytes 466952 | tf_op jit(solution)/shard_map/ppermute | solution.py:355
  23.1 27.2 %copy-start.1 = (s32[2,32]{1,0:T(2,128)S(1)}, s32[2,32]{1,0:T(2,128)}, u32[]{:S(2)}) copy-start(s32[2,32]{1,0:T(2,128)} %offsets.3) | copy-start | bytes 772
  23.2 9.1 %collective-permute-start.3 = (f32[152,256]{1,0:T(8,128)S(1)}, f32[152,256]{1,0:T(8,128)S(1)}, u32[]{:S(2)}, u32[]{:S(2)}) collective-permute-start(f32[152,256]{1,0:T(8,128)S(1)} %get-tuple-element.29), channel_id=1, source_target_pairs={{3,0},{0,1},{1,2},{2,3},{7,4},{4,5},{5,6},{6,7},{11,8},{8,9},{9,10... | collective-permute-start | bytes 466952 | tf_op jit(solution)/shard_map/ppermute | solution.py:355
  32.9 11.9 %collective-permute-start.11 = (f32[304,256]{1,0:T(8,128)S(1)}, f32[304,256]{1,0:T(8,128)S(1)}, u32[]{:S(2)}, u32[]{:S(2)}) collective-permute-start(f32[304,256]{1,0:T(8,128)S(1)} %merge.1.p), channel_id=1, source_target_pairs={{2,0},{3,1},{0,2},{1,3},{6,4},{7,5},{4,6},{5,7},{10,8},{11,9},{8,1... | collective-permute-start | bytes 933896 | tf_op jit(solution)/shard_map/ppermute | solution.py:355
  33.8 11.4 %collective-permute-start.8 = (f32[304,256]{1,0:T(8,128)S(1)}, f32[304,256]{1,0:T(8,128)S(1)}, u32[]{:S(2)}, u32[]{:S(2)}) collective-permute-start(f32[304,256]{1,0:T(8,128)S(1)} %merge.1.p), channel_id=1, source_target_pairs={{0,4},{1,5},{2,6},{3,7},{4,0},{5,1},{6,2},{7,3},{8,12},{9,13},{10,... | collective-permute-start | bytes 933896 | tf_op jit(solution)/shard_map/ppermute | solution.py:358
  34.3 16.0 %collective-permute-start.14 = (f32[304,256]{1,0:T(8,128)S(1)}, f32[304,256]{1,0:T(8,128)S(1)}, u32[]{:S(2)}, u32[]{:S(2)}) collective-permute-start(f32[304,256]{1,0:T(8,128)S(1)} %merge.1.p), channel_id=1, source_target_pairs={{3,0},{0,1},{1,2},{2,3},{7,4},{4,5},{5,6},{6,7},{11,8},{8,9},{9,10... | collective-permute-start | bytes 933896 | tf_op jit(solution)/shard_map/ppermute | solution.py:355
  35.4 14.9 %collective-permute-start.13 = (f32[304,256]{1,0:T(8,128)S(1)}, f32[304,256]{1,0:T(8,128)S(1)}, u32[]{:S(2)}, u32[]{:S(2)}) collective-permute-start(f32[304,256]{1,0:T(8,128)S(1)} %merge.1.p), channel_id=1, source_target_pairs={{1,0},{2,1},{3,2},{0,3},{5,4},{6,5},{7,6},{4,7},{9,8},{10,9},{11,1... | collective-permute-start | bytes 933896 | tf_op jit(solution)/shard_map/ppermute | solution.py:355
  44.8 8.4 %collective-permute-start.12 = (f32[304,256]{1,0:T(8,128)S(1)}, f32[304,256]{1,0:T(8,128)S(1)}, u32[]{:S(2)}, u32[]{:S(2)}) collective-permute-start(f32[304,256]{1,0:T(8,128)S(1)} %collective-permute-done.11.s), channel_id=1, source_target_pairs={{0,4},{1,5},{2,6},{3,7},{4,0},{5,1},{6,2},{7,3},{8,12},{9,13},{10,... | collective-permute-start | bytes 933896 | tf_op jit(solution)/shard_map/ppermute | solution.py:358
  45.3 11.6 %collective-permute-start.10 = (f32[304,256]{1,0:T(8,128)S(1)}, f32[304,256]{1,0:T(8,128)S(1)}, u32[]{:S(2)}, u32[]{:S(2)}) collective-permute-start(f32[304,256]{1,0:T(8,128)S(1)} %collective-permute-done.8.q), channel_id=1, source_target_pairs={{3,0},{0,1},{1,2},{2,3},{7,4},{4,5},{5,6},{6,7},{11,8},{8,9},{9,10... | collective-permute-start | bytes 933896 | tf_op jit(solution)/shard_map/ppermute | solution.py:355
  45.8 11.1 %collective-permute-start.9 = (f32[304,256]{1,0:T(8,128)S(1)}, f32[304,256]{1,0:T(8,128)S(1)}, u32[]{:S(2)}, u32[]{:S(2)}) collective-permute-start(f32[304,256]{1,0:T(8,128)S(1)} %collective-permute-done.8.q), channel_id=1, source_target_pairs={{1,0},{2,1},{3,2},{0,3},{5,4},{6,5},{7,6},{4,7},{9,8},{10,9},{11,1... | collective-permute-start | bytes 933896 | tf_op jit(solution)/shard_map/ppermute | solution.py:355
  64.1 18.2 %collective-permute-start.15 = (f32[512,512]{1,0:T(8,128)S(1)}, f32[512,512]{1,0:T(8,128)S(1)}, u32[]{:S(2)}, u32[]{:S(2)}) collective-permute-start(f32[512,512]{1,0:T(8,128)S(1)} %get-tuple-element.36), channel_id=1, source_target_pairs={{0,8},{8,16},{16,24},{24,32},{32,40},{40,48},{48,56},{56,64},{64,7... | collective-permute-start | bytes 3145736 | tf_op jit(solution)/shard_map/ppermute | solution.py:373

commit v6 on v5

--- a/solution.py
+++ b/solution.py
@@ -1,3 +1,5 @@
+import functools
+
 import jax
 import jax.numpy as jnp
 from jax import lax
@@ -15,6 +17,7 @@
 PROWS = VROWS + TROWS
 SPAN = WIN + 16
 REACH = WIN + HALF
+COLS = 256
 MIB = 1024 * 1024
 F32 = jnp.float32
 BF16 = jnp.bfloat16
@@ -98,28 +101,33 @@
     )(*hbm(reflectors, tfactors, eig))
 
 
-def stage_kernel(eig, halo, wh, wl, rows, sems):
+def stage_kernel(eig, halo, wh, wl, rh, rl, low, lower, rows, sems):
     upper = pltpu.make_async_copy(eig.at[pl.ds(eig.shape[0] - WIN, WIN)], rows.at[pl.ds(0, WIN)], sems.at[0])
-    lower = pltpu.make_async_copy(halo, rows.at[pl.ds(WIN, HALF)], sems.at[1])
+    under = pltpu.make_async_copy(halo, rows.at[pl.ds(WIN, HALF)], sems.at[1])
     upper.start()
-    lower.start()
+    under.start()
     upper.wait()
-    lower.wait()
-    wh[...], wl[...] = split(rows[...])
+    under.wait()
+    wh[...], wl[...] = split(rows[:, :COLS])
+    rh[...], rl[...] = split(rows[:, COLS:])
+    low[...] = rows[WIN:, :COLS]
+    lower[...] = rows[WIN:, COLS:]
 
 
 def stage(eig, halo):
-    columns = eig.shape[1]
-    return pl.pallas_call(
+    split_half = jax.ShapeDtypeStruct((REACH, COLS), BF16)
+    low = jax.ShapeDtypeStruct((HALF, COLS), F32)
+    wh, wl, rh, rl, *lows = pl.pallas_call(
         stage_kernel,
-        out_shape=(jax.ShapeDtypeStruct((REACH, columns), BF16), jax.ShapeDtypeStruct((REACH, columns), BF16)),
+        out_shape=(split_half,) * 4 + (low,) * 2,
         in_specs=[HBM, ANY],
-        out_specs=(VMEM, VMEM),
-        scratch_shapes=[pltpu.VMEM((REACH, columns), F32), pltpu.SemaphoreType.DMA((2,))],
-        compiler_params=pltpu.CompilerParams(vmem_limit_bytes=10 * MIB),
+        out_specs=(VMEM,) * 6,
+        scratch_shapes=[pltpu.VMEM((REACH, eig.shape[1]), F32), pltpu.SemaphoreType.DMA((2,))],
+        compiler_params=pltpu.CompilerParams(vmem_limit_bytes=12 * MIB),
         cost_estimate=cost(0, MIB // 4),
         name="stage",
     )(*hbm(eig), halo)
+    return (wh, rh), (wl, rl), lows
 
 
 def choose_kernel(owners, stay, near, far, back, send):
@@ -230,7 +238,23 @@
     return mm3(th, tl, *split(coef), NN)
 
 
-def update_kernel(offsets, wh, wl, low, u, v, z, old, part, bottom, vh, vl, sh, sl, va, tp):
+def window(offsets, row, tick):
+    begin = jnp.minimum((offsets[tick, row] - WIN) >> 4 << 4, REACH - SPAN)
+    return pl.ds(pl.multiple_of(begin, 16), SPAN)
+
+
+def solve(windows, vh, vl, wh, wl, low, factors, bottom, sh, sl):
+    (fh, fl), (gh, gl), cross = factors
+    lanes = (slice(0, BLOCK), slice(BLOCK, 2 * BLOCK))
+    coef = [mm3(vh[w, part], vl[w, part], wh[w, :], wl[w, :], TN) for w, part in zip(windows, lanes)]
+    (ch, cl), (dh, dl) = split(coef[0]), split(coef[1])
+    sh[:BLOCK, :], sl[:BLOCK, :] = split(mm3(fh, fl, ch, cl, NN))
+    second = mm3(gh, gl, dh, dl, NN) - mm3(*cross, ch, cl, NN)
+    sh[BLOCK:, :], sl[BLOCK:, :] = split(second)
+    bottom[...] = low[...] - mm3(vh[WIN:, :], vl[WIN:, :], sh[...], sl[...], NN)
+
+
+def first_kernel(offsets, wh, wl, low, u, v, z, old, part, bottom, vh, vl, sh, sl, mh, ml, va, tp):
     row, col = lax.axis_index("row"), lax.axis_index("col")
     factors = []
     for tick in range(TICKS):
@@ -244,106 +268,130 @@
         lower = jnp.concatenate([jnp.zeros((128, 128), F32), corner], 1)
         factors.append(split(jnp.concatenate([packed[:, :16, :].reshape(128, BLOCK), lower], 0)))
     (fh, fl), (gh, gl) = factors
-    cross = mm3(vh[:, BLOCK:], vl[:, BLOCK:], vh[:, :BLOCK], vl[:, :BLOCK], TN)
-    cross = split(mm3(*split(mix(gh, gl, cross)), fh, fl, NN))
-    coef = mm3(vh[...], vl[...], wh[...], wl[...], TN)
-    ch, cl = split(coef)
-    sh[:BLOCK, :], sl[:BLOCK, :] = split(mm3(fh, fl, ch[:BLOCK], cl[:BLOCK], NN))
-    second = mm3(gh, gl, ch[BLOCK:], cl[BLOCK:], NN) - mm3(*cross, ch[:BLOCK], cl[:BLOCK], NN)
-    sh[BLOCK:, :], sl[BLOCK:, :] = split(second)
-    bottom[...] = low[...] - mm3(vh[WIN:, :], vl[WIN:, :], sh[...], sl[...], NN)
+    windows = [window(offsets, row, tick) for tick in range(TICKS)]
+    w = windows[0]
+    cross = mm3(vh[w, BLOCK:], vl[w, BLOCK:], vh[w, :BLOCK], vl[w, :BLOCK], TN)
+    factors.append(split(mm3(*split(mix(gh, gl, cross)), fh, fl, NN)))
+    for n, (hi, lo) in enumerate(factors):
+        mh[n], ml[n] = hi, lo
+    solve(windows, vh, vl, wh, wl, low, factors, bottom, sh, sl)
+
+
+def second_kernel(offsets, wh, wl, low, vh, vl, mh, ml, bottom, sh, sl):
+    windows = [window(offsets, lax.axis_index("row"), tick) for tick in range(TICKS)]
+    solve(windows, vh, vl, wh, wl, low, [(mh[n], ml[n]) for n in range(3)], bottom, sh, sl)
 
 
 def update(offsets, wh, wl, halo, pieces, va, tp):
-    columns = halo.shape[1]
     both = TICKS * BLOCK
-    return pl.pallas_call(
-        update_kernel,
+    shape = jax.ShapeDtypeStruct
+    solved = (shape((HALF, COLS), F32), shape((both, COLS), BF16), shape((both, COLS), BF16))
+    bottom, vh, vl, sh, sl, mh, ml, *unused = pl.pallas_call(
+        first_kernel,
         out_shape=(
-            jax.ShapeDtypeStruct((HALF, columns), F32),
-            jax.ShapeDtypeStruct((REACH, both), BF16),
-            jax.ShapeDtypeStruct((REACH, both), BF16),
-            jax.ShapeDtypeStruct((both, columns), BF16),
-            jax.ShapeDtypeStruct((both, columns), BF16),
-            jax.ShapeDtypeStruct(va.shape, F32),
-            jax.ShapeDtypeStruct(tp.shape, F32),
+            solved[0],
+            shape((REACH, both), BF16),
+            shape((REACH, both), BF16),
+            *solved[1:],
+            shape((3, BLOCK, BLOCK), BF16),
+            shape((3, BLOCK, BLOCK), BF16),
+            shape(va.shape, F32),
+            shape(tp.shape, F32),
         ),
         in_specs=[SMEM] + [VMEM] * 8,
-        out_specs=(VMEM,) * 7,
-        input_output_aliases={7: 5, 8: 6},
-        compiler_params=pltpu.CompilerParams(vmem_limit_bytes=24 * MIB),
-        cost_estimate=cost(5_000_000_000, 8 * MIB),
-        name="update",
-    )(offsets, wh, wl, halo, *pieces, va, tp)[:5]
-
-
-def store_kernel(eig, vh, vl, sh, sl, out, rows, middle, sems):
+        out_specs=(VMEM,) * 9,
+        input_output_aliases={7: 7, 8: 8},
+        compiler_params=pltpu.CompilerParams(vmem_limit_bytes=20 * MIB),
+        cost_estimate=cost(3_000_000_000, 8 * MIB),
+        name="first",
+    )(offsets, wh[0], wl[0], halo[0], *pieces, va, tp)
+    second = pl.pallas_call(
+        second_kernel,
+        out_shape=solved,
+        in_specs=[SMEM] + [VMEM] * 7,
+        out_specs=(VMEM,) * 3,
+        compiler_params=pltpu.CompilerParams(vmem_limit_bytes=16 * MIB),
+        cost_estimate=cost(3_000_000_000, 8 * MIB),
+        name="second",
+    )(offsets, wh[1], wl[1], halo[1], vh, vl, mh, ml)
+    return (bottom, second[0]), (vh, vl, sh, sl, *second[1:])
+
+
+def store_kernel(eig, vh, vl, sh, sl, rh, rl, out, rows, middle, sems, last):
     count = eig.shape[0]
+    loads, stores = [], []
+    for k in range(4):
+        there, here = pl.ds(count - WIN + k * 256, 256), pl.ds(k * 256, 256)
+        loads.append(pltpu.make_async_copy(eig.at[there], rows.at[here], sems.at[0, k]))
+        stores.append(pltpu.make_async_copy(rows.at[here], out.at[there], sems.at[1, k]))
     spot = pl.ds(HALF, count - WIN - HALF)
-    load = pltpu.make_async_copy(eig.at[pl.ds(count - WIN, WIN)], rows, sems.at[0])
-    fetch = pltpu.make_async_copy(eig.at[spot], middle, sems.at[1])
-    load.start()
+    fetch = pltpu.make_async_copy(eig.at[spot], middle, last.at[0])
+    keep = pltpu.make_async_copy(middle, out.at[spot], last.at[1])
+    for copy in loads:
+        copy.start()
     fetch.start()
-    fetch.wait()
-    keep = pltpu.make_async_copy(middle, out.at[spot], sems.at[2])
-    keep.start()
-    load.wait()
     for k in range(4):
         part = slice(k * 256, (k + 1) * 256)
-        rows[part, :] = rows[part, :] - mm3(vh[part, :], vl[part, :], sh[...], sl[...], NN)
-    store = pltpu.make_async_copy(rows, out.at[pl.ds(count - WIN, WIN)], sems.at[3])
-    store.start()
+        loads[k].wait()
+        rows[part, :COLS] = rows[part, :COLS] - mm3(vh[part, :], vl[part, :], sh[...], sl[...], NN)
+        rows[part, COLS:] = rows[part, COLS:] - mm3(vh[part, :], vl[part, :], rh[...], rl[...], NN)
+        stores[k].start()
+        if k == 1:
+            fetch.wait()
+            keep.start()
     keep.wait()
-    store.wait()
-
-
-def store(eig, vh, vl, sh, sl):
+    for copy in stores:
+        copy.wait()
+
+
+def store(eig, *solved):
     columns = eig.shape[1]
     return pl.pallas_call(
         store_kernel,
         out_shape=jax.ShapeDtypeStruct(eig.shape, F32),
-        in_specs=[HBM] + [VMEM] * 4,
+        in_specs=[HBM] + [VMEM] * 6,
         out_specs=HBM,
         scratch_shapes=[
             pltpu.VMEM((WIN, columns), F32),
             pltpu.VMEM((eig.shape[0] - WIN - HALF, columns), F32),
-            pltpu.SemaphoreType.DMA((4,)),
+            pltpu.SemaphoreType.DMA((2, 4)),
+            pltpu.SemaphoreType.DMA((2,)),
         ],
         compiler_params=pltpu.CompilerParams(vmem_limit_bytes=16 * MIB),
         cost_estimate=cost(1_600_000_000, 8 * MIB),
         name="store",
-    )(*hbm(eig), vh, vl, sh, sl)
-
-
-def finish_kernel(eig, upper, old, out, rows, sems):
-    head = out.at[pl.ds(0, HALF)]
+    )(*hbm(eig), *solved)
+
+
+def finish_kernel(half, eig, upper, old, out, rows, sems):
+    spot = (pl.ds(0, HALF), pl.ds(half * COLS, COLS))
 
     @pl.when(lax.axis_index("row") > 0)
     def _():
-        copy = pltpu.make_async_copy(upper, head, sems.at[0])
+        copy = pltpu.make_async_copy(upper, out.at[spot], sems.at[0])
         copy.start()
         copy.wait()
 
     @pl.when(lax.axis_index("row") == 0)
     def _():
-        fetch = pltpu.make_async_copy(eig.at[pl.ds(0, HALF)], rows, sems.at[1])
+        fetch = pltpu.make_async_copy(eig.at[spot], rows, sems.at[1])
         fetch.start()
         fetch.wait()
-        copy = pltpu.make_async_copy(rows, head, sems.at[2])
+        copy = pltpu.make_async_copy(rows, out.at[spot], sems.at[2])
         copy.start()
         copy.wait()
 
 
-def finish(eig, upper, out):
-    return pl.pallas_call(
-        finish_kernel,
+def finish(half, eig, upper, out):
+    return pl.pallas_call(
+        functools.partial(finish_kernel, half),
         out_shape=pltpu.HBM(eig.shape, F32),
         in_specs=[HBM, VMEM, HBM],
         out_specs=HBM,
         input_output_aliases={2: 0},
-        scratch_shapes=[pltpu.VMEM((HALF, eig.shape[1]), F32), pltpu.SemaphoreType.DMA((3,))],
+        scratch_shapes=[pltpu.VMEM((HALF, COLS), F32), pltpu.SemaphoreType.DMA((3,))],
         compiler_params=pltpu.CompilerParams(vmem_limit_bytes=4 * MIB),
-        cost_estimate=cost(0, 2 * MIB),
+        cost_estimate=cost(0, MIB),
         name="finish",
     )(*hbm(eig), *vmem(upper), *hbm(out))
 
@@ -364,14 +412,17 @@
 
     got = from_y(choose(owners, ring(*blocks[:4])))
     halo = lax.ppermute(top, "row", [(i + 1, i) for i in range(count - 1)])
-    wh, wl = stage(eigvec, halo)
-    p = merge(owners, ring(*blocks[4:]), got, wh)
+    wh, wl, lows = stage(eigvec, halo)
+    p = merge(owners, ring(*blocks[4:]), got, wh[0])
     q, s, r, l = from_y(p), from_x(p, 2), from_x(p, 1), from_x(p, -1)
     u, v, z = from_x(q, 1), from_x(q, -1), from_y(s)
 
-    bottom, *rest = update(offsets, wh, wl, halo, (u, v, z), *prepare(offsets, (p, r, l, s, q)))
-    upper = lax.ppermute(bottom, "row", [(i, i + 1) for i in range(count - 1)])
-    return finish(eigvec, upper, store(eigvec, *rest))
+    bottoms, solved = update(offsets, wh, wl, lows, (u, v, z), *prepare(offsets, (p, r, l, s, q)))
+    result = store(eigvec, *solved)
+    for half, bottom in enumerate(bottoms):
+        upper = lax.ppermute(bottom, "row", [(i, i + 1) for i in range(count - 1)])
+        result = finish(half, eigvec, upper, result)
+    return result
 
 
 def solution(mesh):

time: 83.7 us -> 82 us (0.980)
  waiting for transfers between devices: 41 us -> 35.4 us
  starting transfers between devices: 22.7 us -> 25.4 us
  Pallas kernels: 19.6 us -> 20.7 us
    ppermute x1 -> x2, waiting for transfers between devices: 11.3 us -> 5.69 us  [per_device(): upper = lax.ppermute(bottom, 'row', [(i, i + 1) for i in range(count - 1)])]
    ppermute x1 -> x2, starting transfers between devices: 1.93 us -> 4.6 us  [per_device(): upper = lax.ppermute(bottom, 'row', [(i, i + 1) for i in range(count - 1)])]
    pallas_call x3 -> x5, Pallas kernels: 10.3 us -> 12.2 us  [the longest x1 5.57 us: update(): pl.pallas_call(first_kernel, out_shape=(solved[0], shape((REACH, both), B...]
  transfers between devices with their start and end apart: 16 -> 17, of which waited for: 11 -> 12; matrix products, arithmetic and copies ran while one was open for 0% -> 0% of each run, Pallas kernels for 10% -> 14%
where the time goes in v6:
time: 82 us; the launch traced here: 81.7 us
  waiting for transfers between devices  35.4 us (43%)
  starting transfers between devices  25.4 us (31%)
  Pallas kernels  20.7 us (25%)
    ppermute x11, waiting for transfers between devices, from_x(): lax.ppermute(value, 'col', [(i // 4 * 4 + (i % 4 + d) % 4, i) for i in ra...  27.7 us
    ppermute x11, starting transfers between devices, from_x(): lax.ppermute(value, 'col', [(i // 4 * 4 + (i % 4 + d) % 4, i) for i in ra...  14.1 us
    ppermute x2, waiting for transfers between devices, per_device(): upper = lax.ppermute(bottom, 'row', [(i, i + 1) for i in range(count - 1)])  5.69 us
    pallas_call x1, Pallas kernels, update(): pl.pallas_call(first_kernel, out_shape=(solved[0], shape((REACH, both), B...  5.57 us
    ppermute x2, starting transfers between devices, per_device(): upper = lax.ppermute(bottom, 'row', [(i, i + 1) for i in range(count - 1)])  4.6 us
    pallas_call x1, Pallas kernels, store(): pl.pallas_call(store_kernel, out_shape=jax.ShapeDtypeStruct(eig.shape, F3...  4.23 us
    ppermute x3, starting transfers between devices, from_y(): return lax.ppermute(value, 'col', [(i, i ^ 4) for i in range(8)])  4.2 us
    pallas_call x1, Pallas kernels, update(): pl.pallas_call(second_kernel, out_shape=solved, in_specs=[SMEM] + [VMEM]...  2.85 us
  transfers between devices with their start and end apart: 17, of which 12 were waited for; matrix products, arithmetic and copies ran while one was open for 0% of the time, Pallas kernels for 14%

profile of v6, /device:TPU:128, one launch (start us, length us, event | category | flops | bytes accessed | tf_op | source)
XLA Modules:
  0.0 81.7 jit_solution(15763673432864888471)
XLA Ops:
  0.0 0.0 copy-start
  0.0 2.1 %pack.1 = (f32[152,256]{1,0:T(8,128)S(1)}, f32[152,256]{1,0:T(8,128)S(1)}, f32[152,256]{1,0:T(8,128)S(1)}, f32[152,256]{1,0:T(8,128)S(1)}, f32[152,256]{1,0:T(8,...) custom-call(f32[1,1,1024,256]{3,2,1,0:T(8,128)} %vectors.1, ...), custom_call_target="tpu_custom_call" | custom-call | bytes 5242880 | tf_op jit(solution)/shard_map/pack/pallas_call | solution.py:92
  2.1 0.0 copy-start.1
  2.1 2.5 %collective-permute-start = (f32[512,512]{1,0:T(8,128)S(1)}, f32[512,512]{1,0:T(8,128)S(1)}, u32[]{:S(2)}, u32[]{:S(2)}) collective-permute-start(f32[512,512]{1,0:T(8,128)S(1)} %get-tuple-element.32), channel_id=1, source_target_pairs={{8,0},{16,8},{24,16},{32,24},{40,32},{48,40},{56,48},{64,56},{72,6... | collective-permute-start | bytes 3145736 | tf_op jit(solution)/shard_map/ppermute | solution.py:414
  4.6 2.8 %collective-permute-start.4 = (f32[152,256]{1,0:T(8,128)S(1)}, f32[152,256]{1,0:T(8,128)S(1)}, u32[]{:S(2)}, u32[]{:S(2)}) collective-permute-start(f32[152,256]{1,0:T(8,128)S(1)} %get-tuple-element.44), channel_id=1, source_target_pairs={{1,0},{2,1},{3,2},{0,3},{5,4},{6,5},{7,6},{4,7},{9,8},{10,9},{11,1... | collective-permute-start | bytes 466952 | tf_op jit(solution)/shard_map/ppermute | solution.py:403
  7.4 0.8 collective-permute-start.5
  8.2 0.9 %collective-permute-start.6 = (f32[152,256]{1,0:T(8,128)S(1)}, f32[152,256]{1,0:T(8,128)S(1)}, u32[]{:S(2)}, u32[]{:S(2)}) collective-permute-start(f32[152,256]{1,0:T(8,128)S(1)} %get-tuple-element.46), channel_id=1, source_target_pairs={{3,0},{0,1},{1,2},{2,3},{7,4},{4,5},{5,6},{6,7},{11,8},{8,9},{9,10... | collective-permute-start | bytes 466952 | tf_op jit(solution)/shard_map/ppermute | solution.py:403
  9.1 5.1 %collective-permute-done.4.near = f32[152,256]{1,0:T(8,128)S(1)} collective-permute-done((f32[152,256]{1,0:T(8,128)S(1)}, f32[152,256]{1,0:T(8,128)S(1)}, u32[]{:S(2)}, u32[]{:S(2)}) %collective-permute-start.4) | collective-permute-done | bytes 155680 | tf_op jit(solution)/shard_map/ppermute | solution.py:403
  14.2 1.7 %collective-permute-done.5.far = f32[152,256]{1,0:T(8,128)S(1)} collective-permute-done((f32[152,256]{1,0:T(8,128)S(1)}, f32[152,256]{1,0:T(8,128)S(1)}, u32[]{:S(2)}, u32[]{:S(2)}) %collective-permute-start.5) | collective-permute-done | bytes 155680 | tf_op jit(solution)/shard_map/ppermute | solution.py:403
  15.9 2.0 %collective-permute-done.6.back = f32[152,256]{1,0:T(8,128)S(1)} collective-permute-done((f32[152,256]{1,0:T(8,128)S(1)}, f32[152,256]{1,0:T(8,128)S(1)}, u32[]{:S(2)}, u32[]{:S(2)}) %collective-permute-start.6) | collective-permute-done | bytes 155680 | tf_op jit(solution)/shard_map/ppermute | solution.py:403
  17.9 0.0 copy-done
  17.9 0.6 choose.1
  18.5 3.3 %collective-permute-start.7 = (f32[304,256]{1,0:T(8,128)S(1)}, f32[304,256]{1,0:T(8,128)S(1)}, u32[]{:S(2)}, u32[]{:S(2)}) collective-permute-start(f32[304,256]{1,0:T(8,128)S(1)} %choose.1), channel_id=1, source_target_pairs={{0,4},{1,5},{2,6},{3,7},{4,0},{5,1},{6,2},{7,3},{8,12},{9,13},{10,... | collective-permute-start | bytes 933896 | tf_op jit(solution)/shard_map/ppermute | solution.py:406
  21.8 0.6 collective-permute-start.1
  22.4 0.8 collective-permute-start.2
  23.2 0.9 %collective-permute-start.3 = (f32[152,256]{1,0:T(8,128)S(1)}, f32[152,256]{1,0:T(8,128)S(1)}, u32[]{:S(2)}, u32[]{:S(2)}) collective-permute-start(f32[152,256]{1,0:T(8,128)S(1)} %get-tuple-element.42), channel_id=1, source_target_pairs={{3,0},{0,1},{1,2},{2,3},{7,4},{4,5},{5,6},{6,7},{11,8},{8,9},{9,10... | collective-permute-start | bytes 466952 | tf_op jit(solution)/shard_map/ppermute | solution.py:403
  24.0 0.0 collective-permute-done.halo
  24.0 2.1 %stage.1 = (bf16[1536,256]{1,0:T(8,128)(2,1)S(1)}, bf16[1536,256]{1,0:T(8,128)(2,1)S(1)}, bf16[1536,256]{1,0:T(8,128)(2,1)S(1)}, bf16[1536,256]{1,0:T(8,128)(2,1...) custom-call(f32[2048,512]{1,0:T(8,128)} %eig.9, f32[512,512]{1,0:T(8,128)S(1)} %collective-permute-done.halo), custom_call_target="tpu_custom_call" | custom-call | bytes 262144 | tf_op jit(solution)/shard_map/stage/pallas_call | solution.py:120
  26.2 2.6 %collective-permute-done.1.near = f32[152,256]{1,0:T(8,128)S(1)} collective-permute-done((f32[152,256]{1,0:T(8,128)S(1)}, f32[152,256]{1,0:T(8,128)S(1)}, u32[]{:S(2)}, u32[]{:S(2)}) %collective-permute-start.1) | collective-permute-done | bytes 155680 | tf_op jit(solution)/shard_map/ppermute | solution.py:403
  28.7 1.8 %collective-permute-done.2.far = f32[152,256]{1,0:T(8,128)S(1)} collective-permute-done((f32[152,256]{1,0:T(8,128)S(1)}, f32[152,256]{1,0:T(8,128)S(1)}, u32[]{:S(2)}, u32[]{:S(2)}) %collective-permute-start.2) | collective-permute-done | bytes 155680 | tf_op jit(solution)/shard_map/ppermute | solution.py:403
  30.6 1.7 %collective-permute-done.3.back = f32[152,256]{1,0:T(8,128)S(1)} collective-permute-done((f32[152,256]{1,0:T(8,128)S(1)}, f32[152,256]{1,0:T(8,128)S(1)}, u32[]{:S(2)}, u32[]{:S(2)}) %collective-permute-start.3) | collective-permute-done | bytes 155680 | tf_op jit(solution)/shard_map/ppermute | solution.py:403
  32.3 0.0 collective-permute-done.7.got
  32.3 0.6 merge.1.p
  33.0 0.9 %collective-permute-start.11 = (f32[304,256]{1,0:T(8,128)S(1)}, f32[304,256]{1,0:T(8,128)S(1)}, u32[]{:S(2)}, u32[]{:S(2)}) collective-permute-start(f32[304,256]{1,0:T(8,128)S(1)} %merge.1.p), channel_id=1, source_target_pairs={{2,0},{3,1},{0,2},{1,3},{6,4},{7,5},{4,6},{5,7},{10,8},{11,9},{8,1... | collective-permute-start | bytes 933896 | tf_op jit(solution)/shard_map/ppermute | solution.py:403
  33.8 0.5 collective-permute-start.8
  34.3 1.1 %collective-permute-start.14 = (f32[304,256]{1,0:T(8,128)S(1)}, f32[304,256]{1,0:T(8,128)S(1)}, u32[]{:S(2)}, u32[]{:S(2)}) collective-permute-start(f32[304,256]{1,0:T(8,128)S(1)} %merge.1.p), channel_id=1, source_target_pairs={{3,0},{0,1},{1,2},{2,3},{7,4},{4,5},{5,6},{6,7},{11,8},{8,9},{9,10... | collective-permute-start | bytes 933896 | tf_op jit(solution)/shard_map/ppermute | solution.py:403
  35.4 2.1 %collective-permute-start.13 = (f32[304,256]{1,0:T(8,128)S(1)}, f32[304,256]{1,0:T(8,128)S(1)}, u32[]{:S(2)}, u32[]{:S(2)}) collective-permute-start(f32[304,256]{1,0:T(8,128)S(1)} %merge.1.p), channel_id=1, source_target_pairs={{1,0},{2,1},{3,2},{0,3},{5,4},{6,5},{7,6},{4,7},{9,8},{10,9},{11,1... | collective-permute-start | bytes 933896 | tf_op jit(solution)/shard_map/ppermute | solution.py:403
  37.5 7.3 %collective-permute-done.11.s = f32[304,256]{1,0:T(8,128)S(1)} collective-permute-done((f32[304,256]{1,0:T(8,128)S(1)}, f32[304,256]{1,0:T(8,128)S(1)}, u32[]{:S(2)}, u32[]{:S(2)}) %collective-permute-start.11) | collective-permute-done | bytes 311328 | tf_op jit(solution)/shard_map/ppermute | solution.py:403
  44.8 0.4 collective-permute-start.12
  45.3 0.0 collective-permute-done.8.q
  45.3 0.5 collective-permute-start.10
  45.8 2.7 %collective-permute-start.9 = (f32[304,256]{1,0:T(8,128)S(1)}, f32[304,256]{1,0:T(8,128)S(1)}, u32[]{:S(2)}, u32[]{:S(2)}) collective-permute-start(f32[304,256]{1,0:T(8,128)S(1)} %collective-permute-done.8.q), channel_id=1, source_target_pairs={{1,0},{2,1},{3,2},{0,3},{5,4},{6,5},{7,6},{4,7},{9,8},{10,9},{11,1... | collective-permute-start | bytes 933896 | tf_op jit(solution)/shard_map/ppermute | solution.py:403
  48.5 1.8 %collective-permute-done.14.l = f32[304,256]{1,0:T(8,128)S(1)} collective-permute-done((f32[304,256]{1,0:T(8,128)S(1)}, f32[304,256]{1,0:T(8,128)S(1)}, u32[]{:S(2)}, u32[]{:S(2)}) %collective-permute-start.14) | collective-permute-done | bytes 311328 | tf_op jit(solution)/shard_map/ppermute | solution.py:403
  50.4 0.0 collective-permute-done.13.r
  50.4 0.0 copy-done.1
  50.4 0.9 %prepare.1 = (f32[2,1552,256]{2,1,0:T(8,128)S(1)}, f32[2,192,256]{2,1,0:T(8,128)S(1)}) custom-call(s32[2,32]{1,0:T(2,128)S(1)} %copy-done.1, f32[304,256]{1,0:T(8,128)S(1)} %merge.1.p, f32[304,256]{1,0:T(8,128)S(1)} %collective-permute-done.13.r, f32[304,256]{1,0:T(8,128)S(1)} %collective-permute-done.14.l, f32[304,256]{1,0:T(8,128)S(1)} %collective-permute-done.11.s, ...), custom_call_target="tpu_custom_call" | custom-call | bytes 6291456 | tf_op jit(solution)/shard_map/prepare/pallas_call | solution.py:223
  51.3 2.0 %collective-permute-done.12.z = f32[304,256]{1,0:T(8,128)S(1)} collective-permute-done((f32[304,256]{1,0:T(8,128)S(1)}, f32[304,256]{1,0:T(8,128)S(1)}, u32[]{:S(2)}, u32[]{:S(2)}) %collective-permute-start.12) | collective-permute-done | bytes 311328 | tf_op jit(solution)/shard_map/ppermute | solution.py:406
  53.3 3.6 %collective-permute-done.10.v = f32[304,256]{1,0:T(8,128)S(1)} collective-permute-done((f32[304,256]{1,0:T(8,128)S(1)}, f32[304,256]{1,0:T(8,128)S(1)}, u32[]{:S(2)}, u32[]{:S(2)}) %collective-permute-start.10) | collective-permute-done | bytes 311328 | tf_op jit(solution)/shard_map/ppermute | solution.py:403
  56.9 0.0 collective-permute-done.9.u
  56.9 5.6 %first.1 = (f32[512,256]{1,0:T(8,128)S(1)}, bf16[1536,512]{1,0:T(8,128)(2,1)S(1)}, bf16[1536,512]{1,0:T(8,128)(2,1)S(1)}, bf16[512,256]{1,0:T(8,128)(2,1)S(1)}, ...) custom-call(s32[2,32]{1,0:T(2,128)S(1)} %copy-done.1, ...), custom_call_target="tpu_custom_call", output_to_operand_aliasing={{7}: (7, {}), {8}: (8, {})} | custom-call | flops 3000000000 | bytes 8388608 | tf_op jit(solution)/shard_map/first/pallas_call | solution.py:289
  62.5 1.9 %collective-permute-start.16 = (f32[512,256]{1,0:T(8,128)S(1)}, f32[512,256]{1,0:T(8,128)S(1)}, u32[]{:S(2)}, u32[]{:S(2)}) collective-permute-start(f32[512,256]{1,0:T(8,128)S(1)} %get-tuple-element.54), channel_id=1, source_target_pairs={{0,8},{8,16},{16,24},{24,32},{32,40},{40,48},{48,56},{56,64},{64,7... | collective-permute-start | bytes 1572872 | tf_op jit(solution)/shard_map/ppermute | solution.py:423
  64.4 2.9 %second.1 = (f32[512,256]{1,0:T(8,128)S(1)}, bf16[512,256]{1,0:T(8,128)(2,1)S(1)}, bf16[512,256]{1,0:T(8,128)(2,1)S(1)}) custom-call(s32[2,32]{1,0:T(2,128)S(1)} %copy-done.1, bf16[1536,256]{1,0:T(8,128)(2,1)S(1)} %get-tuple-element.33.wh, bf16[1536,256]{1,0:T(8,128)(2,1)S(1)} %get-tuple-element.34.wl, f32[512,256]{1,0:T(8,128)S(1)} %get-tuple-element.35.low, ...), custom_call_target="tpu_custom_call" | custom-call | flops 3000000000 | bytes 8388608 | tf_op jit(solution)/shard_map/second/pallas_call | solution.py:308
  67.3 2.7 %collective-permute-start.15 = (f32[512,256]{1,0:T(8,128)S(1)}, f32[512,256]{1,0:T(8,128)S(1)}, u32[]{:S(2)}, u32[]{:S(2)}) collective-permute-start(f32[512,256]{1,0:T(8,128)S(1)} %get-tuple-element.53), channel_id=1, source_target_pairs={{0,8},{8,16},{16,24},{24,32},{32,40},{40,48},{48,56},{56,64},{64,7... | collective-permute-start | bytes 1572872 | tf_op jit(solution)/shard_map/ppermute | solution.py:423
  70.0 4.2 %store.1.old = f32[2048,512]{1,0:T(8,128)} custom-call(f32[2048,512]{1,0:T(8,128)} %eig.9, bf16[1536,512]{1,0:T(8,128)(2,1)S(1)} %get-tuple-element.49.vh, bf16[1536,512]{1,0:T(8,128)(2,1)S(1)} %get-tuple-element.50.vl, bf16[512,256]{1,0:T(8,128)(2,1)S(1)} %get-tuple-element.55.sh, bf16[512,256]{1,0:T(8,128)(2,1)S(1)} %get-tuple-element.56.sl, ...), custom_call_target="tpu_custom_call" | custom-call | flops 1600000000 | bytes 8388608 | tf_op jit(solution)/shard_map/store/pallas_call | solution.py:349
  74.2 0.9 %collective-permute-done.16.upper = f32[512,256]{1,0:T(8,128)S(1)} collective-permute-done((f32[512,256]{1,0:T(8,128)S(1)}, f32[512,256]{1,0:T(8,128)S(1)}, u32[]{:S(2)}, u32[]{:S(2)}) %collective-permute-start.16) | collective-permute-done | bytes 524320 | tf_op jit(solution)/shard_map/ppermute | solution.py:423
  75.1 0.8 %finish.2.old = f32[2048,512]{1,0:T(8,128)} custom-call(f32[2048,512]{1,0:T(8,128)} %eig.9, f32[512,256]{1,0:T(8,128)S(1)} %collective-permute-done.16.upper, f32[2048,512]{1,0:T(8,128)} %store.1.old), custom_call_target="tpu_custom_call", output_to_operand_aliasing={{}: (2, {})} | custom-call | bytes 1048576 | tf_op jit(solution)/shard_map/finish/pallas_call | solution.py:386
  75.9 4.8 %collective-permute-done.15.upper = f32[512,256]{1,0:T(8,128)S(1)} collective-permute-done((f32[512,256]{1,0:T(8,128)S(1)}, f32[512,256]{1,0:T(8,128)S(1)}, u32[]{:S(2)}, u32[]{:S(2)}) %collective-permute-start.15) | collective-permute-done | bytes 524320 | tf_op jit(solution)/shard_map/ppermute | solution.py:423
  80.7 0.8 %finish.3 = f32[2048,512]{1,0:T(8,128)} custom-call(f32[2048,512]{1,0:T(8,128)} %eig.9, f32[512,256]{1,0:T(8,128)S(1)} %collective-permute-done.15.upper, f32[2048,512]{1,0:T(8,128)} %finish.2.old), custom_call_target="tpu_custom_call", output_to_operand_aliasing={{}: (2, {})} | custom-call | bytes 1048576 | tf_op jit(solution)/shard_map/finish/pallas_call | solution.py:386
Async XLA Ops:
  0.0 17.9 %copy-start = (s32[2,32]{1,0:T(2,128)S(1)}, s32[2,32]{1,0:T(2,128)}, u32[]{:S(2)}) copy-start(s32[2,32]{1,0:T(2,128)} %owners.3) | copy-start | bytes 772
  2.1 48.2 %copy-start.1 = (s32[2,32]{1,0:T(2,128)S(1)}, s32[2,32]{1,0:T(2,128)}, u32[]{:S(2)}) copy-start(s32[2,32]{1,0:T(2,128)} %offsets.5) | copy-start | bytes 772
  2.1 21.9 %collective-permute-start = (f32[512,512]{1,0:T(8,128)S(1)}, f32[512,512]{1,0:T(8,128)S(1)}, u32[]{:S(2)}, u32[]{:S(2)}) collective-permute-start(f32[512,512]{1,0:T(8,128)S(1)} %get-tuple-element.32), channel_id=1, source_target_pairs={{8,0},{16,8},{24,16},{32,24},{40,32},{48,40},{56,48},{64,56},{72,6... | collective-permute-start | bytes 3145736 | tf_op jit(solution)/shard_map/ppermute | solution.py:414
  4.6 9.6 %collective-permute-start.4 = (f32[152,256]{1,0:T(8,128)S(1)}, f32[152,256]{1,0:T(8,128)S(1)}, u32[]{:S(2)}, u32[]{:S(2)}) collective-permute-start(f32[152,256]{1,0:T(8,128)S(1)} %get-tuple-element.44), channel_id=1, source_target_pairs={{1,0},{2,1},{3,2},{0,3},{5,4},{6,5},{7,6},{4,7},{9,8},{10,9},{11,1... | collective-permute-start | bytes 466952 | tf_op jit(solution)/shard_map/ppermute | solution.py:403
  7.4 8.5 %collective-permute-start.5 = (f32[152,256]{1,0:T(8,128)S(1)}, f32[152,256]{1,0:T(8,128)S(1)}, u32[]{:S(2)}, u32[]{:S(2)}) collective-permute-start(f32[152,256]{1,0:T(8,128)S(1)} %get-tuple-element.45), channel_id=1, source_target_pairs={{2,0},{3,1},{0,2},{1,3},{6,4},{7,5},{4,6},{5,7},{10,8},{11,9},{8,1... | collective-permute-start | bytes 466952 | tf_op jit(solution)/shard_map/ppermute | solution.py:403
  8.2 9.6 %collective-permute-start.6 = (f32[152,256]{1,0:T(8,128)S(1)}, f32[152,256]{1,0:T(8,128)S(1)}, u32[]{:S(2)}, u32[]{:S(2)}) collective-permute-start(f32[152,256]{1,0:T(8,128)S(1)} %get-tuple-element.46), channel_id=1, source_target_pairs={{3,0},{0,1},{1,2},{2,3},{7,4},{4,5},{5,6},{6,7},{11,8},{8,9},{9,10... | collective-permute-start | bytes 466952 | tf_op jit(solution)/shard_map/ppermute | solution.py:403
  18.5 13.8 %collective-permute-start.7 = (f32[304,256]{1,0:T(8,128)S(1)}, f32[304,256]{1,0:T(8,128)S(1)}, u32[]{:S(2)}, u32[]{:S(2)}) collective-permute-start(f32[304,256]{1,0:T(8,128)S(1)} %choose.1), channel_id=1, source_target_pairs={{0,4},{1,5},{2,6},{3,7},{4,0},{5,1},{6,2},{7,3},{8,12},{9,13},{10,... | collective-permute-start | bytes 933896 | tf_op jit(solution)/shard_map/ppermute | solution.py:406
  21.8 6.9 %collective-permute-start.1 = (f32[152,256]{1,0:T(8,128)S(1)}, f32[152,256]{1,0:T(8,128)S(1)}, u32[]{:S(2)}, u32[]{:S(2)}) collective-permute-start(f32[152,256]{1,0:T(8,128)S(1)} %get-tuple-element.40), channel_id=1, source_target_pairs={{1,0},{2,1},{3,2},{0,3},{5,4},{6,5},{7,6},{4,7},{9,8},{10,9},{11,1... | collective-permute-start | bytes 466952 | tf_op jit(solution)/shard_map/ppermute | solution.py:403
  22.4 8.2 %collective-permute-start.2 = (f32[152,256]{1,0:T(8,128)S(1)}, f32[152,256]{1,0:T(8,128)S(1)}, u32[]{:S(2)}, u32[]{:S(2)}) collective-permute-start(f32[152,256]{1,0:T(8,128)S(1)} %get-tuple-element.41), channel_id=1, source_target_pairs={{2,0},{3,1},{0,2},{1,3},{6,4},{7,5},{4,6},{5,7},{10,8},{11,9},{8,1... | collective-permute-start | bytes 466952 | tf_op jit(solution)/shard_map/ppermute | solution.py:403
  23.2 9.1 %collective-permute-start.3 = (f32[152,256]{1,0:T(8,128)S(1)}, f32[152,256]{1,0:T(8,128)S(1)}, u32[]{:S(2)}, u32[]{:S(2)}) collective-permute-start(f32[152,256]{1,0:T(8,128)S(1)} %get-tuple-element.42), channel_id=1, source_target_pairs={{3,0},{0,1},{1,2},{2,3},{7,4},{4,5},{5,6},{6,7},{11,8},{8,9},{9,10... | collective-permute-start | bytes 466952 | tf_op jit(solution)/shard_map/ppermute | solution.py:403
  33.0 11.9 %collective-permute-start.11 = (f32[304,256]{1,0:T(8,128)S(1)}, f32[304,256]{1,0:T(8,128)S(1)}, u32[]{:S(2)}, u32[]{:S(2)}) collective-permute-start(f32[304,256]{1,0:T(8,128)S(1)} %merge.1.p), channel_id=1, source_target_pairs={{2,0},{3,1},{0,2},{1,3},{6,4},{7,5},{4,6},{5,7},{10,8},{11,9},{8,1... | collective-permute-start | bytes 933896 | tf_op jit(solution)/shard_map/ppermute | solution.py:403
  33.8 11.4 %collective-permute-start.8 = (f32[304,256]{1,0:T(8,128)S(1)}, f32[304,256]{1,0:T(8,128)S(1)}, u32[]{:S(2)}, u32[]{:S(2)}) collective-permute-start(f32[304,256]{1,0:T(8,128)S(1)} %merge.1.p), channel_id=1, source_target_pairs={{0,4},{1,5},{2,6},{3,7},{4,0},{5,1},{6,2},{7,3},{8,12},{9,13},{10,... | collective-permute-start | bytes 933896 | tf_op jit(solution)/shard_map/ppermute | solution.py:406
  34.3 16.0 %collective-permute-start.14 = (f32[304,256]{1,0:T(8,128)S(1)}, f32[304,256]{1,0:T(8,128)S(1)}, u32[]{:S(2)}, u32[]{:S(2)}) collective-permute-start(f32[304,256]{1,0:T(8,128)S(1)} %merge.1.p), channel_id=1, source_target_pairs={{3,0},{0,1},{1,2},{2,3},{7,4},{4,5},{5,6},{6,7},{11,8},{8,9},{9,10... | collective-permute-start | bytes 933896 | tf_op jit(solution)/shard_map/ppermute | solution.py:403
  35.4 14.9 %collective-permute-start.13 = (f32[304,256]{1,0:T(8,128)S(1)}, f32[304,256]{1,0:T(8,128)S(1)}, u32[]{:S(2)}, u32[]{:S(2)}) collective-permute-start(f32[304,256]{1,0:T(8,128)S(1)} %merge.1.p), channel_id=1, source_target_pairs={{1,0},{2,1},{3,2},{0,3},{5,4},{6,5},{7,6},{4,7},{9,8},{10,9},{11,1... | collective-permute-start | bytes 933896 | tf_op jit(solution)/shard_map/ppermute | solution.py:403
  44.8 8.5 %collective-permute-start.12 = (f32[304,256]{1,0:T(8,128)S(1)}, f32[304,256]{1,0:T(8,128)S(1)}, u32[]{:S(2)}, u32[]{:S(2)}) collective-permute-start(f32[304,256]{1,0:T(8,128)S(1)} %collective-permute-done.11.s), channel_id=1, source_target_pairs={{0,4},{1,5},{2,6},{3,7},{4,0},{5,1},{6,2},{7,3},{8,12},{9,13},{10,... | collective-permute-start | bytes 933896 | tf_op jit(solution)/shard_map/ppermute | solution.py:406
  45.3 11.6 %collective-permute-start.10 = (f32[304,256]{1,0:T(8,128)S(1)}, f32[304,256]{1,0:T(8,128)S(1)}, u32[]{:S(2)}, u32[]{:S(2)}) collective-permute-start(f32[304,256]{1,0:T(8,128)S(1)} %collective-permute-done.8.q), channel_id=1, source_target_pairs={{3,0},{0,1},{1,2},{2,3},{7,4},{4,5},{5,6},{6,7},{11,8},{8,9},{9,10... | collective-permute-start | bytes 933896 | tf_op jit(solution)/shard_map/ppermute | solution.py:403
  45.8 11.1 %collective-permute-start.9 = (f32[304,256]{1,0:T(8,128)S(1)}, f32[304,256]{1,0:T(8,128)S(1)}, u32[]{:S(2)}, u32[]{:S(2)}) collective-permute-start(f32[304,256]{1,0:T(8,128)S(1)} %collective-permute-done.8.q), channel_id=1, source_target_pairs={{1,0},{2,1},{3,2},{0,3},{5,4},{6,5},{7,6},{4,7},{9,8},{10,9},{11,1... | collective-permute-start | bytes 933896 | tf_op jit(solution)/shard_map/ppermute | solution.py:403
  62.5 12.6 %collective-permute-start.16 = (f32[512,256]{1,0:T(8,128)S(1)}, f32[512,256]{1,0:T(8,128)S(1)}, u32[]{:S(2)}, u32[]{:S(2)}) collective-permute-start(f32[512,256]{1,0:T(8,128)S(1)} %get-tuple-element.54), channel_id=1, source_target_pairs={{0,8},{8,16},{16,24},{24,32},{32,40},{40,48},{48,56},{56,64},{64,7... | collective-permute-start | bytes 1572872 | tf_op jit(solution)/shard_map/ppermute | solution.py:423
  67.3 13.4 %collective-permute-start.15 = (f32[512,256]{1,0:T(8,128)S(1)}, f32[512,256]{1,0:T(8,128)S(1)}, u32[]{:S(2)}, u32[]{:S(2)}) collective-permute-start(f32[512,256]{1,0:T(8,128)S(1)} %get-tuple-element.53), channel_id=1, source_target_pairs={{0,8},{8,16},{16,24},{24,32},{32,40},{40,48},{48,56},{56,64},{64,7... | collective-permute-start | bytes 1572872 | tf_op jit(solution)/shard_map/ppermute | solution.py:423

commit v7 on v6

--- a/solution.py
+++ b/solution.py
@@ -368,16 +368,21 @@
 
     @pl.when(lax.axis_index("row") > 0)
     def _():
-        copy = pltpu.make_async_copy(upper, out.at[spot], sems.at[0])
-        copy.start()
-        copy.wait()
+        copies = []
+        for n in range(4):
+            part = pl.ds(n * 128, 128)
+            copies.append(pltpu.make_async_copy(upper.at[part], out.at[part, pl.ds(half * COLS, COLS)], sems.at[n]))
+        for copy in copies:
+            copy.start()
+        for copy in copies:
+            copy.wait()
 
     @pl.when(lax.axis_index("row") == 0)
     def _():
-        fetch = pltpu.make_async_copy(eig.at[spot], rows, sems.at[1])
+        fetch = pltpu.make_async_copy(eig.at[spot], rows, sems.at[4])
         fetch.start()
         fetch.wait()
-        copy = pltpu.make_async_copy(rows, out.at[spot], sems.at[2])
+        copy = pltpu.make_async_copy(rows, out.at[spot], sems.at[5])
         copy.start()
         copy.wait()
 
@@ -389,7 +394,7 @@
         in_specs=[HBM, VMEM, HBM],
         out_specs=HBM,
         input_output_aliases={2: 0},
-        scratch_shapes=[pltpu.VMEM((HALF, COLS), F32), pltpu.SemaphoreType.DMA((3,))],
+        scratch_shapes=[pltpu.VMEM((HALF, COLS), F32), pltpu.SemaphoreType.DMA((6,))],
         compiler_params=pltpu.CompilerParams(vmem_limit_bytes=4 * MIB),
         cost_estimate=cost(0, MIB),
         name="finish",

time: 82 us -> 82 us (level)
  no operation moved by 1% of the time
where the time goes in v7:
time: 82 us; the launch traced here: 81.7 us
  waiting for transfers between devices  35.4 us (43%)
  starting transfers between devices  25.4 us (31%)
  Pallas kernels  20.7 us (25%)
    ppermute x11, waiting for transfers between devices, from_x(): lax.ppermute(value, 'col', [(i // 4 * 4 + (i % 4 + d) % 4, i) for i in ra...  27.7 us
    ppermute x11, starting transfers between devices, from_x(): lax.ppermute(value, 'col', [(i // 4 * 4 + (i % 4 + d) % 4, i) for i in ra...  14.1 us
    ppermute x2, waiting for transfers between devices, per_device(): upper = lax.ppermute(bottom, 'row', [(i, i + 1) for i in range(count - 1)])  5.67 us
    pallas_call x1, Pallas kernels, update(): pl.pallas_call(first_kernel, out_shape=(solved[0], shape((REACH, both), B...  5.57 us
    ppermute x2, starting transfers between devices, per_device(): upper = lax.ppermute(bottom, 'row', [(i, i + 1) for i in range(count - 1)])  4.6 us
    pallas_call x1, Pallas kernels, store(): pl.pallas_call(store_kernel, out_shape=jax.ShapeDtypeStruct(eig.shape, F3...  4.23 us
    ppermute x3, starting transfers between devices, from_y(): return lax.ppermute(value, 'col', [(i, i ^ 4) for i in range(8)])  4.2 us
    pallas_call x1, Pallas kernels, update(): pl.pallas_call(second_kernel, out_shape=solved, in_specs=[SMEM] + [VMEM]...  2.85 us
  transfers between devices with their start and end apart: 17, of which 12 were waited for; matrix products, arithmetic and copies ran while one was open for 0% of the time, Pallas kernels for 14%

profile of v7, /device:TPU:128, one launch (start us, length us, event | category | flops | bytes accessed | tf_op | source)
XLA Modules:
  0.0 81.7 jit_solution(7369598889080813147)
XLA Ops:
  0.0 0.0 copy-start
  0.0 2.1 %pack.1 = (f32[152,256]{1,0:T(8,128)S(1)}, f32[152,256]{1,0:T(8,128)S(1)}, f32[152,256]{1,0:T(8,128)S(1)}, f32[152,256]{1,0:T(8,128)S(1)}, f32[152,256]{1,0:T(8,...) custom-call(f32[1,1,1024,256]{3,2,1,0:T(8,128)} %vectors.1, ...), custom_call_target="tpu_custom_call" | custom-call | bytes 5242880 | tf_op jit(solution)/shard_map/pack/pallas_call | solution.py:92
  2.1 0.0 copy-start.1
  2.1 2.5 %collective-permute-start = (f32[512,512]{1,0:T(8,128)S(1)}, f32[512,512]{1,0:T(8,128)S(1)}, u32[]{:S(2)}, u32[]{:S(2)}) collective-permute-start(f32[512,512]{1,0:T(8,128)S(1)} %get-tuple-element.32), channel_id=1, source_target_pairs={{8,0},{16,8},{24,16},{32,24},{40,32},{48,40},{56,48},{64,56},{72,6... | collective-permute-start | bytes 3145736 | tf_op jit(solution)/shard_map/ppermute | solution.py:419
  4.6 2.8 %collective-permute-start.4 = (f32[152,256]{1,0:T(8,128)S(1)}, f32[152,256]{1,0:T(8,128)S(1)}, u32[]{:S(2)}, u32[]{:S(2)}) collective-permute-start(f32[152,256]{1,0:T(8,128)S(1)} %get-tuple-element.44), channel_id=1, source_target_pairs={{1,0},{2,1},{3,2},{0,3},{5,4},{6,5},{7,6},{4,7},{9,8},{10,9},{11,1... | collective-permute-start | bytes 466952 | tf_op jit(solution)/shard_map/ppermute | solution.py:408
  7.4 0.8 collective-permute-start.5
  8.2 0.9 %collective-permute-start.6 = (f32[152,256]{1,0:T(8,128)S(1)}, f32[152,256]{1,0:T(8,128)S(1)}, u32[]{:S(2)}, u32[]{:S(2)}) collective-permute-start(f32[152,256]{1,0:T(8,128)S(1)} %get-tuple-element.46), channel_id=1, source_target_pairs={{3,0},{0,1},{1,2},{2,3},{7,4},{4,5},{5,6},{6,7},{11,8},{8,9},{9,10... | collective-permute-start | bytes 466952 | tf_op jit(solution)/shard_map/ppermute | solution.py:408
  9.1 5.1 %collective-permute-done.4.near = f32[152,256]{1,0:T(8,128)S(1)} collective-permute-done((f32[152,256]{1,0:T(8,128)S(1)}, f32[152,256]{1,0:T(8,128)S(1)}, u32[]{:S(2)}, u32[]{:S(2)}) %collective-permute-start.4) | collective-permute-done | bytes 155680 | tf_op jit(solution)/shard_map/ppermute | solution.py:408
  14.2 1.7 %collective-permute-done.5.far = f32[152,256]{1,0:T(8,128)S(1)} collective-permute-done((f32[152,256]{1,0:T(8,128)S(1)}, f32[152,256]{1,0:T(8,128)S(1)}, u32[]{:S(2)}, u32[]{:S(2)}) %collective-permute-start.5) | collective-permute-done | bytes 155680 | tf_op jit(solution)/shard_map/ppermute | solution.py:408
  15.9 2.0 %collective-permute-done.6.back = f32[152,256]{1,0:T(8,128)S(1)} collective-permute-done((f32[152,256]{1,0:T(8,128)S(1)}, f32[152,256]{1,0:T(8,128)S(1)}, u32[]{:S(2)}, u32[]{:S(2)}) %collective-permute-start.6) | collective-permute-done | bytes 155680 | tf_op jit(solution)/shard_map/ppermute | solution.py:408
  17.9 0.0 copy-done
  17.9 0.6 choose.1
  18.5 3.3 %collective-permute-start.7 = (f32[304,256]{1,0:T(8,128)S(1)}, f32[304,256]{1,0:T(8,128)S(1)}, u32[]{:S(2)}, u32[]{:S(2)}) collective-permute-start(f32[304,256]{1,0:T(8,128)S(1)} %choose.1), channel_id=1, source_target_pairs={{0,4},{1,5},{2,6},{3,7},{4,0},{5,1},{6,2},{7,3},{8,12},{9,13},{10,... | collective-permute-start | bytes 933896 | tf_op jit(solution)/shard_map/ppermute | solution.py:411
  21.8 0.6 collective-permute-start.1
  22.4 0.8 collective-permute-start.2
  23.2 0.9 %collective-permute-start.3 = (f32[152,256]{1,0:T(8,128)S(1)}, f32[152,256]{1,0:T(8,128)S(1)}, u32[]{:S(2)}, u32[]{:S(2)}) collective-permute-start(f32[152,256]{1,0:T(8,128)S(1)} %get-tuple-element.42), channel_id=1, source_target_pairs={{3,0},{0,1},{1,2},{2,3},{7,4},{4,5},{5,6},{6,7},{11,8},{8,9},{9,10... | collective-permute-start | bytes 466952 | tf_op jit(solution)/shard_map/ppermute | solution.py:408
  24.0 0.0 collective-permute-done.halo
  24.0 2.1 %stage.1 = (bf16[1536,256]{1,0:T(8,128)(2,1)S(1)}, bf16[1536,256]{1,0:T(8,128)(2,1)S(1)}, bf16[1536,256]{1,0:T(8,128)(2,1)S(1)}, bf16[1536,256]{1,0:T(8,128)(2,1...) custom-call(f32[2048,512]{1,0:T(8,128)} %eig.9, f32[512,512]{1,0:T(8,128)S(1)} %collective-permute-done.halo), custom_call_target="tpu_custom_call" | custom-call | bytes 262144 | tf_op jit(solution)/shard_map/stage/pallas_call | solution.py:120
  26.2 2.6 %collective-permute-done.1.near = f32[152,256]{1,0:T(8,128)S(1)} collective-permute-done((f32[152,256]{1,0:T(8,128)S(1)}, f32[152,256]{1,0:T(8,128)S(1)}, u32[]{:S(2)}, u32[]{:S(2)}) %collective-permute-start.1) | collective-permute-done | bytes 155680 | tf_op jit(solution)/shard_map/ppermute | solution.py:408
  28.7 1.8 %collective-permute-done.2.far = f32[152,256]{1,0:T(8,128)S(1)} collective-permute-done((f32[152,256]{1,0:T(8,128)S(1)}, f32[152,256]{1,0:T(8,128)S(1)}, u32[]{:S(2)}, u32[]{:S(2)}) %collective-permute-start.2) | collective-permute-done | bytes 155680 | tf_op jit(solution)/shard_map/ppermute | solution.py:408
  30.6 1.7 %collective-permute-done.3.back = f32[152,256]{1,0:T(8,128)S(1)} collective-permute-done((f32[152,256]{1,0:T(8,128)S(1)}, f32[152,256]{1,0:T(8,128)S(1)}, u32[]{:S(2)}, u32[]{:S(2)}) %collective-permute-start.3) | collective-permute-done | bytes 155680 | tf_op jit(solution)/shard_map/ppermute | solution.py:408
  32.3 0.0 collective-permute-done.7.got
  32.3 0.6 merge.1.p
  33.0 0.9 %collective-permute-start.11 = (f32[304,256]{1,0:T(8,128)S(1)}, f32[304,256]{1,0:T(8,128)S(1)}, u32[]{:S(2)}, u32[]{:S(2)}) collective-permute-start(f32[304,256]{1,0:T(8,128)S(1)} %merge.1.p), channel_id=1, source_target_pairs={{2,0},{3,1},{0,2},{1,3},{6,4},{7,5},{4,6},{5,7},{10,8},{11,9},{8,1... | collective-permute-start | bytes 933896 | tf_op jit(solution)/shard_map/ppermute | solution.py:408
  33.8 0.5 collective-permute-start.8
  34.3 1.1 %collective-permute-start.14 = (f32[304,256]{1,0:T(8,128)S(1)}, f32[304,256]{1,0:T(8,128)S(1)}, u32[]{:S(2)}, u32[]{:S(2)}) collective-permute-start(f32[304,256]{1,0:T(8,128)S(1)} %merge.1.p), channel_id=1, source_target_pairs={{3,0},{0,1},{1,2},{2,3},{7,4},{4,5},{5,6},{6,7},{11,8},{8,9},{9,10... | collective-permute-start | bytes 933896 | tf_op jit(solution)/shard_map/ppermute | solution.py:408
  35.4 2.1 %collective-permute-start.13 = (f32[304,256]{1,0:T(8,128)S(1)}, f32[304,256]{1,0:T(8,128)S(1)}, u32[]{:S(2)}, u32[]{:S(2)}) collective-permute-start(f32[304,256]{1,0:T(8,128)S(1)} %merge.1.p), channel_id=1, source_target_pairs={{1,0},{2,1},{3,2},{0,3},{5,4},{6,5},{7,6},{4,7},{9,8},{10,9},{11,1... | collective-permute-start | bytes 933896 | tf_op jit(solution)/shard_map/ppermute | solution.py:408
  37.5 7.3 %collective-permute-done.11.s = f32[304,256]{1,0:T(8,128)S(1)} collective-permute-done((f32[304,256]{1,0:T(8,128)S(1)}, f32[304,256]{1,0:T(8,128)S(1)}, u32[]{:S(2)}, u32[]{:S(2)}) %collective-permute-start.11) | collective-permute-done | bytes 311328 | tf_op jit(solution)/shard_map/ppermute | solution.py:408
  44.8 0.4 collective-permute-start.12
  45.3 0.0 collective-permute-done.8.q
  45.3 0.5 collective-permute-start.10
  45.8 2.7 %collective-permute-start.9 = (f32[304,256]{1,0:T(8,128)S(1)}, f32[304,256]{1,0:T(8,128)S(1)}, u32[]{:S(2)}, u32[]{:S(2)}) collective-permute-start(f32[304,256]{1,0:T(8,128)S(1)} %collective-permute-done.8.q), channel_id=1, source_target_pairs={{1,0},{2,1},{3,2},{0,3},{5,4},{6,5},{7,6},{4,7},{9,8},{10,9},{11,1... | collective-permute-start | bytes 933896 | tf_op jit(solution)/shard_map/ppermute | solution.py:408
  48.5 1.8 %collective-permute-done.14.l = f32[304,256]{1,0:T(8,128)S(1)} collective-permute-done((f32[304,256]{1,0:T(8,128)S(1)}, f32[304,256]{1,0:T(8,128)S(1)}, u32[]{:S(2)}, u32[]{:S(2)}) %collective-permute-start.14) | collective-permute-done | bytes 311328 | tf_op jit(solution)/shard_map/ppermute | solution.py:408
  50.4 0.0 collective-permute-done.13.r
  50.4 0.0 copy-done.1
  50.4 0.9 %prepare.1 = (f32[2,1552,256]{2,1,0:T(8,128)S(1)}, f32[2,192,256]{2,1,0:T(8,128)S(1)}) custom-call(s32[2,32]{1,0:T(2,128)S(1)} %copy-done.1, f32[304,256]{1,0:T(8,128)S(1)} %merge.1.p, f32[304,256]{1,0:T(8,128)S(1)} %collective-permute-done.13.r, f32[304,256]{1,0:T(8,128)S(1)} %collective-permute-done.14.l, f32[304,256]{1,0:T(8,128)S(1)} %collective-permute-done.11.s, ...), custom_call_target="tpu_custom_call" | custom-call | bytes 6291456 | tf_op jit(solution)/shard_map/prepare/pallas_call | solution.py:223
  51.3 2.0 %collective-permute-done.12.z = f32[304,256]{1,0:T(8,128)S(1)} collective-permute-done((f32[304,256]{1,0:T(8,128)S(1)}, f32[304,256]{1,0:T(8,128)S(1)}, u32[]{:S(2)}, u32[]{:S(2)}) %collective-permute-start.12) | collective-permute-done | bytes 311328 | tf_op jit(solution)/shard_map/ppermute | solution.py:411
  53.3 3.6 %collective-permute-done.10.v = f32[304,256]{1,0:T(8,128)S(1)} collective-permute-done((f32[304,256]{1,0:T(8,128)S(1)}, f32[304,256]{1,0:T(8,128)S(1)}, u32[]{:S(2)}, u32[]{:S(2)}) %collective-permute-start.10) | collective-permute-done | bytes 311328 | tf_op jit(solution)/shard_map/ppermute | solution.py:408
  56.9 0.0 collective-permute-done.9.u
  56.9 5.6 %first.1 = (f32[512,256]{1,0:T(8,128)S(1)}, bf16[1536,512]{1,0:T(8,128)(2,1)S(1)}, bf16[1536,512]{1,0:T(8,128)(2,1)S(1)}, bf16[512,256]{1,0:T(8,128)(2,1)S(1)}, ...) custom-call(s32[2,32]{1,0:T(2,128)S(1)} %copy-done.1, ...), custom_call_target="tpu_custom_call", output_to_operand_aliasing={{7}: (7, {}), {8}: (8, {})} | custom-call | flops 3000000000 | bytes 8388608 | tf_op jit(solution)/shard_map/first/pallas_call | solution.py:289
  62.5 1.9 %collective-permute-start.16 = (f32[512,256]{1,0:T(8,128)S(1)}, f32[512,256]{1,0:T(8,128)S(1)}, u32[]{:S(2)}, u32[]{:S(2)}) collective-permute-start(f32[512,256]{1,0:T(8,128)S(1)} %get-tuple-element.54), channel_id=1, source_target_pairs={{0,8},{8,16},{16,24},{24,32},{32,40},{40,48},{48,56},{56,64},{64,7... | collective-permute-start | bytes 1572872 | tf_op jit(solution)/shard_map/ppermute | solution.py:428
  64.4 2.9 %second.1 = (f32[512,256]{1,0:T(8,128)S(1)}, bf16[512,256]{1,0:T(8,128)(2,1)S(1)}, bf16[512,256]{1,0:T(8,128)(2,1)S(1)}) custom-call(s32[2,32]{1,0:T(2,128)S(1)} %copy-done.1, bf16[1536,256]{1,0:T(8,128)(2,1)S(1)} %get-tuple-element.33.wh, bf16[1536,256]{1,0:T(8,128)(2,1)S(1)} %get-tuple-element.34.wl, f32[512,256]{1,0:T(8,128)S(1)} %get-tuple-element.35.low, ...), custom_call_target="tpu_custom_call" | custom-call | flops 3000000000 | bytes 8388608 | tf_op jit(solution)/shard_map/second/pallas_call | solution.py:308
  67.3 2.7 %collective-permute-start.15 = (f32[512,256]{1,0:T(8,128)S(1)}, f32[512,256]{1,0:T(8,128)S(1)}, u32[]{:S(2)}, u32[]{:S(2)}) collective-permute-start(f32[512,256]{1,0:T(8,128)S(1)} %get-tuple-element.53), channel_id=1, source_target_pairs={{0,8},{8,16},{16,24},{24,32},{32,40},{40,48},{48,56},{56,64},{64,7... | collective-permute-start | bytes 1572872 | tf_op jit(solution)/shard_map/ppermute | solution.py:428
  70.0 4.2 %store.1.old = f32[2048,512]{1,0:T(8,128)} custom-call(f32[2048,512]{1,0:T(8,128)} %eig.9, bf16[1536,512]{1,0:T(8,128)(2,1)S(1)} %get-tuple-element.49.vh, bf16[1536,512]{1,0:T(8,128)(2,1)S(1)} %get-tuple-element.50.vl, bf16[512,256]{1,0:T(8,128)(2,1)S(1)} %get-tuple-element.55.sh, bf16[512,256]{1,0:T(8,128)(2,1)S(1)} %get-tuple-element.56.sl, ...), custom_call_target="tpu_custom_call" | custom-call | flops 1600000000 | bytes 8388608 | tf_op jit(solution)/shard_map/store/pallas_call | solution.py:349
  74.2 0.9 %collective-permute-done.16.upper = f32[512,256]{1,0:T(8,128)S(1)} collective-permute-done((f32[512,256]{1,0:T(8,128)S(1)}, f32[512,256]{1,0:T(8,128)S(1)}, u32[]{:S(2)}, u32[]{:S(2)}) %collective-permute-start.16) | collective-permute-done | bytes 524320 | tf_op jit(solution)/shard_map/ppermute | solution.py:428
  75.1 0.8 %finish.2.old = f32[2048,512]{1,0:T(8,128)} custom-call(f32[2048,512]{1,0:T(8,128)} %eig.9, f32[512,256]{1,0:T(8,128)S(1)} %collective-permute-done.16.upper, f32[2048,512]{1,0:T(8,128)} %store.1.old), custom_call_target="tpu_custom_call", output_to_operand_aliasing={{}: (2, {})} | custom-call | bytes 1048576 | tf_op jit(solution)/shard_map/finish/pallas_call | solution.py:391
  76.0 4.8 %collective-permute-done.15.upper = f32[512,256]{1,0:T(8,128)S(1)} collective-permute-done((f32[512,256]{1,0:T(8,128)S(1)}, f32[512,256]{1,0:T(8,128)S(1)}, u32[]{:S(2)}, u32[]{:S(2)}) %collective-permute-start.15) | collective-permute-done | bytes 524320 | tf_op jit(solution)/shard_map/ppermute | solution.py:428
  80.7 0.8 %finish.3 = f32[2048,512]{1,0:T(8,128)} custom-call(f32[2048,512]{1,0:T(8,128)} %eig.9, f32[512,256]{1,0:T(8,128)S(1)} %collective-permute-done.15.upper, f32[2048,512]{1,0:T(8,128)} %finish.2.old), custom_call_target="tpu_custom_call", output_to_operand_aliasing={{}: (2, {})} | custom-call | bytes 1048576 | tf_op jit(solution)/shard_map/finish/pallas_call | solution.py:391
Async XLA Ops:
  0.0 17.9 %copy-start = (s32[2,32]{1,0:T(2,128)S(1)}, s32[2,32]{1,0:T(2,128)}, u32[]{:S(2)}) copy-start(s32[2,32]{1,0:T(2,128)} %owners.3) | copy-start | bytes 772
  2.1 48.2 %copy-start.1 = (s32[2,32]{1,0:T(2,128)S(1)}, s32[2,32]{1,0:T(2,128)}, u32[]{:S(2)}) copy-start(s32[2,32]{1,0:T(2,128)} %offsets.5) | copy-start | bytes 772
  2.1 21.9 %collective-permute-start = (f32[512,512]{1,0:T(8,128)S(1)}, f32[512,512]{1,0:T(8,128)S(1)}, u32[]{:S(2)}, u32[]{:S(2)}) collective-permute-start(f32[512,512]{1,0:T(8,128)S(1)} %get-tuple-element.32), channel_id=1, source_target_pairs={{8,0},{16,8},{24,16},{32,24},{40,32},{48,40},{56,48},{64,56},{72,6... | collective-permute-start | bytes 3145736 | tf_op jit(solution)/shard_map/ppermute | solution.py:419
  4.6 9.6 %collective-permute-start.4 = (f32[152,256]{1,0:T(8,128)S(1)}, f32[152,256]{1,0:T(8,128)S(1)}, u32[]{:S(2)}, u32[]{:S(2)}) collective-permute-start(f32[152,256]{1,0:T(8,128)S(1)} %get-tuple-element.44), channel_id=1, source_target_pairs={{1,0},{2,1},{3,2},{0,3},{5,4},{6,5},{7,6},{4,7},{9,8},{10,9},{11,1... | collective-permute-start | bytes 466952 | tf_op jit(solution)/shard_map/ppermute | solution.py:408
  7.4 8.5 %collective-permute-start.5 = (f32[152,256]{1,0:T(8,128)S(1)}, f32[152,256]{1,0:T(8,128)S(1)}, u32[]{:S(2)}, u32[]{:S(2)}) collective-permute-start(f32[152,256]{1,0:T(8,128)S(1)} %get-tuple-element.45), channel_id=1, source_target_pairs={{2,0},{3,1},{0,2},{1,3},{6,4},{7,5},{4,6},{5,7},{10,8},{11,9},{8,1... | collective-permute-start | bytes 466952 | tf_op jit(solution)/shard_map/ppermute | solution.py:408
  8.2 9.6 %collective-permute-start.6 = (f32[152,256]{1,0:T(8,128)S(1)}, f32[152,256]{1,0:T(8,128)S(1)}, u32[]{:S(2)}, u32[]{:S(2)}) collective-permute-start(f32[152,256]{1,0:T(8,128)S(1)} %get-tuple-element.46), channel_id=1, source_target_pairs={{3,0},{0,1},{1,2},{2,3},{7,4},{4,5},{5,6},{6,7},{11,8},{8,9},{9,10... | collective-permute-start | bytes 466952 | tf_op jit(solution)/shard_map/ppermute | solution.py:408
  18.5 13.8 %collective-permute-start.7 = (f32[304,256]{1,0:T(8,128)S(1)}, f32[304,256]{1,0:T(8,128)S(1)}, u32[]{:S(2)}, u32[]{:S(2)}) collective-permute-start(f32[304,256]{1,0:T(8,128)S(1)} %choose.1), channel_id=1, source_target_pairs={{0,4},{1,5},{2,6},{3,7},{4,0},{5,1},{6,2},{7,3},{8,12},{9,13},{10,... | collective-permute-start | bytes 933896 | tf_op jit(solution)/shard_map/ppermute | solution.py:411
  21.8 6.9 %collective-permute-start.1 = (f32[152,256]{1,0:T(8,128)S(1)}, f32[152,256]{1,0:T(8,128)S(1)}, u32[]{:S(2)}, u32[]{:S(2)}) collective-permute-start(f32[152,256]{1,0:T(8,128)S(1)} %get-tuple-element.40), channel_id=1, source_target_pairs={{1,0},{2,1},{3,2},{0,3},{5,4},{6,5},{7,6},{4,7},{9,8},{10,9},{11,1... | collective-permute-start | bytes 466952 | tf_op jit(solution)/shard_map/ppermute | solution.py:408
  22.4 8.2 %collective-permute-start.2 = (f32[152,256]{1,0:T(8,128)S(1)}, f32[152,256]{1,0:T(8,128)S(1)}, u32[]{:S(2)}, u32[]{:S(2)}) collective-permute-start(f32[152,256]{1,0:T(8,128)S(1)} %get-tuple-element.41), channel_id=1, source_target_pairs={{2,0},{3,1},{0,2},{1,3},{6,4},{7,5},{4,6},{5,7},{10,8},{11,9},{8,1... | collective-permute-start | bytes 466952 | tf_op jit(solution)/shard_map/ppermute | solution.py:408
  23.2 9.1 %collective-permute-start.3 = (f32[152,256]{1,0:T(8,128)S(1)}, f32[152,256]{1,0:T(8,128)S(1)}, u32[]{:S(2)}, u32[]{:S(2)}) collective-permute-start(f32[152,256]{1,0:T(8,128)S(1)} %get-tuple-element.42), channel_id=1, source_target_pairs={{3,0},{0,1},{1,2},{2,3},{7,4},{4,5},{5,6},{6,7},{11,8},{8,9},{9,10... | collective-permute-start | bytes 466952 | tf_op jit(solution)/shard_map/ppermute | solution.py:408
  33.0 11.9 %collective-permute-start.11 = (f32[304,256]{1,0:T(8,128)S(1)}, f32[304,256]{1,0:T(8,128)S(1)}, u32[]{:S(2)}, u32[]{:S(2)}) collective-permute-start(f32[304,256]{1,0:T(8,128)S(1)} %merge.1.p), channel_id=1, source_target_pairs={{2,0},{3,1},{0,2},{1,3},{6,4},{7,5},{4,6},{5,7},{10,8},{11,9},{8,1... | collective-permute-start | bytes 933896 | tf_op jit(solution)/shard_map/ppermute | solution.py:408
  33.8 11.4 %collective-permute-start.8 = (f32[304,256]{1,0:T(8,128)S(1)}, f32[304,256]{1,0:T(8,128)S(1)}, u32[]{:S(2)}, u32[]{:S(2)}) collective-permute-start(f32[304,256]{1,0:T(8,128)S(1)} %merge.1.p), channel_id=1, source_target_pairs={{0,4},{1,5},{2,6},{3,7},{4,0},{5,1},{6,2},{7,3},{8,12},{9,13},{10,... | collective-permute-start | bytes 933896 | tf_op jit(solution)/shard_map/ppermute | solution.py:411
  34.3 16.0 %collective-permute-start.14 = (f32[304,256]{1,0:T(8,128)S(1)}, f32[304,256]{1,0:T(8,128)S(1)}, u32[]{:S(2)}, u32[]{:S(2)}) collective-permute-start(f32[304,256]{1,0:T(8,128)S(1)} %merge.1.p), channel_id=1, source_target_pairs={{3,0},{0,1},{1,2},{2,3},{7,4},{4,5},{5,6},{6,7},{11,8},{8,9},{9,10... | collective-permute-start | bytes 933896 | tf_op jit(solution)/shard_map/ppermute | solution.py:408
  35.4 14.9 %collective-permute-start.13 = (f32[304,256]{1,0:T(8,128)S(1)}, f32[304,256]{1,0:T(8,128)S(1)}, u32[]{:S(2)}, u32[]{:S(2)}) collective-permute-start(f32[304,256]{1,0:T(8,128)S(1)} %merge.1.p), channel_id=1, source_target_pairs={{1,0},{2,1},{3,2},{0,3},{5,4},{6,5},{7,6},{4,7},{9,8},{10,9},{11,1... | collective-permute-start | bytes 933896 | tf_op jit(solution)/shard_map/ppermute | solution.py:408
  44.8 8.5 %collective-permute-start.12 = (f32[304,256]{1,0:T(8,128)S(1)}, f32[304,256]{1,0:T(8,128)S(1)}, u32[]{:S(2)}, u32[]{:S(2)}) collective-permute-start(f32[304,256]{1,0:T(8,128)S(1)} %collective-permute-done.11.s), channel_id=1, source_target_pairs={{0,4},{1,5},{2,6},{3,7},{4,0},{5,1},{6,2},{7,3},{8,12},{9,13},{10,... | collective-permute-start | bytes 933896 | tf_op jit(solution)/shard_map/ppermute | solution.py:411
  45.3 11.6 %collective-permute-start.10 = (f32[304,256]{1,0:T(8,128)S(1)}, f32[304,256]{1,0:T(8,128)S(1)}, u32[]{:S(2)}, u32[]{:S(2)}) collective-permute-start(f32[304,256]{1,0:T(8,128)S(1)} %collective-permute-done.8.q), channel_id=1, source_target_pairs={{3,0},{0,1},{1,2},{2,3},{7,4},{4,5},{5,6},{6,7},{11,8},{8,9},{9,10... | collective-permute-start | bytes 933896 | tf_op jit(solution)/shard_map/ppermute | solution.py:408
  45.8 11.1 %collective-permute-start.9 = (f32[304,256]{1,0:T(8,128)S(1)}, f32[304,256]{1,0:T(8,128)S(1)}, u32[]{:S(2)}, u32[]{:S(2)}) collective-permute-start(f32[304,256]{1,0:T(8,128)S(1)} %collective-permute-done.8.q), channel_id=1, source_target_pairs={{1,0},{2,1},{3,2},{0,3},{5,4},{6,5},{7,6},{4,7},{9,8},{10,9},{11,1... | collective-permute-start | bytes 933896 | tf_op jit(solution)/shard_map/ppermute | solution.py:408
  62.5 12.6 %collective-permute-start.16 = (f32[512,256]{1,0:T(8,128)S(1)}, f32[512,256]{1,0:T(8,128)S(1)}, u32[]{:S(2)}, u32[]{:S(2)}) collective-permute-start(f32[512,256]{1,0:T(8,128)S(1)} %get-tuple-element.54), channel_id=1, source_target_pairs={{0,8},{8,16},{16,24},{24,32},{32,40},{40,48},{48,56},{56,64},{64,7... | collective-permute-start | bytes 1572872 | tf_op jit(solution)/shard_map/ppermute | solution.py:428
  67.3 13.4 %collective-permute-start.15 = (f32[512,256]{1,0:T(8,128)S(1)}, f32[512,256]{1,0:T(8,128)S(1)}, u32[]{:S(2)}, u32[]{:S(2)}) collective-permute-start(f32[512,256]{1,0:T(8,128)S(1)} %get-tuple-element.53), channel_id=1, source_target_pairs={{0,8},{8,16},{16,24},{24,32},{32,40},{40,48},{48,56},{56,64},{64,7... | collective-permute-start | bytes 1572872 | tf_op jit(solution)/shard_map/ppermute | solution.py:428
